TPU v7x, 32 devices: a whole 2x2x4 slice. The times are simulated.
32 devices in a mesh: grp: 2 (over x), stn: 8 (over z, y), chan: 2 (over core).
Axes of the slice: x: 2, y: 2, z: 4, core: 2. Of those that a mesh axis runs over, the one named last changes fastest.
Arguments:
- voltage: bfloat16 [2, 32, 1048576], P(None, ('grp', 'stn'), 'chan'), parts along dimension 1, may hold values from -6 to 6
- earlier_samples: bfloat16 [2, 32, 61440], P(None, ('grp', 'stn')), parts along dimension 1, may hold values from -6 to 6
- prototype: float32 [16, 4096], replicated, may hold values from -1.5 to 1.5
Outputs:
- visibilities: float32 [2, 8192, 256], P(None, ('grp', 'stn', 'chan')), parts along dimension 1
There are 2 independent parts, one for each index of `grp`. A program takes and returns all parts, laid end to end along the dimension named above; an argument that names none is the same for every part. Nothing has to cross between parts.
All inputs are finite; a program needn't handle non-finite values.
Results may differ from a plain program's by a relative error of at most 0.0044.
Values may be sent and summed in bfloat16 or wider, within the bound.
No kernel may reach another device: no remote copies, remote signals or barrier semaphores. Data moves between devices by JAX's collectives and lax.ppermute only.
A program may use at most 64 MiB of HBM per device.

v0:
```python
import math

import jax
import jax.numpy as jnp
from jax import lax
from jax.sharding import PartitionSpec as P

FA = 64


def passed_along(block, axis, distance):
    devices = range(lax.axis_size(axis))
    route = [(i - distance, i) for i in devices if i - distance in devices]
    return lax.ppermute(block, axis, route)


def small_tables(length):
    row_index = lax.broadcasted_iota(jnp.int32, (length, length), 0)
    col_index = lax.broadcasted_iota(jnp.int32, (length, length), 1)
    phase_angle = (row_index * col_index % length).astype(jnp.float32) * (2.0 * math.pi / length)
    return (jnp.cos(phase_angle).astype(jnp.bfloat16), jnp.sin(phase_angle).astype(jnp.bfloat16))


def shards(voltage, earlier_samples, prototype):
    components, local_inputs, samples = voltage.shape
    tap_count, channels = prototype.shape
    spectra_here = samples // channels
    frames = voltage.reshape(components, local_inputs, spectra_here, channels)
    tail_frames = frames[:, :, spectra_here - (tap_count - 1) :]
    passed = passed_along(tail_frames, "chan", 1)
    earlier = earlier_samples.reshape(components, local_inputs, tap_count - 1, channels)
    leading = lax.axis_index("chan") == 0
    history = jnp.where(leading, earlier, passed)
    stacked = jnp.concatenate([history, frames], axis=2)
    filtered = jnp.zeros((components, local_inputs, spectra_here, channels), jnp.float32)
    for tap_number in range(tap_count):
        window_frames = stacked[:, :, tap_number : tap_number + spectra_here].astype(jnp.float32)
        filtered = filtered + prototype[tap_number] * window_frames
    half_rows = local_inputs * spectra_here
    first_factor = FA
    second_factor = channels // first_factor
    factored = filtered.astype(jnp.bfloat16).reshape(
        components, half_rows, first_factor, second_factor
    )
    first_cos, first_sin = small_tables(first_factor)
    second_cos, second_sin = small_tables(second_factor)
    with_cos = jnp.einsum("crab,ak->crkb", factored, first_cos, preferred_element_type=jnp.float32)
    with_sin = jnp.einsum("crab,ak->crkb", factored, first_sin, preferred_element_type=jnp.float32)
    g_real = with_cos[0] + with_sin[1]
    g_imag = with_cos[1] - with_sin[0]
    row_k = lax.broadcasted_iota(jnp.int32, (first_factor, second_factor), 0)
    col_b = lax.broadcasted_iota(jnp.int32, (first_factor, second_factor), 1)
    twist = (row_k * col_b % channels).astype(jnp.float32) * (2.0 * math.pi / channels)
    twist_cos = jnp.cos(twist)
    twist_sin = jnp.sin(twist)
    inner = jnp.stack(
        [g_real * twist_cos + g_imag * twist_sin, g_imag * twist_cos - g_real * twist_sin]
    ).astype(jnp.bfloat16)
    second_a = jnp.einsum("crkb,bm->crkm", inner, second_cos, preferred_element_type=jnp.float32)
    second_b = jnp.einsum("crkb,bm->crkm", inner, second_sin, preferred_element_type=jnp.float32)
    scale_factor = channels ** (-0.5)
    real_part = (second_a[0] + second_b[1]) * scale_factor
    imag_part = (second_a[1] - second_b[0]) * scale_factor
    ordered = jnp.transpose(jnp.stack([real_part, imag_part]), (0, 1, 3, 2))
    spectra = ordered.astype(jnp.bfloat16).reshape(components, local_inputs, spectra_here, channels)
    station_count = lax.axis_size("stn")
    core_count = lax.axis_size("chan")
    owners = station_count * core_count
    owned = channels // owners
    shaped = spectra.reshape(components, local_inputs, spectra_here, owners, owned)
    moved = lax.all_to_all(shaped, ("stn", "chan"), split_axis=3, concat_axis=3, tiled=True)
    moved = moved.reshape(components, local_inputs, spectra_here, station_count, core_count, owned)
    moved = jnp.transpose(moved, (0, 3, 1, 4, 2, 5)).reshape(
        components, station_count * local_inputs, core_count * spectra_here, owned
    )
    all_inputs = moved.shape[1]
    spectra_total = moved.shape[2]
    products = jnp.einsum("xisc,yjsc->xycij", moved, moved, preferred_element_type=jnp.float32)
    real_sum = products[0, 0] + products[1, 1]
    imag_sum = products[1, 0] - products[0, 1]
    averaged = jnp.stack([real_sum, imag_sum]) / spectra_total
    return averaged.reshape(components, owned, all_inputs * all_inputs)


def solution(mesh):
    in_specs = (P(None, ("grp", "stn"), "chan"), P(None, ("grp", "stn"), None), P())
    out_specs = P(None, ("grp", "stn", "chan"), None)
    return jax.shard_map(shards, mesh=mesh, in_specs=in_specs, out_specs=out_specs, check_vma=False)
```

profile of v0, /device:TPU:1, one launch (start us, length us, event | category | flops | bytes accessed | tf_op | source)
XLA Modules:
  0.0 262.1 jit_solution(16261250131941861124)
XLA Ops:
  0.0 0.0 copy-start.2
  0.0 0.0 copy-start.1
  0.0 7.0 %reshape.101 = bf16[2,2,128,4096]{3,2,1,0:T(8,128)(2,1)} reshape(bf16[2,2,524288]{2,1,0:T(2,128)(2,1)} %param.3) | data formatting | bytes 8388608 | tf_op jit(solution)/shard_map/reshape | solution.py:28
  7.0 1.2 slice.176
  8.2 1.3 collective-permute-start
  9.5 0.0 copy-done.2
  9.5 0.2 fusion.65
  9.7 0.0 copy-done.1
  9.7 0.3 reshape.100
  10.1 0.1 fusion.43
  10.2 1.8 collective-permute-done
  12.0 0.1 broadcast_select_fusion
  12.0 44.5 %add_convert_fusion = bf16[2,2,128,4096]{3,2,1,0:T(8,128)(2,1)} fusion(bf16[2,2,128,4096]{3,2,1,0:T(8,128)(2,1)} %reshape.101, bf16[2,2,15,4096]{3,2,1,0:T(8,128)(2,1)S(1)} %broadcast_select_fusion, f32[4096]{0:T(1024)S(1)} %bitcast.78, f32[4096]{0:T(1024)S(1)} %bitcast.79, f32[4096]{0:T(1024)S(1)} %bitcast.65, f32[4096]{0:T(1024)S(1)} %bitcast.66, ...), kind=kLoop, calls=%fused_computation.14 | loop fusion | flops 195035136 | bytes 9142272 | tf_op jit(solution)/shard_map/convert_element_type | solution.py:42
  56.5 12.6 %reshape.109 = bf16[2,256,64,64]{3,2,1,0:T(8,128)(2,1)} reshape(bf16[2,2,128,4096]{3,2,1,0:T(8,128)(2,1)} %add_convert_fusion) | data formatting | bytes 8388608 | tf_op jit(solution)/shard_map/reshape | solution.py:42
  69.2 13.5 %copy.18 = bf16[2,256,64,64]{1,2,3,0:T(8,128)(2,1)} copy(bf16[2,256,64,64]{3,2,1,0:T(8,128)(2,1)} %reshape.109) | data formatting | bytes 8388608 | tf_op jit(solution)/shard_map/reshape | solution.py:42
  82.7 0.0 copy-start
  82.7 3.7 %convolution_bitcast_fusion = f32[2,256,64,64]{1,2,3,0:T(8,128)S(1)} fusion(bf16[2,256,64,64]{1,2,3,0:T(8,128)(2,1)} %copy.18), kind=kOutput, calls=%fused_computation.58 | convolution fusion | flops 268496896 | bytes 12582912 | tf_op jit(solution)/shard_map/crab,ak->crkb/dot_general | solution.py:48
  86.4 0.0 copy-done
  86.4 1.4 convolution_bitcast_fusion.1
  87.8 2.0 add_convert_fusion.1
  89.8 0.4 pad_maximum_fusion.1
  90.1 3.4 %fusion.21 = f32[2,256,64,64]{1,3,2,0:T(8,128)S(1)} fusion(bf16[2,256,64,64]{1,2,3,0:T(8,128)(2,1)S(1)} %pad_maximum_fusion.1), kind=kOutput, calls=%fused_computation.53 | convolution fusion | flops 268496896 | bytes 12582912 | tf_op jit(solution)/shard_map/crkb,bm->crkm/dot_general | solution.py:59
  93.6 3.5 %fusion.23 = f32[2,256,64,64]{1,3,2,0:T(8,128)S(1)} fusion(bf16[2,256,64,64]{1,2,3,0:T(8,128)(2,1)S(1)} %pad_maximum_fusion.1), kind=kOutput, calls=%fused_computation.55 | convolution fusion | flops 268496896 | bytes 12582912 | tf_op jit(solution)/shard_map/crkb,bm->crkm/dot_general | solution.py:60
  97.1 2.2 fusion.17
  99.2 0.4 maximum_bitcast_fusion
  99.6 4.4 %copy.22 = bf16[2,256,64,64]{1,3,2,0:T(8,128)(2,1)} copy(bf16[2,256,64,64]{1,2,3,0:T(8,128)(2,1)S(1)} %maximum_bitcast_fusion) | data formatting | bytes 8388608 | tf_op jit(solution)/shard_map/convert_element_type | solution.py:65
  104.0 7.0 %reshape_reshape.3 = bf16[2,2,128,16,256]{2,1,4,3,0:T(2,128)(2,1)} reshape(bf16[2,256,64,64]{1,3,2,0:T(8,128)(2,1)} %copy.22) | data formatting | bytes 8388608 | tf_op jit(solution)/shard_map/reshape;reshape | solution.py:70
  111.0 5.6 %copy.23 = bf16[2,2,128,16,256]{2,1,4,0,3:T(2,128)(2,1)S(1)} copy(bf16[2,2,128,16,256]{2,1,4,3,0:T(2,128)(2,1)} %reshape_reshape.3) | data formatting | bytes 8388608 | tf_op jit(solution)/shard_map/reshape;reshape | solution.py:70
  116.5 99.3 %all_to_all.5 = bf16[2,2,128,16,256]{2,1,4,0,3:T(2,128)(2,1)} all-to-all(bf16[2,2,128,16,256]{2,1,4,0,3:T(2,128)(2,1)S(1)} %copy.23), channel_id=1, replica_groups=mesh['grp'=2,'stn'=8,'chan'=2] {'stn','chan'}, dimensions={3} | all-to-all | bytes 8388608 | tf_op jit(solution)/shard_map/all_to_all | solution.py:71
  215.9 11.1 %copy.24 = bf16[2,2,128,16,256]{4,2,3,1,0:T(8,128)(2,1)} copy(bf16[2,2,128,16,256]{2,1,4,0,3:T(2,128)(2,1)} %all_to_all.5) | data formatting | bytes 8388608 | tf_op jit(solution)/shard_map/all_to_all | solution.py:71
  227.0 11.2 %copy.25 = bf16[2,8,2,2,128,256]{4,3,2,1,0,5:T(2,128)(2,1)} copy(bf16[2,8,2,2,128,256]{5,4,3,1,2,0:T(8,128)(2,1)} %bitcast.61) | data formatting | bytes 8388608 | tf_op jit(solution)/shard_map/transpose | solution.py:73
  238.2 7.6 %reshape.107 = bf16[2,16,256,256,1]{2,1,0,3,4:T(8,128)(2,1)} reshape(bf16[2,8,2,2,128,256]{4,3,2,1,0,5:T(2,128)(2,1)} %copy.25) | data formatting | bytes 8388608 | tf_op jit(solution)/shard_map/reshape | solution.py:73
  245.8 9.7 %fusion.25 = f32[2,2,256,16,16]{3,4,0,1,2:T(8,128)S(1)} fusion(bf16[2,16,256,256,1]{2,1,0,3,4:T(8,128)(2,1)} %reshape.107), kind=kOutput, calls=%fused_computation.57 | convolution fusion | flops 134217728 | bytes 5242880 | tf_op jit(solution)/shard_map/xisc,yjsc->xycij/dot_general | solution.py:78
  255.5 1.9 slice_add_fusion.2
  257.4 2.6 copy.26
  260.0 1.1 copy.27
  261.1 1.0 copy.28
  (1 shorter events, 0.0 us)
Async XLA Ops:
  0.0 9.5 %copy-start.2 = (f32[16,4096]{1,0:T(8,128)S(1)}, f32[16,4096]{1,0:T(8,128)}, u32[]{:S(2)}) copy-start(f32[16,4096]{1,0:T(8,128)} %param.5) | copy-start | bytes 786436
  0.0 9.7 %copy-start.1 = (bf16[2,2,61440]{2,1,0:T(2,128)(2,1)S(1)}, bf16[2,2,61440]{2,1,0:T(2,128)(2,1)}, u32[]{:S(2)}) copy-start(bf16[2,2,61440]{2,1,0:T(2,128)(2,1)} %param.4) | copy-start | bytes 1474564
  8.2 3.8 %collective-permute-start = (bf16[2,2,15,4096]{3,2,1,0:T(8,128)(2,1)S(1)}, bf16[2,2,15,4096]{3,2,1,0:T(8,128)(2,1)S(1)}, u32[]{:S(2)}, u32[]{:S(2)}) collective-permute-start(bf16[2,2,15,4096]{3,2,1,0:T(8,128)(2,1)S(1)} %slice.176), channel_id=1, source_target_pairs={{0,1},{2,3},{4,5},{6,7},{8,9},{10,11},{12,13},{14,15},{16,17},{18,... | collective-permute-start | bytes 1474568 | tf_op jit(solution)/shard_map/ppermute | solution.py:14
  82.7 3.7 %copy-start = (bf16[2,256,64,64]{1,2,3,0:T(8,128)(2,1)S(1)}, bf16[2,256,64,64]{1,2,3,0:T(8,128)(2,1)}, u32[]{:S(2)}) copy-start(bf16[2,256,64,64]{1,2,3,0:T(8,128)(2,1)} %copy.18) | copy-start | bytes 12582916
where the time goes:
time: 264 us; the launch traced here: 262 us
  blocking collectives  99.3 us (38%)
  local copies, waits for them, and re-layouts  86.4 us (33%)
  other arithmetic  51.5 us (20%)
  matrix products  21.6 us (8%)
    all_to_all x1, blocking collectives, shards(): lax.all_to_all(shaped, ('stn', 'chan'), split_axis=3, concat_axis=3, tile...  99.3 us
    convert_element_type x1, other arithmetic, shards(): filtered.astype(jnp.bfloat16)  44.5 us
    reshape x2, local copies, waits for them, and re-layouts, shards(): filtered.astype(jnp.bfloat16)  26.2 us
    another operation x2, local copies, waits for them, and re-layouts, shards(): spectra.reshape(components, local_inputs, spectra_here, owners, owned)  12.5 us
    transpose x1, local copies, waits for them, and re-layouts, shards(): jnp.transpose(moved, (0, 3, 1, 4, 2, 5))  11.2 us
    all_to_all x1, local copies, waits for them, and re-layouts, shards(): lax.all_to_all(shaped, ('stn', 'chan'), split_axis=3, concat_axis=3, tile...  11.1 us
    dot_general x1, matrix products, shards(): jnp.einsum('xisc,yjsc->xycij', moved, moved, preferred_element_type=jnp.f...  9.68 us
    reshape x1, local copies, waits for them, and re-layouts, shards(): jnp.transpose(moved, (0, 3, 1, 4, 2, 5))  7.59 us
  transfers between devices with their start and end apart: 1, of which 1 were waited for; matrix products, arithmetic and copies ran while one was open for 0% of the time, Pallas kernels for 0%

commit v1 on v0

v1 whole, which is shorter than its diff:
```python
import functools

import jax
import jax.numpy as jnp
import numpy as np
from jax import lax
from jax.experimental import pallas as pl
from jax.experimental.pallas import tpu as pltpu
from jax.sharding import PartitionSpec as P


FA = 64
LANES = 128
STEP = 8
SHARES = (4, 8, 4)
F32 = jnp.float32
BF16 = jnp.bfloat16
ANY = pl.BlockSpec(memory_space=pl.ANY)
VMEM = pl.BlockSpec(memory_space=pltpu.VMEM)


def cos_sin(index, length):
    angle = (index % length).astype(np.float32) * np.float32(2.0 * np.pi / length)
    return np.cos(angle), np.sin(angle)


def small_tables(length):
    cos, sin = cos_sin(np.outer(np.arange(length), np.arange(length)), length)
    return cos.astype(BF16).astype(np.float32), sin.astype(BF16).astype(np.float32)


def rotation(cos, sin):
    return np.stack([np.stack([cos, sin]), np.stack([-sin, cos])])


def first_table():
    turn = rotation(*small_tables(FA))
    turn = turn.reshape(2, 2, FA // 2, 2, FA)
    table = np.einsum("dchlk,ef->edklchf", turn, np.eye(2))
    return table.reshape(4 * FA, 4 * FA).astype(BF16)


def second_table(length, stations):
    turn = rotation(*small_tables(length)) * (FA * length) ** -0.5
    turn = turn.reshape(2, 2, length, stations, length // stations)
    table = np.einsum("dcbnm,st->nsdmctb", turn, np.eye(2))
    return table.reshape(4 * length, 4 * length).astype(BF16)


def twist_tables(length):
    cos, sin = cos_sin(np.outer(np.arange(FA), np.arange(length)), FA * length)
    return np.stack([np.tile(cos, (1, 2)), np.tile(sin, (1, 2))]).astype(np.float32)


def rows_dot(left, right, axis):
    return lax.dot_general(left, right, (((1,), (axis,)), ((), ())), preferred_element_type=F32)


def spectra_kernel(first, count, taps, stations, last, *refs):
    samples, earlier, passed, prototype, first_hbm, twist_hbm, second_hbm, _ = refs[:8]
    outs = refs[8 : 8 + stations]
    refs = refs[8 + stations :]
    tail = None
    if last:
        tail, refs = refs[0], refs[1:]
    frames, wide, filtered, proto, weights, first_ref, twist_ref, second_in, second, sems = refs
    per = FA
    held = (taps - 1) * per
    total = held + count * per
    tables = [
        pltpu.make_async_copy(source, target, sems.at[at])
        for at, (source, target) in enumerate(
            ((first_hbm, first_ref), (twist_hbm, twist_ref), (second_hbm, second_in))
        )
    ]
    proto_copy = pltpu.make_async_copy(prototype, proto, sems.at[3])
    proto_copy.start()
    lead = 0 if first >= taps - 1 else held
    copies = [
        pltpu.make_async_copy(
            samples.at[comp, pl.ds(first * per - held + lead, total - lead)],
            frames.at[comp, pl.ds(lead, total - lead)],
            sems.at[4 + comp],
        )
        for comp in range(2)
    ]
    for copy in copies + tables:
        copy.start()
    if lead:
        chan = lax.axis_index("chan")
        history = frames.at[:, pl.ds(0, held)]

        @pl.when(chan == 0)
        def _():
            pltpu.make_async_copy(earlier, history, sems.at[6]).start()

        @pl.when(chan != 0)
        def _():
            pltpu.make_async_copy(passed, history, sems.at[6]).start()

        copies.append(pltpu.make_async_copy(earlier, history, sems.at[6]))
    proto_copy.wait()
    for high in range(per // 2):
        for group in range(taps // 8):
            lane = high * LANES
            rows = proto[group * 8 : (group + 1) * 8, lane : lane + LANES]
            for member in range(2):
                at = group * 8 * per + 2 * high + member
                weights[pl.ds(at, 8, stride=per)] = rows
    for copy in copies:
        copy.wait()
    if last:
        tail_copy = pltpu.make_async_copy(
            frames.at[:, pl.ds(count * per, held)], tail, sems.at[6]
        )
        tail_copy.start()

    def widen(frame, carry):
        at = pl.multiple_of(frame * per, per)
        for comp in range(2):
            wide[comp, pl.ds(at, per)] = frames[comp, pl.ds(at, per)].astype(F32)
        return carry

    lax.fori_loop(0, total // per, widen, 0)

    def strip(index, carry):
        comp = index // (per // 16)
        row = (index % (per // 16)) * 16

        def run(block, carry):
            window = []
            for step in range(taps - 1 + STEP):
                at = pl.multiple_of((block * STEP + step) * per + row, 16)
                window.append(wide[comp, pl.ds(at, 16)])
            sums = None
            for tap in range(taps):
                weight = weights[pl.ds(pl.multiple_of(tap * per + row, 16), 16)]
                terms = [weight * window[tap + step] for step in range(STEP)]
                sums = terms if sums is None else [x + y for x, y in zip(sums, terms)]
            for step in range(STEP):
                at = pl.multiple_of(comp * per + row, 16)
                filtered[block * STEP + step, pl.ds(at, 16)] = sums[step].astype(BF16)
            return carry

        return lax.fori_loop(0, count // STEP, run, carry)

    lax.fori_loop(0, 2 * per // 16, strip, 0)
    for copy in tables:
        copy.wait()
    share = second_in.shape[0] // stations
    me = lax.axis_index("stn")
    for offset in range(stations):
        start = pl.multiple_of((me ^ offset) * share, share)
        second[offset * share : (offset + 1) * share] = second_in[pl.ds(start, share)]
    low_half = lax.broadcasted_iota(jnp.int32, (2 * per, LANES), 1) < LANES // 2

    def transform(index, carry):
        mixed = []
        for pair in range(2):
            even = filtered[index * 4 + 2 * pair].astype(F32)
            odd = filtered[index * 4 + 2 * pair + 1].astype(F32)
            low = jnp.where(low_half, even, pltpu.roll(odd, LANES // 2, 1))
            high = jnp.where(low_half, pltpu.roll(even, LANES // 2, 1), odd)
            mixed.append(jnp.concatenate([low.astype(BF16), high.astype(BF16)], axis=0))
        g = rows_dot(first_ref[...], jnp.concatenate(mixed, axis=1), 0)
        cos, sin = twist_ref[0], twist_ref[1]
        inner = []
        for member in range(2):
            for pair in range(2):
                lane = pair * LANES
                g_re = g[2 * member * FA : (2 * member + 1) * FA, lane : lane + LANES]
                g_im = g[(2 * member + 1) * FA : (2 * member + 2) * FA, lane : lane + LANES]
                inner_re = (g_re * cos + g_im * sin).astype(BF16)
                inner_im = (g_im * cos - g_re * sin).astype(BF16)
                inner.append(jnp.concatenate([inner_re, inner_im], axis=1))
        spectra = rows_dot(second[...], jnp.concatenate(inner, axis=0), 1).astype(BF16)
        for member in range(2):
            lane = member * LANES
            for offset in range(stations):
                row = offset * share
                outs[offset][index, member] = spectra[row : row + share, lane : lane + LANES]
        return carry

    lax.fori_loop(0, count // 4, transform, 0, unroll=2)
    if last:
        tail_copy.wait()


def spectra_of(first, count, samples, earlier, passed, prototype, after, stations, last):
    taps, channels = prototype.shape
    length = channels // FA
    share = 4 * length // stations
    held = (taps - 1) * FA
    rows = held + count * FA
    tables = (first_table(), twist_tables(length), second_table(length, stations))
    out_shape = [jax.ShapeDtypeStruct((count // 4, 2, share, LANES), BF16)] * stations
    if last:
        out_shape.append(jax.ShapeDtypeStruct((2, held, LANES), BF16))
    return pl.pallas_call(
        functools.partial(spectra_kernel, first, count, taps, stations, last),
        out_shape=out_shape,
        in_specs=[ANY] * 8,
        out_specs=[VMEM] * stations + [ANY] * last,
        scratch_shapes=[
            pltpu.VMEM((2, rows, LANES), BF16),
            pltpu.VMEM((2, rows, LANES), F32),
            pltpu.VMEM((count, 2 * FA, LANES), BF16),
            pltpu.VMEM((taps, channels), F32),
            pltpu.VMEM((taps * FA, LANES), F32),
            pltpu.VMEM((4 * FA, 4 * FA), BF16),
            pltpu.VMEM((2, FA, LANES), F32),
            pltpu.VMEM((4 * length, 4 * length), BF16),
            pltpu.VMEM((4 * length, 4 * length), BF16),
            pltpu.SemaphoreType.DMA((7,)),
        ],
        cost_estimate=pl.CostEstimate(
            flops=count * 8 * 10**6, bytes_accessed=count * 65536, transcendentals=0
        ),
    )(samples, earlier, passed, prototype, *tables, after)


def pair_rows(inputs):
    pairs = [(a, b) for a in range(inputs) for b in range(a, inputs)]
    return {pair: row for row, pair in enumerate(pairs)}


def products_kernel(stations, carried, fold, *refs):
    blocks = refs[:stations]
    before = refs[stations] if carried else None
    out = refs[-1]
    rows = pair_rows(2 * stations)
    span = blocks[0].shape[2] // 4
    group = 4

    def load(member, step, low):
        tile = blocks[member // 2][step, member % 2, low * 2 * span : (low + 1) * 2 * span]
        both = tile.astype(F32)
        return both[:span], both[span:]

    for left in range(0, 2 * stations, group):
        for right in range(left, 2 * stations, group):
            a_list = range(left, left + group)
            b_list = range(right, right + group)
            members = [(a, b) for a in a_list for b in b_list if a <= b]
            wanted = [(a, b, comp) for a, b in members for comp in range(2) if a != b or comp == 0]

            def body(step, sums):
                for low in range(2):
                    a_side = {a: load(a, step, low) for a in a_list}
                    b_side = a_side
                    if right != left:
                        b_side = {b: load(b, step, low) for b in b_list}
                    new = []
                    for total, (a, b, comp) in zip(sums, wanted):
                        a_re, a_im = a_side[a]
                        b_re, b_im = b_side[b]
                        if comp == 0:
                            new.append(total + a_re * b_re + a_im * b_im)
                        else:
                            new.append(total + a_im * b_re - a_re * b_im)
                    sums = new
                return sums

            start = []
            for a, b, comp in wanted:
                at = (2 * rows[a, b] + comp) * span
                if carried:
                    start.append(before[at : at + span])
                else:
                    start.append(jnp.zeros((span, LANES), F32))
            sums = lax.fori_loop(0, blocks[0].shape[0], body, start)
            sums = dict(zip(wanted, sums))
            for a, b in members:
                re = sums[a, b, 0]
                im = sums.get((a, b, 1), jnp.zeros_like(re))
                at = rows[a, b] * span
                if fold:
                    low_half = lax.broadcasted_iota(jnp.int32, re.shape, 1) < LANES // 2
                    re = re + pltpu.roll(re, LANES // 2, 1)
                    im = im + pltpu.roll(im, LANES // 2, 1)
                    out[at : at + span] = jnp.where(low_half, re, im)
                else:
                    out[2 * at : 2 * at + span] = re
                    out[2 * at + span : 2 * at + 2 * span] = im


def products_of(blocks, before, fold):
    stations = len(blocks)
    count = len(pair_rows(2 * stations)) * (1 if fold else 2)
    span = blocks[0].shape[2] // 4
    carried = before is not None
    arrays = list(blocks) + ([before] if carried else [])
    steps = 4 * blocks[0].shape[0]
    return pl.pallas_call(
        functools.partial(products_kernel, stations, carried, fold),
        out_shape=jax.ShapeDtypeStruct((count * span, LANES), F32),
        in_specs=[VMEM] * len(arrays),
        out_specs=VMEM,
        cost_estimate=pl.CostEstimate(
            flops=steps * 4 * 10**6, bytes_accessed=steps * 65536, transcendentals=0
        ),
        name="products",
    )(*arrays)


def visibility_kernel(stations, total, own, other, out):
    inputs = 2 * stations
    rows = pair_rows(inputs)
    count = len(rows)
    span = own.shape[0] // count
    mine = span // 2
    width = inputs * inputs
    turn = 2 * lax.axis_index("stn")
    row = lax.broadcasted_iota(jnp.int32, (count, width), 0)
    col = lax.broadcasted_iota(jnp.int32, (count, width), 1)
    i_rel = jnp.zeros_like(row)
    for a in range(1, inputs):
        i_rel = i_rel + (row >= rows[a, a]).astype(jnp.int32)
    j_rel = row - (i_rel * inputs - i_rel * (i_rel - 1) // 2) + i_rel
    i_at, j_at = i_rel ^ turn, j_rel ^ turn
    plain = col == i_at * inputs + j_at
    mirror = col == j_at * inputs + i_at
    picks = [
        jnp.where(plain, 1.0, jnp.where(mirror, sign, 0.0)).astype(BF16) for sign in (1.0, -1.0)
    ]
    core = lax.axis_index("chan")
    for low in range(mine):
        at = pl.ds(core * mine + low, count, stride=span)
        lanes = ((own[at] + other[at]) * (1.0 / total)).T
        for comp in range(2):
            rest = lanes[comp * FA : (comp + 1) * FA]
            value = None
            for _ in range(3):
                piece = rest.astype(BF16)
                part = rows_dot(piece, picks[comp], 0)
                value = part if value is None else value + part
                rest = rest - piece.astype(F32)
            out[comp, low * FA : (low + 1) * FA] = value


def send_order(stations):
    return sorted(range(1, stations), key=lambda d: (d < stations // 2, d))


def shards(voltage, earlier_samples, prototype):
    components, local_inputs, samples = voltage.shape
    _, channels = prototype.shape
    spectra_here = samples // channels
    length = channels // FA
    stations = lax.axis_size("stn")
    cores = lax.axis_size("chan")
    total = spectra_here * cores

    def by_tile(block):
        tiles = block.reshape(components, local_inputs, -1, LANES)
        return jnp.transpose(tiles, (0, 2, 1, 3)).reshape(components, -1, LANES)

    stream = by_tile(voltage)
    earlier = by_tile(earlier_samples)
    whole = sum(SHARES)
    first = spectra_here
    chunks = []
    passed, after = earlier, earlier
    for chunk, share in enumerate(SHARES):
        count = spectra_here * share // whole
        first -= count
        history = earlier if first else passed
        blocks = list(
            spectra_of(
                first, count, stream, earlier, history, prototype, after, stations, chunk == 0
            )
        )
        if chunk == 0:
            route = [(i, i + 1) for i in range(cores - 1)]
            passed = lax.ppermute(blocks.pop(), "chan", route)
        after = blocks[0]
        chunks.append(blocks)
    if 2 * length // stations == 16:
        sums = None
        for chunk, blocks in enumerate(chunks):
            for offset in send_order(stations):
                route = [(i, i ^ offset) for i in range(stations)]
                blocks[offset] = lax.ppermute(blocks[offset], "stn", route)
            sums = products_of(blocks, sums, chunk == len(chunks) - 1)
        other = lax.ppermute(sums, "chan", [(i, i ^ 1) for i in range(cores)])
        owned = channels // (stations * cores)
        return pl.pallas_call(
            functools.partial(visibility_kernel, stations, total),
            out_shape=jax.ShapeDtypeStruct((2, owned, 4 * stations * stations), F32),
            in_specs=[VMEM, VMEM],
            out_specs=VMEM,
            name="visibility",
        )(sums, other)
    joined = [jnp.concatenate([blocks[d] for blocks in chunks]) for d in range(stations)]
    joined = jnp.stack(joined)[jnp.arange(stations) ^ lax.axis_index("stn")]
    span = length // stations // cores
    joined = joined.reshape(stations, spectra_here // 4, 2, 2, 2, cores, span, 2, FA)
    joined = jnp.transpose(joined, (4, 2, 1, 7, 3, 0, 5, 6, 8))
    joined = joined.reshape(2, 2, spectra_here, stations * cores, span * FA)
    moved = lax.all_to_all(joined, ("stn", "chan"), split_axis=3, concat_axis=3, tiled=True)
    moved = moved.reshape(2, 2, spectra_here, stations, cores, span * FA)
    moved = jnp.transpose(moved, (0, 3, 1, 4, 2, 5))
    moved = moved.reshape(2, 2 * stations, total, span * FA)
    products = jnp.einsum("xisc,yjsc->xycij", moved, moved, preferred_element_type=F32)
    real_sum = products[0, 0] + products[1, 1]
    imag_sum = products[1, 0] - products[0, 1]
    averaged = jnp.stack([real_sum, imag_sum]) / total
    return averaged.reshape(2, span * FA, 4 * stations * stations)


def solution(mesh):
    in_specs = (P(None, ("grp", "stn"), "chan"), P(None, ("grp", "stn"), None), P())
    out_specs = P(None, ("grp", "stn", "chan"), None)

    return jax.shard_map(shards, mesh=mesh, in_specs=in_specs, out_specs=out_specs, check_vma=False)
```

time: 264 us -> 138 us (0.52)
  blocking collectives: 99.3 us -> 0 us
  local copies, waits for them, and re-layouts: 86.4 us -> 1.59 us
  Pallas kernels: 0 us -> 52.9 us
  other arithmetic: 51.5 us -> 0 us
  starting transfers between devices: 1.29 us -> 52.4 us
  waiting for transfers between devices: 1.76 us -> 29.7 us
  matrix products: 21.6 us -> 0 us
    all_to_all x1 -> x0, blocking collectives: 99.3 us -> none  [shards(): lax.all_to_all(shaped, ('stn', 'chan'), split_axis=3, concat_axis=3, tile...]
    pallas_call x0 -> x7, Pallas kernels: none -> 52.9 us  [the longest x3 29.6 us: spectra_of(): pl.pallas_call(functools.partial(spectra_kernel, first, count, taps, stat...]
    ppermute x1 -> x23, starting transfers between devices: 1.29 us -> 52.4 us  [the longest x21 38.2 us: shards(): blocks[offset] = lax.ppermute(blocks[offset], 'stn', route)]
    convert_element_type x2 -> x0, other arithmetic: 44.9 us -> none  [the longest x1 44.5 us: shards(): filtered.astype(jnp.bfloat16)]
    reshape x5 -> x0, local copies, waits for them, and re-layouts: 41.1 us -> none  [the longest x2 26.2 us: shards(): filtered.astype(jnp.bfloat16)]
    ppermute x1 -> x23, waiting for transfers between devices: 1.76 us -> 29.7 us  [the longest x21 27.9 us: shards(): blocks[offset] = lax.ppermute(blocks[offset], 'stn', route)]
    dot_general x5 -> x0, matrix products: 21.6 us -> none  [the longest x1 9.68 us: shards(): jnp.einsum('xisc,yjsc->xycij', moved, moved, preferred_element_type=jnp.f...]
    another operation x2 -> x0, local copies, waits for them, and re-layouts: 12.5 us -> none  [shards(): spectra.reshape(components, local_inputs, spectra_here, owners, owned)]
  transfers between devices with their start and end apart: 1 -> 23, of which waited for: 1 -> 4; matrix products, arithmetic and copies ran while one was open for 0% -> 0% of each run, Pallas kernels for 0% -> 26%
where the time goes in v1:
time: 138 us; the launch traced here: 137 us
  Pallas kernels  52.9 us (38%)
  starting transfers between devices  52.4 us (38%)
  waiting for transfers between devices  29.7 us (22%)
  local copies, waits for them, and re-layouts  1.59 us (1%)
    ppermute x21, starting transfers between devices, shards(): blocks[offset] = lax.ppermute(blocks[offset], 'stn', route)  38.2 us
    pallas_call x3, Pallas kernels, spectra_of(): pl.pallas_call(functools.partial(spectra_kernel, first, count, taps, stat...  29.6 us
    ppermute x21, waiting for transfers between devices, shards(): blocks[offset] = lax.ppermute(blocks[offset], 'stn', route)  27.9 us
    pallas_call x3, Pallas kernels, products_of(): pl.pallas_call(functools.partial(products_kernel, stations, carried, fold...  20.7 us
    ppermute x1, starting transfers between devices, shards(): other = lax.ppermute(sums, 'chan', [(i, i ^ 1) for i in range(cores)])  13 us
  transfers between devices with their start and end apart: 23, of which 4 were waited for; matrix products, arithmetic and copies ran while one was open for 0% of the time, Pallas kernels for 26%

profile of v1, /device:TPU:1, one launch (start us, length us, event | category | flops | bytes accessed | tf_op | source)
XLA Modules:
  0.0 136.9 jit_solution(7794601934245220340)
XLA Ops:
  0.0 7.9 %shard_map.118 = (bf16[8,2,32,128]{3,2,1,0:T(8,128)(2,1)}, bf16[8,2,32,128]{3,2,1,0:T(8,128)(2,1)}, bf16[8,2,32,128]{3,2,1,0:T(8,128)(2,1)}, bf16[8,2,32,128]{3,...) custom-call(bf16[2,8192,128]{2,1,0:T(8,128)(2,1)} %bitcast.10, ...), custom_call_target="tpu_custom_call" | custom-call | flops 256000000 | bytes 2097152 | tf_op jit(solution)/shard_map/pallas_call | solution.py:199
  7.9 2.1 %collective-permute-start.15 = (bf16[8,2,32,128]{3,2,1,0:T(8,128)(2,1)}, bf16[8,2,32,128]{3,2,1,0:T(8,128)(2,1)S(1)}, u32[]{:S(2)}, u32[]{:S(2)}) collective-permute-start(bf16[8,2,32,128]{3,2,1,0:T(8,128)(2,1)} %get-tuple-element.48), channel_id=1, source_target_pairs={{0,2},{2,0},{4,6},{6,4},{8,10},{10,8},{12,14},{14,12},{1,3},{3,1},... | collective-permute-start | bytes 393224 | tf_op jit(solution)/shard_map/ppermute | solution.py:383
  10.0 1.3 collective-permute-start
  11.3 1.4 collective-permute-start.16
  12.7 0.0 collective-permute-start.17
  12.7 2.4 %collective-permute-start.18 = (bf16[8,2,32,128]{3,2,1,0:T(8,128)(2,1)}, bf16[8,2,32,128]{3,2,1,0:T(8,128)(2,1)S(1)}, u32[]{:S(2)}, u32[]{:S(2)}) collective-permute-start(bf16[8,2,32,128]{3,2,1,0:T(8,128)(2,1)} %get-tuple-element.51), channel_id=1, source_target_pairs={{0,8},{2,10},{4,12},{6,14},{8,0},{10,2},{12,4},{14,6},{1,9},{3,11}... | collective-permute-start | bytes 393224 | tf_op jit(solution)/shard_map/ppermute | solution.py:383
  15.1 1.5 %collective-permute-start.19 = (bf16[8,2,32,128]{3,2,1,0:T(8,128)(2,1)}, bf16[8,2,32,128]{3,2,1,0:T(8,128)(2,1)S(1)}, u32[]{:S(2)}, u32[]{:S(2)}) collective-permute-start(bf16[8,2,32,128]{3,2,1,0:T(8,128)(2,1)} %get-tuple-element.52), channel_id=1, source_target_pairs={{0,10},{2,8},{4,14},{6,12},{8,2},{10,0},{12,6},{14,4},{1,11},{3,9}... | collective-permute-start | bytes 393224 | tf_op jit(solution)/shard_map/ppermute | solution.py:383
  16.6 13.8 %shard_map.119 = (bf16[16,2,32,128]{3,2,1,0:T(8,128)(2,1)}, bf16[16,2,32,128]{3,2,1,0:T(8,128)(2,1)}, bf16[16,2,32,128]{3,2,1,0:T(8,128)(2,1)}, bf16[16,2,32,128...) custom-call(bf16[2,8192,128]{2,1,0:T(8,128)(2,1)} %bitcast.11, ...), custom_call_target="tpu_custom_call" | custom-call | flops 512000000 | bytes 4194304 | tf_op jit(solution)/shard_map/pallas_call | solution.py:199
  30.5 0.0 collective-permute-done.16.refs_2_
  30.5 0.3 collective-permute-start.8
  30.8 1.3 collective-permute-start.9
  32.1 1.7 %collective-permute-start.20 = (bf16[8,2,32,128]{3,2,1,0:T(8,128)(2,1)S(1)}, bf16[8,2,32,128]{3,2,1,0:T(8,128)(2,1)S(1)}, u32[]{:S(2)}, u32[]{:S(2)}) collective-permute-start(bf16[8,2,32,128]{3,2,1,0:T(8,128)(2,1)S(1)} %copy-done.23), channel_id=1, source_target_pairs={{0,12},{2,14},{4,8},{6,10},{8,4},{10,6},{12,0},{14,2},{1,13},{3,15... | collective-permute-start | bytes 393224 | tf_op jit(solution)/shard_map/ppermute | solution.py:383
  33.8 0.0 collective-permute-done.19.refs_5_
  33.8 2.6 %collective-permute-start.21 = (bf16[8,2,32,128]{3,2,1,0:T(8,128)(2,1)S(1)}, bf16[8,2,32,128]{3,2,1,0:T(8,128)(2,1)S(1)}, u32[]{:S(2)}, u32[]{:S(2)}) collective-permute-start(bf16[8,2,32,128]{3,2,1,0:T(8,128)(2,1)S(1)} %copy-done.22), channel_id=1, source_target_pairs={{0,14},{2,12},{4,10},{6,8},{8,6},{10,4},{12,2},{14,0},{1,15},{3,13... | collective-permute-start | bytes 393224 | tf_op jit(solution)/shard_map/ppermute | solution.py:383
  36.4 3.9 %collective-permute-done.20.refs_6_ = bf16[8,2,32,128]{3,2,1,0:T(8,128)(2,1)S(1)} collective-permute-done((bf16[8,2,32,128]{3,2,1,0:T(8,128)(2,1)S(1)}, bf16[8,2,32,128]{3,2,1,0:T(8,128)(2,1)S(1)}, u32[]{:S(2)}, u32[]{:S(2)}) %collective-permute-start.20) | collective-permute-done | bytes 131104 | tf_op jit(solution)/shard_map/ppermute | solution.py:383
  40.3 3.8 %collective-permute-done.21.refs_7_ = bf16[8,2,32,128]{3,2,1,0:T(8,128)(2,1)S(1)} collective-permute-done((bf16[8,2,32,128]{3,2,1,0:T(8,128)(2,1)S(1)}, bf16[8,2,32,128]{3,2,1,0:T(8,128)(2,1)S(1)}, u32[]{:S(2)}, u32[]{:S(2)}) %collective-permute-start.21) | collective-permute-done | bytes 131104 | tf_op jit(solution)/shard_map/ppermute | solution.py:383
  44.1 0.0 collective-permute-done.8.refs_1_
  44.1 2.3 %collective-permute-start.12 = (bf16[16,2,32,128]{3,2,1,0:T(8,128)(2,1)}, bf16[16,2,32,128]{3,2,1,0:T(8,128)(2,1)S(1)}, u32[]{:S(2)}, u32[]{:S(2)}) collective-permute-start(bf16[16,2,32,128]{3,2,1,0:T(8,128)(2,1)} %get-tuple-element.45), channel_id=1, source_target_pairs={{0,10},{2,8},{4,14},{6,12},{8,2},{10,0},{12,6},{14,4},{1,11},{3,9}... | collective-permute-start | bytes 786440 | tf_op jit(solution)/shard_map/ppermute | solution.py:383
  46.4 0.0 collective-permute-done.9.refs_2_
  46.4 2.1 %collective-permute-start.13 = (bf16[16,2,32,128]{3,2,1,0:T(8,128)(2,1)}, bf16[16,2,32,128]{3,2,1,0:T(8,128)(2,1)S(1)}, u32[]{:S(2)}, u32[]{:S(2)}) collective-permute-start(bf16[16,2,32,128]{3,2,1,0:T(8,128)(2,1)} %get-tuple-element.46), channel_id=1, source_target_pairs={{0,12},{2,14},{4,8},{6,10},{8,4},{10,6},{12,0},{14,2},{1,13},{3,15... | collective-permute-start | bytes 786440 | tf_op jit(solution)/shard_map/ppermute | solution.py:383
  48.5 0.0 collective-permute-done.refs_2_
  48.5 2.2 %collective-permute-start.14 = (bf16[16,2,32,128]{3,2,1,0:T(8,128)(2,1)}, bf16[16,2,32,128]{3,2,1,0:T(8,128)(2,1)S(1)}, u32[]{:S(2)}, u32[]{:S(2)}) collective-permute-start(bf16[16,2,32,128]{3,2,1,0:T(8,128)(2,1)} %get-tuple-element.47), channel_id=1, source_target_pairs={{0,14},{2,12},{4,10},{6,8},{8,6},{10,4},{12,2},{14,0},{1,15},{3,13... | collective-permute-start | bytes 786440 | tf_op jit(solution)/shard_map/ppermute | solution.py:383
  50.6 7.9 %shard_map.120 = (bf16[8,2,32,128]{3,2,1,0:T(8,128)(2,1)}, bf16[8,2,32,128]{3,2,1,0:T(8,128)(2,1)}, bf16[8,2,32,128]{3,2,1,0:T(8,128)(2,1)}, bf16[8,2,32,128]{3,...) custom-call(bf16[2,8192,128]{2,1,0:T(8,128)(2,1)} %bitcast.12, ...), custom_call_target="tpu_custom_call" | custom-call | flops 256000000 | bytes 2097152 | tf_op jit(solution)/shard_map/pallas_call | solution.py:199
  58.5 0.0 collective-permute-done.10.refs_3_
  58.6 0.0 copy-start.4
  58.6 0.3 collective-permute-start.1
  58.9 0.0 collective-permute-done.11.refs_4_
  58.9 20.2 %collective-permute-done.12.refs_5_ = bf16[16,2,32,128]{3,2,1,0:T(8,128)(2,1)S(1)} collective-permute-done((bf16[16,2,32,128]{3,2,1,0:T(8,128)(2,1)}, bf16[16,2,32,128]{3,2,1,0:T(8,128)(2,1)S(1)}, u32[]{:S(2)}, u32[]{:S(2)}) %collective-permute-start.12) | collective-permute-done | bytes 262176 | tf_op jit(solution)/shard_map/ppermute | solution.py:383
  79.1 0.0 collective-permute-start.3
  79.1 0.0 collective-permute-done.13.refs_6_
  79.1 6.6 %collective-permute-start.4 = (bf16[8,2,32,128]{3,2,1,0:T(8,128)(2,1)}, bf16[8,2,32,128]{3,2,1,0:T(8,128)(2,1)S(1)}, u32[]{:S(2)}, u32[]{:S(2)}) collective-permute-start(bf16[8,2,32,128]{3,2,1,0:T(8,128)(2,1)} %get-tuple-element.37), channel_id=1, source_target_pairs={{0,8},{2,10},{4,12},{6,14},{8,0},{10,2},{12,4},{14,6},{1,9},{3,11}... | collective-permute-start | bytes 393224 | tf_op jit(solution)/shard_map/ppermute | solution.py:383
  85.8 0.0 collective-permute-done.14.refs_7_
  85.8 7.6 %collective-permute-start.5 = (bf16[8,2,32,128]{3,2,1,0:T(8,128)(2,1)}, bf16[8,2,32,128]{3,2,1,0:T(8,128)(2,1)S(1)}, u32[]{:S(2)}, u32[]{:S(2)}) collective-permute-start(bf16[8,2,32,128]{3,2,1,0:T(8,128)(2,1)} %get-tuple-element.38), channel_id=1, source_target_pairs={{0,10},{2,8},{4,14},{6,12},{8,2},{10,0},{12,6},{14,4},{1,11},{3,9}... | collective-permute-start | bytes 393224 | tf_op jit(solution)/shard_map/ppermute | solution.py:383
  93.4 1.3 collective-permute-start.6
  94.7 0.0 collective-permute-done.2.refs_2_
  94.7 2.4 %collective-permute-start.7 = (bf16[8,2,32,128]{3,2,1,0:T(8,128)(2,1)}, bf16[8,2,32,128]{3,2,1,0:T(8,128)(2,1)}, u32[]{:S(2)}, u32[]{:S(2)}) collective-permute-start(bf16[8,2,32,128]{3,2,1,0:T(8,128)(2,1)} %get-tuple-element.40), channel_id=1, source_target_pairs={{0,14},{2,12},{4,10},{6,8},{8,6},{10,4},{12,2},{14,0},{1,15},{3,13... | collective-permute-start | bytes 393224 | tf_op jit(solution)/shard_map/ppermute | solution.py:383
  97.2 5.3 %products.3.refs_8_ = f32[2176,128]{1,0:T(8,128)} custom-call(bf16[8,2,32,128]{3,2,1,0:T(8,128)(2,1)} %get-tuple-element.31.refs_7_.refs_0_, bf16[8,2,32,128]{3,2,1,0:T(8,128)(2,1)} %copy-done.9, bf16[8,2,32,128]{3,2,1,0:T(8,128)(2,1)} %copy-done.10, bf16[8,2,32,128]{3,2,1,0:T(8,128)(2,1)} %copy-done.11, bf16[8,2,32,128]{3,2,1,0:T(8,128)(2,1)} %copy-done.12, ...), custom_call_target="tpu_custom_call" | custom-call | flops 128000000 | bytes 2097152 | tf_op jit(solution)/shard_map/products/pallas_call | solution.py:294
  102.6 9.0 %products.4.refs_8_ = f32[2176,128]{1,0:T(8,128)} custom-call(bf16[16,2,32,128]{3,2,1,0:T(8,128)(2,1)} %get-tuple-element.32.refs_7_.refs_0_, bf16[16,2,32,128]{3,2,1,0:T(8,128)(2,1)} %copy-done.2, bf16[16,2,32,128]{3,2,1,0:T(8,128)(2,1)} %copy-done.3, bf16[16,2,32,128]{3,2,1,0:T(8,128)(2,1)} %copy-done.4, bf16[16,2,32,128]{3,2,1,0:T(8,128)(2,1)} %copy-done.5, ...), custom_call_target="tpu_custom_call" | custom-call | flops 256000000 | bytes 4194304 | tf_op jit(solution)/shard_map/products/pallas_call | solution.py:294
  111.5 0.0 copy-start.18
  111.6 0.6 copy-done.18
  112.2 0.1 copy-done.19
  112.3 0.0 copy-done.20
  112.3 0.0 copy-done.21
  112.3 6.4 %products.5.own = f32[1088,128]{1,0:T(8,128)} custom-call(bf16[8,2,32,128]{3,2,1,0:T(8,128)(2,1)} %get-tuple-element.33.refs_0_, bf16[8,2,32,128]{3,2,1,0:T(8,128)(2,1)} %copy-done.16, bf16[8,2,32,128]{3,2,1,0:T(8,128)(2,1)} %copy-done.17, bf16[8,2,32,128]{3,2,1,0:T(8,128)(2,1)} %copy-done.18, bf16[8,2,32,128]{3,2,1,0:T(8,128)(2,1)} %copy-done.19, ...), custom_call_target="tpu_custom_call" | custom-call | flops 128000000 | bytes 2097152 | tf_op jit(solution)/shard_map/products/pallas_call | solution.py:294
  118.7 13.0 %collective-permute-start.22 = (f32[1088,128]{1,0:T(8,128)}, f32[1088,128]{1,0:T(8,128)S(1)}, u32[]{:S(2)}, u32[]{:S(2)}) collective-permute-start(f32[1088,128]{1,0:T(8,128)} %products.5.own), channel_id=1, source_target_pairs={{0,1},{1,0},{2,3},{3,2},{4,5},{5,4},{6,7},{7,6},{8,9},{9,8},{10,11... | collective-permute-start | bytes 1671176 | tf_op jit(solution)/shard_map/ppermute | solution.py:385
  131.7 1.8 %collective-permute-done.22.other = f32[1088,128]{1,0:T(8,128)S(1)} collective-permute-done((f32[1088,128]{1,0:T(8,128)}, f32[1088,128]{1,0:T(8,128)S(1)}, u32[]{:S(2)}, u32[]{:S(2)}) %collective-permute-start.22) | collective-permute-done | bytes 557088 | tf_op jit(solution)/shard_map/ppermute | solution.py:385
  133.5 0.8 copy-done
  134.3 2.6 %visibility.1 = f32[2,256,256]{2,1,0:T(8,128)} custom-call(f32[1088,128]{1,0:T(8,128)} %products.5.own, f32[1088,128]{1,0:T(8,128)} %copy-done), custom_call_target="tpu_custom_call" | custom-call | tf_op jit(solution)/shard_map/visibility/pallas_call | solution.py:387
  (53 shorter events, 0.1 us)
Async XLA Ops:
  7.9 7.2 %collective-permute-start.15 = (bf16[8,2,32,128]{3,2,1,0:T(8,128)(2,1)}, bf16[8,2,32,128]{3,2,1,0:T(8,128)(2,1)S(1)}, u32[]{:S(2)}, u32[]{:S(2)}) collective-permute-start(bf16[8,2,32,128]{3,2,1,0:T(8,128)(2,1)} %get-tuple-element.48), channel_id=1, source_target_pairs={{0,2},{2,0},{4,6},{6,4},{8,10},{10,8},{12,14},{14,12},{1,3},{3,1},... | collective-permute-start | bytes 393224 | tf_op jit(solution)/shard_map/ppermute | solution.py:383
  10.0 38.4 %collective-permute-start = (bf16[2,960,128]{2,1,0:T(8,128)(2,1)}, bf16[2,960,128]{2,1,0:T(8,128)(2,1)S(1)}, u32[]{:S(2)}, u32[]{:S(2)}) collective-permute-start(bf16[2,960,128]{2,1,0:T(8,128)(2,1)} %get-tuple-element.30), channel_id=1, source_target_pairs={{0,1},{2,3},{4,5},{6,7},{8,9},{10,11},{12,13},{14,15},{16,17},{18,... | collective-permute-start | bytes 1474568 | tf_op jit(solution)/shard_map/ppermute | solution.py:375
  11.3 19.1 %collective-permute-start.16 = (bf16[8,2,32,128]{3,2,1,0:T(8,128)(2,1)}, bf16[8,2,32,128]{3,2,1,0:T(8,128)(2,1)S(1)}, u32[]{:S(2)}, u32[]{:S(2)}) collective-permute-start(bf16[8,2,32,128]{3,2,1,0:T(8,128)(2,1)} %get-tuple-element.49), channel_id=1, source_target_pairs={{0,4},{2,6},{4,0},{6,2},{8,12},{10,14},{12,8},{14,10},{1,5},{3,7},... | collective-permute-start | bytes 393224 | tf_op jit(solution)/shard_map/ppermute | solution.py:383
  12.7 18.1 %collective-permute-start.17 = (bf16[8,2,32,128]{3,2,1,0:T(8,128)(2,1)}, bf16[8,2,32,128]{3,2,1,0:T(8,128)(2,1)S(1)}, u32[]{:S(2)}, u32[]{:S(2)}) collective-permute-start(bf16[8,2,32,128]{3,2,1,0:T(8,128)(2,1)} %get-tuple-element.50), channel_id=1, source_target_pairs={{0,6},{2,4},{4,2},{6,0},{8,14},{10,12},{12,10},{14,8},{1,7},{3,5},... | collective-permute-start | bytes 393224 | tf_op jit(solution)/shard_map/ppermute | solution.py:383
  12.7 19.4 %collective-permute-start.18 = (bf16[8,2,32,128]{3,2,1,0:T(8,128)(2,1)}, bf16[8,2,32,128]{3,2,1,0:T(8,128)(2,1)S(1)}, u32[]{:S(2)}, u32[]{:S(2)}) collective-permute-start(bf16[8,2,32,128]{3,2,1,0:T(8,128)(2,1)} %get-tuple-element.51), channel_id=1, source_target_pairs={{0,8},{2,10},{4,12},{6,14},{8,0},{10,2},{12,4},{14,6},{1,9},{3,11}... | collective-permute-start | bytes 393224 | tf_op jit(solution)/shard_map/ppermute | solution.py:383
  15.1 15.3 %copy-start.9 = (bf16[8,2,32,128]{3,2,1,0:T(8,128)(2,1)}, bf16[8,2,32,128]{3,2,1,0:T(8,128)(2,1)S(1)}, u32[]{:S(2)}) copy-start(bf16[8,2,32,128]{3,2,1,0:T(8,128)(2,1)S(1)} %collective-permute-done.15.refs_1_) | copy-start | bytes 393220
  15.1 18.7 %collective-permute-start.19 = (bf16[8,2,32,128]{3,2,1,0:T(8,128)(2,1)}, bf16[8,2,32,128]{3,2,1,0:T(8,128)(2,1)S(1)}, u32[]{:S(2)}, u32[]{:S(2)}) collective-permute-start(bf16[8,2,32,128]{3,2,1,0:T(8,128)(2,1)} %get-tuple-element.52), channel_id=1, source_target_pairs={{0,10},{2,8},{4,14},{6,12},{8,2},{10,0},{12,6},{14,4},{1,11},{3,9}... | collective-permute-start | bytes 393224 | tf_op jit(solution)/shard_map/ppermute | solution.py:383
  16.6 15.4 %copy-start.23 = (bf16[8,2,32,128]{3,2,1,0:T(8,128)(2,1)S(1)}, bf16[8,2,32,128]{3,2,1,0:T(8,128)(2,1)}, u32[]{:S(2)}) copy-start(bf16[8,2,32,128]{3,2,1,0:T(8,128)(2,1)} %get-tuple-element.53) | copy-start | bytes 393220
  16.6 17.2 %copy-start.22 = (bf16[8,2,32,128]{3,2,1,0:T(8,128)(2,1)S(1)}, bf16[8,2,32,128]{3,2,1,0:T(8,128)(2,1)}, u32[]{:S(2)}) copy-start(bf16[8,2,32,128]{3,2,1,0:T(8,128)(2,1)} %get-tuple-element.54) | copy-start | bytes 393220
  30.5 66.7 %copy-start.10 = (bf16[8,2,32,128]{3,2,1,0:T(8,128)(2,1)}, bf16[8,2,32,128]{3,2,1,0:T(8,128)(2,1)S(1)}, u32[]{:S(2)}) copy-start(bf16[8,2,32,128]{3,2,1,0:T(8,128)(2,1)S(1)} %collective-permute-done.16.refs_2_) | copy-start | bytes 393220
  30.5 13.6 %collective-permute-start.8 = (bf16[16,2,32,128]{3,2,1,0:T(8,128)(2,1)}, bf16[16,2,32,128]{3,2,1,0:T(8,128)(2,1)S(1)}, u32[]{:S(2)}, u32[]{:S(2)}) collective-permute-start(bf16[16,2,32,128]{3,2,1,0:T(8,128)(2,1)} %get-tuple-element.41), channel_id=1, source_target_pairs={{0,2},{2,0},{4,6},{6,4},{8,10},{10,8},{12,14},{14,12},{1,3},{3,1},... | collective-permute-start | bytes 786440 | tf_op jit(solution)/shard_map/ppermute | solution.py:383
  30.8 66.4 %copy-start.11 = (bf16[8,2,32,128]{3,2,1,0:T(8,128)(2,1)}, bf16[8,2,32,128]{3,2,1,0:T(8,128)(2,1)S(1)}, u32[]{:S(2)}) copy-start(bf16[8,2,32,128]{3,2,1,0:T(8,128)(2,1)S(1)} %collective-permute-done.17.refs_3_) | copy-start | bytes 393220
  30.8 15.6 %collective-permute-start.9 = (bf16[16,2,32,128]{3,2,1,0:T(8,128)(2,1)}, bf16[16,2,32,128]{3,2,1,0:T(8,128)(2,1)S(1)}, u32[]{:S(2)}, u32[]{:S(2)}) collective-permute-start(bf16[16,2,32,128]{3,2,1,0:T(8,128)(2,1)} %get-tuple-element.42), channel_id=1, source_target_pairs={{0,4},{2,6},{4,0},{6,2},{8,12},{10,14},{12,8},{14,10},{1,5},{3,7},... | collective-permute-start | bytes 786440 | tf_op jit(solution)/shard_map/ppermute | solution.py:383
  32.1 65.1 %copy-start.12 = (bf16[8,2,32,128]{3,2,1,0:T(8,128)(2,1)}, bf16[8,2,32,128]{3,2,1,0:T(8,128)(2,1)S(1)}, u32[]{:S(2)}) copy-start(bf16[8,2,32,128]{3,2,1,0:T(8,128)(2,1)S(1)} %collective-permute-done.18.refs_4_) | copy-start | bytes 393220
  32.1 8.2 %collective-permute-start.20 = (bf16[8,2,32,128]{3,2,1,0:T(8,128)(2,1)S(1)}, bf16[8,2,32,128]{3,2,1,0:T(8,128)(2,1)S(1)}, u32[]{:S(2)}, u32[]{:S(2)}) collective-permute-start(bf16[8,2,32,128]{3,2,1,0:T(8,128)(2,1)S(1)} %copy-done.23), channel_id=1, source_target_pairs={{0,12},{2,14},{4,8},{6,10},{8,4},{10,6},{12,0},{14,2},{1,13},{3,15... | collective-permute-start | bytes 393224 | tf_op jit(solution)/shard_map/ppermute | solution.py:383
  33.8 63.3 %copy-start.13 = (bf16[8,2,32,128]{3,2,1,0:T(8,128)(2,1)}, bf16[8,2,32,128]{3,2,1,0:T(8,128)(2,1)S(1)}, u32[]{:S(2)}) copy-start(bf16[8,2,32,128]{3,2,1,0:T(8,128)(2,1)S(1)} %collective-permute-done.19.refs_5_) | copy-start | bytes 393220
  33.8 10.3 %collective-permute-start.21 = (bf16[8,2,32,128]{3,2,1,0:T(8,128)(2,1)S(1)}, bf16[8,2,32,128]{3,2,1,0:T(8,128)(2,1)S(1)}, u32[]{:S(2)}, u32[]{:S(2)}) collective-permute-start(bf16[8,2,32,128]{3,2,1,0:T(8,128)(2,1)S(1)} %copy-done.22), channel_id=1, source_target_pairs={{0,14},{2,12},{4,10},{6,8},{8,6},{10,4},{12,2},{14,0},{1,15},{3,13... | collective-permute-start | bytes 393224 | tf_op jit(solution)/shard_map/ppermute | solution.py:383
  40.3 56.8 %copy-start.14 = (bf16[8,2,32,128]{3,2,1,0:T(8,128)(2,1)}, bf16[8,2,32,128]{3,2,1,0:T(8,128)(2,1)S(1)}, u32[]{:S(2)}) copy-start(bf16[8,2,32,128]{3,2,1,0:T(8,128)(2,1)S(1)} %collective-permute-done.20.refs_6_) | copy-start | bytes 393220
  40.3 18.2 %collective-permute-start.10 = (bf16[16,2,32,128]{3,2,1,0:T(8,128)(2,1)}, bf16[16,2,32,128]{3,2,1,0:T(8,128)(2,1)S(1)}, u32[]{:S(2)}, u32[]{:S(2)}) collective-permute-start(bf16[16,2,32,128]{3,2,1,0:T(8,128)(2,1)} %get-tuple-element.43), channel_id=1, source_target_pairs={{0,6},{2,4},{4,2},{6,0},{8,14},{10,12},{12,10},{14,8},{1,7},{3,5},... | collective-permute-start | bytes 786440 | tf_op jit(solution)/shard_map/ppermute | solution.py:383
  44.1 53.1 %copy-start.15 = (bf16[8,2,32,128]{3,2,1,0:T(8,128)(2,1)}, bf16[8,2,32,128]{3,2,1,0:T(8,128)(2,1)S(1)}, u32[]{:S(2)}) copy-start(bf16[8,2,32,128]{3,2,1,0:T(8,128)(2,1)S(1)} %collective-permute-done.21.refs_7_) | copy-start | bytes 393220
  44.1 14.8 %collective-permute-start.11 = (bf16[16,2,32,128]{3,2,1,0:T(8,128)(2,1)}, bf16[16,2,32,128]{3,2,1,0:T(8,128)(2,1)S(1)}, u32[]{:S(2)}, u32[]{:S(2)}) collective-permute-start(bf16[16,2,32,128]{3,2,1,0:T(8,128)(2,1)} %get-tuple-element.44), channel_id=1, source_target_pairs={{0,8},{2,10},{4,12},{6,14},{8,0},{10,2},{12,4},{14,6},{1,9},{3,11}... | collective-permute-start | bytes 786440 | tf_op jit(solution)/shard_map/ppermute | solution.py:383
  44.1 58.4 %copy-start.2 = (bf16[16,2,32,128]{3,2,1,0:T(8,128)(2,1)}, bf16[16,2,32,128]{3,2,1,0:T(8,128)(2,1)S(1)}, u32[]{:S(2)}) copy-start(bf16[16,2,32,128]{3,2,1,0:T(8,128)(2,1)S(1)} %collective-permute-done.8.refs_1_) | copy-start | bytes 786436
  44.1 35.0 %collective-permute-start.12 = (bf16[16,2,32,128]{3,2,1,0:T(8,128)(2,1)}, bf16[16,2,32,128]{3,2,1,0:T(8,128)(2,1)S(1)}, u32[]{:S(2)}, u32[]{:S(2)}) collective-permute-start(bf16[16,2,32,128]{3,2,1,0:T(8,128)(2,1)} %get-tuple-element.45), channel_id=1, source_target_pairs={{0,10},{2,8},{4,14},{6,12},{8,2},{10,0},{12,6},{14,4},{1,11},{3,9}... | collective-permute-start | bytes 786440 | tf_op jit(solution)/shard_map/ppermute | solution.py:383
  46.4 56.1 %copy-start.3 = (bf16[16,2,32,128]{3,2,1,0:T(8,128)(2,1)}, bf16[16,2,32,128]{3,2,1,0:T(8,128)(2,1)S(1)}, u32[]{:S(2)}) copy-start(bf16[16,2,32,128]{3,2,1,0:T(8,128)(2,1)S(1)} %collective-permute-done.9.refs_2_) | copy-start | bytes 786436
  46.4 32.7 %collective-permute-start.13 = (bf16[16,2,32,128]{3,2,1,0:T(8,128)(2,1)}, bf16[16,2,32,128]{3,2,1,0:T(8,128)(2,1)S(1)}, u32[]{:S(2)}, u32[]{:S(2)}) collective-permute-start(bf16[16,2,32,128]{3,2,1,0:T(8,128)(2,1)} %get-tuple-element.46), channel_id=1, source_target_pairs={{0,12},{2,14},{4,8},{6,10},{8,4},{10,6},{12,0},{14,2},{1,13},{3,15... | collective-permute-start | bytes 786440 | tf_op jit(solution)/shard_map/ppermute | solution.py:383
  48.5 2.2 %copy-start.1 = (bf16[2,960,128]{2,1,0:T(8,128)(2,1)}, bf16[2,960,128]{2,1,0:T(8,128)(2,1)S(1)}, u32[]{:S(2)}) copy-start(bf16[2,960,128]{2,1,0:T(8,128)(2,1)S(1)} %collective-permute-done.refs_2_) | copy-start | bytes 1474564
  48.5 37.3 %collective-permute-start.14 = (bf16[16,2,32,128]{3,2,1,0:T(8,128)(2,1)}, bf16[16,2,32,128]{3,2,1,0:T(8,128)(2,1)S(1)}, u32[]{:S(2)}, u32[]{:S(2)}) collective-permute-start(bf16[16,2,32,128]{3,2,1,0:T(8,128)(2,1)} %get-tuple-element.47), channel_id=1, source_target_pairs={{0,14},{2,12},{4,10},{6,8},{8,6},{10,4},{12,2},{14,0},{1,15},{3,13... | collective-permute-start | bytes 786440 | tf_op jit(solution)/shard_map/ppermute | solution.py:383
  58.6 44.0 %copy-start.4 = (bf16[16,2,32,128]{3,2,1,0:T(8,128)(2,1)}, bf16[16,2,32,128]{3,2,1,0:T(8,128)(2,1)S(1)}, u32[]{:S(2)}) copy-start(bf16[16,2,32,128]{3,2,1,0:T(8,128)(2,1)S(1)} %collective-permute-done.10.refs_3_) | copy-start | bytes 786436
  58.6 34.8 %collective-permute-start.1 = (bf16[8,2,32,128]{3,2,1,0:T(8,128)(2,1)}, bf16[8,2,32,128]{3,2,1,0:T(8,128)(2,1)S(1)}, u32[]{:S(2)}, u32[]{:S(2)}) collective-permute-start(bf16[8,2,32,128]{3,2,1,0:T(8,128)(2,1)} %get-tuple-element.34), channel_id=1, source_target_pairs={{0,2},{2,0},{4,6},{6,4},{8,10},{10,8},{12,14},{14,12},{1,3},{3,1},... | collective-permute-start | bytes 393224 | tf_op jit(solution)/shard_map/ppermute | solution.py:383
  58.9 43.6 %copy-start.5 = (bf16[16,2,32,128]{3,2,1,0:T(8,128)(2,1)}, bf16[16,2,32,128]{3,2,1,0:T(8,128)(2,1)S(1)}, u32[]{:S(2)}) copy-start(bf16[16,2,32,128]{3,2,1,0:T(8,128)(2,1)S(1)} %collective-permute-done.11.refs_4_) | copy-start | bytes 786436
  58.9 35.8 %collective-permute-start.2 = (bf16[8,2,32,128]{3,2,1,0:T(8,128)(2,1)}, bf16[8,2,32,128]{3,2,1,0:T(8,128)(2,1)S(1)}, u32[]{:S(2)}, u32[]{:S(2)}) collective-permute-start(bf16[8,2,32,128]{3,2,1,0:T(8,128)(2,1)} %get-tuple-element.35), channel_id=1, source_target_pairs={{0,4},{2,6},{4,0},{6,2},{8,12},{10,14},{12,8},{14,10},{1,5},{3,7},... | collective-permute-start | bytes 393224 | tf_op jit(solution)/shard_map/ppermute | solution.py:383
  79.1 23.4 %copy-start.6 = (bf16[16,2,32,128]{3,2,1,0:T(8,128)(2,1)}, bf16[16,2,32,128]{3,2,1,0:T(8,128)(2,1)S(1)}, u32[]{:S(2)}) copy-start(bf16[16,2,32,128]{3,2,1,0:T(8,128)(2,1)S(1)} %collective-permute-done.12.refs_5_) | copy-start | bytes 786436
  79.1 32.4 %collective-permute-start.3 = (bf16[8,2,32,128]{3,2,1,0:T(8,128)(2,1)}, bf16[8,2,32,128]{3,2,1,0:T(8,128)(2,1)S(1)}, u32[]{:S(2)}, u32[]{:S(2)}) collective-permute-start(bf16[8,2,32,128]{3,2,1,0:T(8,128)(2,1)} %get-tuple-element.36), channel_id=1, source_target_pairs={{0,6},{2,4},{4,2},{6,0},{8,14},{10,12},{12,10},{14,8},{1,7},{3,5},... | collective-permute-start | bytes 393224 | tf_op jit(solution)/shard_map/ppermute | solution.py:383
  79.1 23.4 %copy-start.7 = (bf16[16,2,32,128]{3,2,1,0:T(8,128)(2,1)}, bf16[16,2,32,128]{3,2,1,0:T(8,128)(2,1)S(1)}, u32[]{:S(2)}) copy-start(bf16[16,2,32,128]{3,2,1,0:T(8,128)(2,1)S(1)} %collective-permute-done.13.refs_6_) | copy-start | bytes 786436
  79.1 32.4 %collective-permute-start.4 = (bf16[8,2,32,128]{3,2,1,0:T(8,128)(2,1)}, bf16[8,2,32,128]{3,2,1,0:T(8,128)(2,1)S(1)}, u32[]{:S(2)}, u32[]{:S(2)}) collective-permute-start(bf16[8,2,32,128]{3,2,1,0:T(8,128)(2,1)} %get-tuple-element.37), channel_id=1, source_target_pairs={{0,8},{2,10},{4,12},{6,14},{8,0},{10,2},{12,4},{14,6},{1,9},{3,11}... | collective-permute-start | bytes 393224 | tf_op jit(solution)/shard_map/ppermute | solution.py:383
  85.8 16.8 %copy-start.8 = (bf16[16,2,32,128]{3,2,1,0:T(8,128)(2,1)}, bf16[16,2,32,128]{3,2,1,0:T(8,128)(2,1)S(1)}, u32[]{:S(2)}) copy-start(bf16[16,2,32,128]{3,2,1,0:T(8,128)(2,1)S(1)} %collective-permute-done.14.refs_7_) | copy-start | bytes 786436
  85.8 25.8 %collective-permute-start.5 = (bf16[8,2,32,128]{3,2,1,0:T(8,128)(2,1)}, bf16[8,2,32,128]{3,2,1,0:T(8,128)(2,1)S(1)}, u32[]{:S(2)}, u32[]{:S(2)}) collective-permute-start(bf16[8,2,32,128]{3,2,1,0:T(8,128)(2,1)} %get-tuple-element.38), channel_id=1, source_target_pairs={{0,10},{2,8},{4,14},{6,12},{8,2},{10,0},{12,6},{14,4},{1,11},{3,9}... | collective-permute-start | bytes 393224 | tf_op jit(solution)/shard_map/ppermute | solution.py:383
  93.4 18.1 %copy-start.16 = (bf16[8,2,32,128]{3,2,1,0:T(8,128)(2,1)}, bf16[8,2,32,128]{3,2,1,0:T(8,128)(2,1)S(1)}, u32[]{:S(2)}) copy-start(bf16[8,2,32,128]{3,2,1,0:T(8,128)(2,1)S(1)} %collective-permute-done.1.refs_1_) | copy-start | bytes 393220
  93.4 18.2 %collective-permute-start.6 = (bf16[8,2,32,128]{3,2,1,0:T(8,128)(2,1)}, bf16[8,2,32,128]{3,2,1,0:T(8,128)(2,1)S(1)}, u32[]{:S(2)}, u32[]{:S(2)}) collective-permute-start(bf16[8,2,32,128]{3,2,1,0:T(8,128)(2,1)} %get-tuple-element.39), channel_id=1, source_target_pairs={{0,12},{2,14},{4,8},{6,10},{8,4},{10,6},{12,0},{14,2},{1,13},{3,15... | collective-permute-start | bytes 393224 | tf_op jit(solution)/shard_map/ppermute | solution.py:383
  94.7 16.8 %copy-start.17 = (bf16[8,2,32,128]{3,2,1,0:T(8,128)(2,1)}, bf16[8,2,32,128]{3,2,1,0:T(8,128)(2,1)S(1)}, u32[]{:S(2)}) copy-start(bf16[8,2,32,128]{3,2,1,0:T(8,128)(2,1)S(1)} %collective-permute-done.2.refs_2_) | copy-start | bytes 393220
  94.7 16.9 %collective-permute-start.7 = (bf16[8,2,32,128]{3,2,1,0:T(8,128)(2,1)}, bf16[8,2,32,128]{3,2,1,0:T(8,128)(2,1)}, u32[]{:S(2)}, u32[]{:S(2)}) collective-permute-start(bf16[8,2,32,128]{3,2,1,0:T(8,128)(2,1)} %get-tuple-element.40), channel_id=1, source_target_pairs={{0,14},{2,12},{4,10},{6,8},{8,6},{10,4},{12,2},{14,0},{1,15},{3,13... | collective-permute-start | bytes 393224 | tf_op jit(solution)/shard_map/ppermute | solution.py:383
  111.5 0.7 copy-start.18
  111.6 0.7 copy-start.19
  111.6 0.7 copy-start.20
  111.6 0.7 copy-start.21
  118.7 14.8 %collective-permute-start.22 = (f32[1088,128]{1,0:T(8,128)}, f32[1088,128]{1,0:T(8,128)S(1)}, u32[]{:S(2)}, u32[]{:S(2)}) collective-permute-start(f32[1088,128]{1,0:T(8,128)} %products.5.own), channel_id=1, source_target_pairs={{0,1},{1,0},{2,3},{3,2},{4,5},{5,4},{6,7},{7,6},{8,9},{9,8},{10,11... | collective-permute-start | bytes 1671176 | tf_op jit(solution)/shard_map/ppermute | solution.py:385
  133.5 0.8 copy-start

commit v2 on v1

--- a/solution.py
+++ b/solution.py
@@ -12,7 +12,7 @@
 FA = 64
 LANES = 128
 STEP = 8
-SHARES = (4, 8, 4)
+SHARES = (3, 4, 7, 2)
 F32 = jnp.float32
 BF16 = jnp.bfloat16
 ANY = pl.BlockSpec(memory_space=pl.ANY)
@@ -57,9 +57,9 @@
 
 
 def spectra_kernel(first, count, taps, stations, last, *refs):
-    samples, earlier, passed, prototype, first_hbm, twist_hbm, second_hbm, _ = refs[:8]
-    outs = refs[8 : 8 + stations]
-    refs = refs[8 + stations :]
+    samples, earlier, passed, prototype, first_hbm, twist_hbm, second_hbm = refs[:7]
+    outs = refs[7 : 7 + stations]
+    refs = refs[7 + stations :]
     tail = None
     if last:
         tail, refs = refs[0], refs[1:]
@@ -181,12 +181,12 @@
                 outs[offset][index, member] = spectra[row : row + share, lane : lane + LANES]
         return carry
 
-    lax.fori_loop(0, count // 4, transform, 0, unroll=2)
+    lax.fori_loop(0, count // 4, transform, 0, unroll=2 if count % 16 else 4)
     if last:
         tail_copy.wait()
 
 
-def spectra_of(first, count, samples, earlier, passed, prototype, after, stations, last):
+def spectra_of(first, count, samples, earlier, passed, prototype, stations, last):
     taps, channels = prototype.shape
     length = channels // FA
     share = 4 * length // stations
@@ -199,7 +199,7 @@
     return pl.pallas_call(
         functools.partial(spectra_kernel, first, count, taps, stations, last),
         out_shape=out_shape,
-        in_specs=[ANY] * 8,
+        in_specs=[ANY] * 7,
         out_specs=[VMEM] * stations + [ANY] * last,
         scratch_shapes=[
             pltpu.VMEM((2, rows, LANES), BF16),
@@ -216,7 +216,8 @@
         cost_estimate=pl.CostEstimate(
             flops=count * 8 * 10**6, bytes_accessed=count * 65536, transcendentals=0
         ),
-    )(samples, earlier, passed, prototype, *tables, after)
+        compiler_params=pltpu.CompilerParams(vmem_limit_bytes=(58 if last else 20) * 2**20),
+    )(samples, earlier, passed, prototype, *tables)
 
 
 def pair_rows(inputs):
@@ -299,6 +300,7 @@
         cost_estimate=pl.CostEstimate(
             flops=steps * 4 * 10**6, bytes_accessed=steps * 65536, transcendentals=0
         ),
+        compiler_params=pltpu.CompilerParams(vmem_limit_bytes=12 * 2**20),
         name="products",
     )(*arrays)
 
@@ -360,20 +362,19 @@
     whole = sum(SHARES)
     first = spectra_here
     chunks = []
-    passed, after = earlier, earlier
+    passed = earlier
     for chunk, share in enumerate(SHARES):
         count = spectra_here * share // whole
         first -= count
         history = earlier if first else passed
         blocks = list(
             spectra_of(
-                first, count, stream, earlier, history, prototype, after, stations, chunk == 0
+                first, count, stream, earlier, history, prototype, stations, chunk == 0
             )
         )
         if chunk == 0:
             route = [(i, i + 1) for i in range(cores - 1)]
             passed = lax.ppermute(blocks.pop(), "chan", route)
-        after = blocks[0]
         chunks.append(blocks)
     if 2 * length // stations == 16:
         sums = None
@@ -389,6 +390,7 @@
             out_shape=jax.ShapeDtypeStruct((2, owned, 4 * stations * stations), F32),
             in_specs=[VMEM, VMEM],
             out_specs=VMEM,
+            compiler_params=pltpu.CompilerParams(vmem_limit_bytes=12 * 2**20),
             name="visibility",
         )(sums, other)
     joined = [jnp.concatenate([blocks[d] for blocks in chunks]) for d in range(stations)]

time: 138 us -> 126 us (0.913)
  Pallas kernels: 52.9 us -> 41.1 us
  starting transfers between devices: 52.4 us -> 59.4 us
  waiting for transfers between devices: 29.7 us -> 24.3 us
  local copies, waits for them, and re-layouts: 1.59 us -> 0.04 us
    ppermute x21 -> x28, starting transfers between devices: 38.2 us -> 54.6 us  [shards(): blocks[offset] = lax.ppermute(blocks[offset], 'stn', route)]
    ppermute x1, starting transfers between devices: 13 us -> 3.47 us  [shards(): other = lax.ppermute(sums, 'chan', [(i, i ^ 1) for i in range(cores)])]
    pallas_call x3 -> x4, Pallas kernels: 20.7 us -> 13 us  [products_of(): pl.pallas_call(functools.partial(products_kernel, stations, carried, fold...]
    ppermute x21 -> x28, waiting for transfers between devices: 27.9 us -> 22.7 us  [shards(): blocks[offset] = lax.ppermute(blocks[offset], 'stn', route)]
    pallas_call x3 -> x4, Pallas kernels: 29.6 us -> 26.7 us  [spectra_of(): pl.pallas_call(functools.partial(spectra_kernel, first, count, taps, stat...]
    unnamed x48 -> x16, local copies, waits for them, and re-layouts: 1.59 us -> 0.04 us
  transfers between devices with their start and end apart: 23 -> 30, of which waited for: 4 -> 5; matrix products, arithmetic and copies ran while one was open for 0% -> 0% of each run, Pallas kernels for 26% -> 25%
where the time goes in v2:
time: 126 us; the launch traced here: 125 us
  starting transfers between devices  59.4 us (47%)
  Pallas kernels  41.1 us (33%)
  waiting for transfers between devices  24.3 us (19%)
    ppermute x28, starting transfers between devices, shards(): blocks[offset] = lax.ppermute(blocks[offset], 'stn', route)  54.6 us
    pallas_call x4, Pallas kernels, spectra_of(): pl.pallas_call(functools.partial(spectra_kernel, first, count, taps, stat...  26.7 us
    ppermute x28, waiting for transfers between devices, shards(): blocks[offset] = lax.ppermute(blocks[offset], 'stn', route)  22.7 us
    pallas_call x4, Pallas kernels, products_of(): pl.pallas_call(functools.partial(products_kernel, stations, carried, fold...  13 us
    ppermute x1, starting transfers between devices, shards(): other = lax.ppermute(sums, 'chan', [(i, i ^ 1) for i in range(cores)])  3.47 us
  transfers between devices with their start and end apart: 30, of which 5 were waited for; matrix products, arithmetic and copies ran while one was open for 0% of the time, Pallas kernels for 25%

profile of v2, /device:TPU:1, one launch (start us, length us, event | category | flops | bytes accessed | tf_op | source)
XLA Modules:
  0.0 125.0 jit_solution(2578062910914606999)
XLA Ops:
  0.0 0.0 copy-start.3
  0.0 0.0 copy-start.4
  0.0 0.0 copy-start.5
  0.0 6.6 %shard_map.145 = (bf16[6,2,32,128]{3,2,1,0:T(8,128)(2,1)}, bf16[6,2,32,128]{3,2,1,0:T(8,128)(2,1)}, bf16[6,2,32,128]{3,2,1,0:T(8,128)(2,1)}, bf16[6,2,32,128]{3,...) custom-call(bf16[2,8192,128]{2,1,0:T(8,128)(2,1)} %bitcast.10, ...), custom_call_target="tpu_custom_call" | custom-call | flops 192000000 | bytes 1572864 | tf_op jit(solution)/shard_map/pallas_call | solution.py:199
  6.6 2.1 %collective-permute-start.22 = (bf16[6,2,32,128]{3,2,1,0:T(8,128)(2,1)}, bf16[6,2,32,128]{3,2,1,0:T(8,128)(2,1)S(1)}, u32[]{:S(2)}, u32[]{:S(2)}) collective-permute-start(bf16[6,2,32,128]{3,2,1,0:T(8,128)(2,1)} %get-tuple-element.64), channel_id=1, source_target_pairs={{0,2},{2,0},{4,6},{6,4},{8,10},{10,8},{12,14},{14,12},{1,3},{3,1},... | collective-permute-start | bytes 294920 | tf_op jit(solution)/shard_map/ppermute | solution.py:384
  8.7 1.3 %collective-permute-start.23 = (bf16[6,2,32,128]{3,2,1,0:T(8,128)(2,1)}, bf16[6,2,32,128]{3,2,1,0:T(8,128)(2,1)S(1)}, u32[]{:S(2)}, u32[]{:S(2)}) collective-permute-start(bf16[6,2,32,128]{3,2,1,0:T(8,128)(2,1)} %get-tuple-element.65), channel_id=1, source_target_pairs={{0,4},{2,6},{4,0},{6,2},{8,12},{10,14},{12,8},{14,10},{1,5},{3,7},... | collective-permute-start | bytes 294920 | tf_op jit(solution)/shard_map/ppermute | solution.py:384
  10.0 2.4 %collective-permute-start.25 = (bf16[6,2,32,128]{3,2,1,0:T(8,128)(2,1)}, bf16[6,2,32,128]{3,2,1,0:T(8,128)(2,1)S(1)}, u32[]{:S(2)}, u32[]{:S(2)}) collective-permute-start(bf16[6,2,32,128]{3,2,1,0:T(8,128)(2,1)} %get-tuple-element.67), channel_id=1, source_target_pairs={{0,8},{2,10},{4,12},{6,14},{8,0},{10,2},{12,4},{14,6},{1,9},{3,11}... | collective-permute-start | bytes 294920 | tf_op jit(solution)/shard_map/ppermute | solution.py:384
  12.5 1.3 %collective-permute-start = (bf16[2,960,128]{2,1,0:T(8,128)(2,1)}, bf16[2,960,128]{2,1,0:T(8,128)(2,1)S(1)}, u32[]{:S(2)}, u32[]{:S(2)}) collective-permute-start(bf16[2,960,128]{2,1,0:T(8,128)(2,1)} %get-tuple-element.38), channel_id=1, source_target_pairs={{0,1},{2,3},{4,5},{6,7},{8,9},{10,11},{12,13},{14,15},{16,17},{18,... | collective-permute-start | bytes 1474568 | tf_op jit(solution)/shard_map/ppermute | solution.py:377
  13.8 1.1 collective-permute-start.26
  14.8 0.0 collective-permute-done.23.refs_2_
  14.8 3.3 %collective-permute-start.27 = (bf16[6,2,32,128]{3,2,1,0:T(8,128)(2,1)}, bf16[6,2,32,128]{3,2,1,0:T(8,128)(2,1)S(1)}, u32[]{:S(2)}, u32[]{:S(2)}) collective-permute-start(bf16[6,2,32,128]{3,2,1,0:T(8,128)(2,1)} %get-tuple-element.69), channel_id=1, source_target_pairs={{0,12},{2,14},{4,8},{6,10},{8,4},{10,6},{12,0},{14,2},{1,13},{3,15... | collective-permute-start | bytes 294920 | tf_op jit(solution)/shard_map/ppermute | solution.py:384
  18.2 6.1 %shard_map.148 = (bf16[8,2,32,128]{3,2,1,0:T(8,128)(2,1)S(1)}, bf16[8,2,32,128]{3,2,1,0:T(8,128)(2,1)S(1)}, bf16[8,2,32,128]{3,2,1,0:T(8,128)(2,1)S(1)}, bf16[8,...) custom-call(bf16[2,8192,128]{2,1,0:T(8,128)(2,1)S(1)} %bitcast.11, ...), custom_call_target="tpu_custom_call" | custom-call | flops 256000000 | bytes 2097152 | tf_op jit(solution)/shard_map/pallas_call | solution.py:199
  24.3 0.0 collective-permute-done.24.refs_3_
  24.4 0.3 collective-permute-start.15
  24.6 0.0 collective-permute-done.25.refs_4_
  24.7 1.0 collective-permute-start.28
  25.6 0.4 collective-permute-done.26.refs_5_
  26.1 0.0 collective-permute-start.16
  26.1 2.4 %collective-permute-start.17 = (bf16[8,2,32,128]{3,2,1,0:T(8,128)(2,1)S(1)}, bf16[8,2,32,128]{3,2,1,0:T(8,128)(2,1)S(1)}, u32[]{:S(2)}, u32[]{:S(2)}) collective-permute-start(bf16[8,2,32,128]{3,2,1,0:T(8,128)(2,1)S(1)} %get-tuple-element.58), channel_id=1, source_target_pairs={{0,6},{2,4},{4,2},{6,0},{8,14},{10,12},{12,10},{14,8},{1,7},{3,5},... | collective-permute-start | bytes 393224 | tf_op jit(solution)/shard_map/ppermute | solution.py:384
  28.4 2.5 %collective-permute-done.28.refs_7_ = bf16[6,2,32,128]{3,2,1,0:T(8,128)(2,1)S(1)} collective-permute-done((bf16[6,2,32,128]{3,2,1,0:T(8,128)(2,1)S(1)}, bf16[6,2,32,128]{3,2,1,0:T(8,128)(2,1)S(1)}, u32[]{:S(2)}, u32[]{:S(2)}) %collective-permute-start.28) | collective-permute-done | bytes 98336 | tf_op jit(solution)/shard_map/ppermute | solution.py:384
  30.9 1.3 %collective-permute-start.18 = (bf16[8,2,32,128]{3,2,1,0:T(8,128)(2,1)S(1)}, bf16[8,2,32,128]{3,2,1,0:T(8,128)(2,1)S(1)}, u32[]{:S(2)}, u32[]{:S(2)}) collective-permute-start(bf16[8,2,32,128]{3,2,1,0:T(8,128)(2,1)S(1)} %get-tuple-element.59), channel_id=1, source_target_pairs={{0,8},{2,10},{4,12},{6,14},{8,0},{10,2},{12,4},{14,6},{1,9},{3,11}... | collective-permute-start | bytes 393224 | tf_op jit(solution)/shard_map/ppermute | solution.py:384
  32.2 2.1 %collective-permute-start.19 = (bf16[8,2,32,128]{3,2,1,0:T(8,128)(2,1)S(1)}, bf16[8,2,32,128]{3,2,1,0:T(8,128)(2,1)S(1)}, u32[]{:S(2)}, u32[]{:S(2)}) collective-permute-start(bf16[8,2,32,128]{3,2,1,0:T(8,128)(2,1)S(1)} %get-tuple-element.60), channel_id=1, source_target_pairs={{0,10},{2,8},{4,14},{6,12},{8,2},{10,0},{12,6},{14,4},{1,11},{3,9}... | collective-permute-start | bytes 393224 | tf_op jit(solution)/shard_map/ppermute | solution.py:384
  34.3 10.6 %shard_map.147 = (bf16[14,2,32,128]{3,2,1,0:T(8,128)(2,1)S(1)}, bf16[14,2,32,128]{3,2,1,0:T(8,128)(2,1)S(1)}, bf16[14,2,32,128]{3,2,1,0:T(8,128)(2,1)S(1)}, bf16...) custom-call(bf16[2,8192,128]{2,1,0:T(8,128)(2,1)S(1)} %bitcast.12, ...), custom_call_target="tpu_custom_call" | custom-call | flops 448000000 | bytes 3670016 | tf_op jit(solution)/shard_map/pallas_call | solution.py:199
  44.9 0.1 collective-permute-start.10
  45.0 0.4 collective-permute-start.11
  45.4 3.0 %collective-permute-start.20 = (bf16[8,2,32,128]{3,2,1,0:T(8,128)(2,1)S(1)}, bf16[8,2,32,128]{3,2,1,0:T(8,128)(2,1)S(1)}, u32[]{:S(2)}, u32[]{:S(2)}) collective-permute-start(bf16[8,2,32,128]{3,2,1,0:T(8,128)(2,1)S(1)} %get-tuple-element.61), channel_id=1, source_target_pairs={{0,12},{2,14},{4,8},{6,10},{8,4},{10,6},{12,0},{14,2},{1,13},{3,15... | collective-permute-start | bytes 393224 | tf_op jit(solution)/shard_map/ppermute | solution.py:384
  48.4 1.1 collective-permute-start.21
  49.5 7.1 %collective-permute-done.20.refs_6_ = bf16[8,2,32,128]{3,2,1,0:T(8,128)(2,1)S(1)} collective-permute-done((bf16[8,2,32,128]{3,2,1,0:T(8,128)(2,1)S(1)}, bf16[8,2,32,128]{3,2,1,0:T(8,128)(2,1)S(1)}, u32[]{:S(2)}, u32[]{:S(2)}) %collective-permute-start.20) | collective-permute-done | bytes 131104 | tf_op jit(solution)/shard_map/ppermute | solution.py:384
  56.6 9.9 %collective-permute-start.12 = (bf16[14,2,32,128]{3,2,1,0:T(8,128)(2,1)S(1)}, bf16[14,2,32,128]{3,2,1,0:T(8,128)(2,1)S(1)}, u32[]{:S(2)}, u32[]{:S(2)}) collective-permute-start(bf16[14,2,32,128]{3,2,1,0:T(8,128)(2,1)S(1)} %get-tuple-element.52), channel_id=1, source_target_pairs={{0,10},{2,8},{4,14},{6,12},{8,2},{10,0},{12,6},{14,4},{1,11},{3,9}... | collective-permute-start | bytes 688136 | tf_op jit(solution)/shard_map/ppermute | solution.py:384
  66.5 0.5 collective-permute-start.13
  67.0 4.2 %collective-permute-start.14 = (bf16[14,2,32,128]{3,2,1,0:T(8,128)(2,1)S(1)}, bf16[14,2,32,128]{3,2,1,0:T(8,128)(2,1)S(1)}, u32[]{:S(2)}, u32[]{:S(2)}) collective-permute-start(bf16[14,2,32,128]{3,2,1,0:T(8,128)(2,1)S(1)} %get-tuple-element.54), channel_id=1, source_target_pairs={{0,14},{2,12},{4,10},{6,8},{8,6},{10,4},{12,2},{14,0},{1,15},{3,13... | collective-permute-start | bytes 688136 | tf_op jit(solution)/shard_map/ppermute | solution.py:384
  71.2 0.2 collective-permute-start.9
  71.4 3.4 %shard_map.146 = (bf16[4,2,32,128]{3,2,1,0:T(8,128)(2,1)S(1)}, bf16[4,2,32,128]{3,2,1,0:T(8,128)(2,1)S(1)}, bf16[4,2,32,128]{3,2,1,0:T(8,128)(2,1)S(1)}, bf16[4,...) custom-call(bf16[2,8192,128]{2,1,0:T(8,128)(2,1)S(1)} %bitcast.13, ...), custom_call_target="tpu_custom_call" | custom-call | flops 128000000 | bytes 1048576 | tf_op jit(solution)/shard_map/pallas_call | solution.py:199
  74.8 12.6 %collective-permute-done.12.refs_5_ = bf16[14,2,32,128]{3,2,1,0:T(8,128)(2,1)S(1)} collective-permute-done((bf16[14,2,32,128]{3,2,1,0:T(8,128)(2,1)S(1)}, bf16[14,2,32,128]{3,2,1,0:T(8,128)(2,1)S(1)}, u32[]{:S(2)}, u32[]{:S(2)}) %collective-permute-start.12) | collective-permute-done | bytes 229408 | tf_op jit(solution)/shard_map/ppermute | solution.py:384
  87.4 1.7 %collective-permute-start.1 = (bf16[4,2,32,128]{3,2,1,0:T(8,128)(2,1)S(1)}, bf16[4,2,32,128]{3,2,1,0:T(8,128)(2,1)S(1)}, u32[]{:S(2)}, u32[]{:S(2)}) collective-permute-start(bf16[4,2,32,128]{3,2,1,0:T(8,128)(2,1)S(1)} %get-tuple-element.40), channel_id=1, source_target_pairs={{0,2},{2,0},{4,6},{6,4},{8,10},{10,8},{12,14},{14,12},{1,3},{3,1},... | collective-permute-start | bytes 196616 | tf_op jit(solution)/shard_map/ppermute | solution.py:384
  89.1 4.0 %collective-permute-start.2 = (bf16[4,2,32,128]{3,2,1,0:T(8,128)(2,1)S(1)}, bf16[4,2,32,128]{3,2,1,0:T(8,128)(2,1)S(1)}, u32[]{:S(2)}, u32[]{:S(2)}) collective-permute-start(bf16[4,2,32,128]{3,2,1,0:T(8,128)(2,1)S(1)} %get-tuple-element.41), channel_id=1, source_target_pairs={{0,4},{2,6},{4,0},{6,2},{8,12},{10,14},{12,8},{14,10},{1,5},{3,7},... | collective-permute-start | bytes 196616 | tf_op jit(solution)/shard_map/ppermute | solution.py:384
  93.1 5.8 %collective-permute-start.3 = (bf16[4,2,32,128]{3,2,1,0:T(8,128)(2,1)S(1)}, bf16[4,2,32,128]{3,2,1,0:T(8,128)(2,1)S(1)}, u32[]{:S(2)}, u32[]{:S(2)}) collective-permute-start(bf16[4,2,32,128]{3,2,1,0:T(8,128)(2,1)S(1)} %get-tuple-element.42), channel_id=1, source_target_pairs={{0,6},{2,4},{4,2},{6,0},{8,14},{10,12},{12,10},{14,8},{1,7},{3,5},... | collective-permute-start | bytes 196616 | tf_op jit(solution)/shard_map/ppermute | solution.py:384
  99.0 0.2 collective-permute-start.4
  99.2 1.7 %collective-permute-start.5 = (bf16[4,2,32,128]{3,2,1,0:T(8,128)(2,1)S(1)}, bf16[4,2,32,128]{3,2,1,0:T(8,128)(2,1)S(1)}, u32[]{:S(2)}, u32[]{:S(2)}) collective-permute-start(bf16[4,2,32,128]{3,2,1,0:T(8,128)(2,1)S(1)} %get-tuple-element.44), channel_id=1, source_target_pairs={{0,10},{2,8},{4,14},{6,12},{8,2},{10,0},{12,6},{14,4},{1,11},{3,9}... | collective-permute-start | bytes 196616 | tf_op jit(solution)/shard_map/ppermute | solution.py:384
  100.9 2.8 %collective-permute-start.6 = (bf16[4,2,32,128]{3,2,1,0:T(8,128)(2,1)S(1)}, bf16[4,2,32,128]{3,2,1,0:T(8,128)(2,1)S(1)}, u32[]{:S(2)}, u32[]{:S(2)}) collective-permute-start(bf16[4,2,32,128]{3,2,1,0:T(8,128)(2,1)S(1)} %get-tuple-element.45), channel_id=1, source_target_pairs={{0,12},{2,14},{4,8},{6,10},{8,4},{10,6},{12,0},{14,2},{1,13},{3,15... | collective-permute-start | bytes 196616 | tf_op jit(solution)/shard_map/ppermute | solution.py:384
  103.6 1.9 %collective-permute-start.7 = (bf16[4,2,32,128]{3,2,1,0:T(8,128)(2,1)S(1)}, bf16[4,2,32,128]{3,2,1,0:T(8,128)(2,1)S(1)}, u32[]{:S(2)}, u32[]{:S(2)}) collective-permute-start(bf16[4,2,32,128]{3,2,1,0:T(8,128)(2,1)S(1)} %get-tuple-element.46), channel_id=1, source_target_pairs={{0,14},{2,12},{4,10},{6,8},{8,6},{10,4},{12,2},{14,0},{1,15},{3,13... | collective-permute-start | bytes 196616 | tf_op jit(solution)/shard_map/ppermute | solution.py:384
  105.5 2.3 %products.4.refs_8_ = f32[2176,128]{1,0:T(8,128)S(1)} custom-call(bf16[6,2,32,128]{3,2,1,0:T(8,128)(2,1)S(1)} %copy-done.6, bf16[6,2,32,128]{3,2,1,0:T(8,128)(2,1)S(1)} %collective-permute-done.22.refs_1_, bf16[6,2,32,128]{3,2,1,0:T(8,128)(2,1)S(1)} %collective-permute-done.23.refs_2_, bf16[6,2,32,128]{3,2,1,0:T(8,128)(2,1)S(1)} %collective-permute-done.24.refs_3_, ...), custom_call_target="tpu_custom_call" | custom-call | flops 96000000 | bytes 1572864 | tf_op jit(solution)/shard_map/products/pallas_call | solution.py:295
  107.8 3.0 %products.5.refs_8_ = f32[2176,128]{1,0:T(8,128)S(1)} custom-call(bf16[8,2,32,128]{3,2,1,0:T(8,128)(2,1)S(1)} %get-tuple-element.55.refs_0_, bf16[8,2,32,128]{3,2,1,0:T(8,128)(2,1)S(1)} %collective-permute-done.15.refs_1_, bf16[8,2,32,128]{3,2,1,0:T(8,128)(2,1)S(1)} %collective-permute-done.16.refs_2_, ...), custom_call_target="tpu_custom_call" | custom-call | flops 128000000 | bytes 2097152 | tf_op jit(solution)/shard_map/products/pallas_call | solution.py:295
  110.9 5.3 %products.6.refs_8_ = f32[2176,128]{1,0:T(8,128)S(1)} custom-call(bf16[14,2,32,128]{3,2,1,0:T(8,128)(2,1)S(1)} %get-tuple-element.47.refs_0_, bf16[14,2,32,128]{3,2,1,0:T(8,128)(2,1)S(1)} %collective-permute-done.8.refs_1_, bf16[14,2,32,128]{3,2,1,0:T(8,128)(2,1)S(1)} %collective-permute-done.9.refs_2_, ...), custom_call_target="tpu_custom_call" | custom-call | flops 224000000 | bytes 3670016 | tf_op jit(solution)/shard_map/products/pallas_call | solution.py:295
  116.2 2.4 %products.7.own = f32[1088,128]{1,0:T(8,128)S(1)} custom-call(bf16[4,2,32,128]{3,2,1,0:T(8,128)(2,1)S(1)} %get-tuple-element.39.refs_0_, bf16[4,2,32,128]{3,2,1,0:T(8,128)(2,1)S(1)} %collective-permute-done.1.refs_1_, bf16[4,2,32,128]{3,2,1,0:T(8,128)(2,1)S(1)} %collective-permute-done.2.refs_2_, bf16[4,2,32,128]{3,2,1,0:T(8,128)(2,1)S(1)} %collective-permute-done.3.refs_3_, ...), custom_call_target="tpu_custom_call" | custom-call | flops 64000000 | bytes 1048576 | tf_op jit(solution)/shard_map/products/pallas_call | solution.py:295
  118.6 3.5 %collective-permute-start.29 = (f32[1088,128]{1,0:T(8,128)S(1)}, f32[1088,128]{1,0:T(8,128)S(1)}, u32[]{:S(2)}, u32[]{:S(2)}) collective-permute-start(f32[1088,128]{1,0:T(8,128)S(1)} %products.7.own), channel_id=1, source_target_pairs={{0,1},{1,0},{2,3},{3,2},{4,5},{5,4},{6,7},{7,6},{8,9},{9,8},{10,11... | collective-permute-start | bytes 1671176 | tf_op jit(solution)/shard_map/ppermute | solution.py:386
  122.1 1.6 %collective-permute-done.29.other = f32[1088,128]{1,0:T(8,128)S(1)} collective-permute-done((f32[1088,128]{1,0:T(8,128)S(1)}, f32[1088,128]{1,0:T(8,128)S(1)}, u32[]{:S(2)}, u32[]{:S(2)}) %collective-permute-start.29) | collective-permute-done | bytes 557088 | tf_op jit(solution)/shard_map/ppermute | solution.py:386
  123.7 1.3 %visibility.1 = f32[2,256,256]{2,1,0:T(8,128)} custom-call(f32[1088,128]{1,0:T(8,128)S(1)} %products.7.own, f32[1088,128]{1,0:T(8,128)S(1)} %collective-permute-done.29.other), custom_call_target="tpu_custom_call" | custom-call | tf_op jit(solution)/shard_map/visibility/pallas_call | solution.py:388
  (37 shorter events, 0.1 us)
Async XLA Ops:
  0.0 18.2 %copy-start = (bf16[2,2,524288]{2,1,0:T(2,128)(2,1)S(1)}, bf16[2,2,524288]{2,1,0:T(2,128)(2,1)}, u32[]{:S(2)}) copy-start(bf16[2,2,524288]{2,1,0:T(2,128)(2,1)} %param.15) | copy-start | bytes 12582916
  0.0 18.2 %copy-start.1 = (bf16[2,2,61440]{2,1,0:T(2,128)(2,1)S(1)}, bf16[2,2,61440]{2,1,0:T(2,128)(2,1)}, u32[]{:S(2)}) copy-start(bf16[2,2,61440]{2,1,0:T(2,128)(2,1)} %param.16) | copy-start | bytes 1474564
  0.0 18.2 %copy-start.2 = (f32[16,4096]{1,0:T(8,128)S(1)}, f32[16,4096]{1,0:T(8,128)}, u32[]{:S(2)}) copy-start(f32[16,4096]{1,0:T(8,128)} %refs_3_.7) | copy-start | bytes 786436
  0.0 18.2 %copy-start.3 = (bf16[256,256]{1,0:T(8,128)(2,1)S(1)}, bf16[256,256]{1,0:T(8,128)(2,1)}, u32[]{:S(2)}) copy-start(bf16[256,256]{1,0:T(8,128)(2,1)} %constant.6.clone.refs_4_) | copy-start | bytes 393220
  0.0 18.2 %copy-start.4 = (bf16[256,256]{1,0:T(8,128)(2,1)S(1)}, bf16[256,256]{1,0:T(8,128)(2,1)}, u32[]{:S(2)}) copy-start(bf16[256,256]{1,0:T(8,128)(2,1)} %constant.8.clone.refs_6_) | copy-start | bytes 393220
  0.0 18.2 %copy-start.5 = (f32[2,64,128]{2,1,0:T(8,128)S(1)}, f32[2,64,128]{2,1,0:T(8,128)}, u32[]{:S(2)}) copy-start(f32[2,64,128]{2,1,0:T(8,128)} %constant.7.clone.refs_5_) | copy-start | bytes 196612
  6.6 7.1 %collective-permute-start.22 = (bf16[6,2,32,128]{3,2,1,0:T(8,128)(2,1)}, bf16[6,2,32,128]{3,2,1,0:T(8,128)(2,1)S(1)}, u32[]{:S(2)}, u32[]{:S(2)}) collective-permute-start(bf16[6,2,32,128]{3,2,1,0:T(8,128)(2,1)} %get-tuple-element.64), channel_id=1, source_target_pairs={{0,2},{2,0},{4,6},{6,4},{8,10},{10,8},{12,14},{14,12},{1,3},{3,1},... | collective-permute-start | bytes 294920 | tf_op jit(solution)/shard_map/ppermute | solution.py:384
  8.7 6.1 %collective-permute-start.23 = (bf16[6,2,32,128]{3,2,1,0:T(8,128)(2,1)}, bf16[6,2,32,128]{3,2,1,0:T(8,128)(2,1)S(1)}, u32[]{:S(2)}, u32[]{:S(2)}) collective-permute-start(bf16[6,2,32,128]{3,2,1,0:T(8,128)(2,1)} %get-tuple-element.65), channel_id=1, source_target_pairs={{0,4},{2,6},{4,0},{6,2},{8,12},{10,14},{12,8},{14,10},{1,5},{3,7},... | collective-permute-start | bytes 294920 | tf_op jit(solution)/shard_map/ppermute | solution.py:384
  10.0 14.3 %collective-permute-start.24 = (bf16[6,2,32,128]{3,2,1,0:T(8,128)(2,1)}, bf16[6,2,32,128]{3,2,1,0:T(8,128)(2,1)S(1)}, u32[]{:S(2)}, u32[]{:S(2)}) collective-permute-start(bf16[6,2,32,128]{3,2,1,0:T(8,128)(2,1)} %get-tuple-element.66), channel_id=1, source_target_pairs={{0,6},{2,4},{4,2},{6,0},{8,14},{10,12},{12,10},{14,8},{1,7},{3,5},... | collective-permute-start | bytes 294920 | tf_op jit(solution)/shard_map/ppermute | solution.py:384
  10.0 14.6 %collective-permute-start.25 = (bf16[6,2,32,128]{3,2,1,0:T(8,128)(2,1)}, bf16[6,2,32,128]{3,2,1,0:T(8,128)(2,1)S(1)}, u32[]{:S(2)}, u32[]{:S(2)}) collective-permute-start(bf16[6,2,32,128]{3,2,1,0:T(8,128)(2,1)} %get-tuple-element.67), channel_id=1, source_target_pairs={{0,8},{2,10},{4,12},{6,14},{8,0},{10,2},{12,4},{14,6},{1,9},{3,11}... | collective-permute-start | bytes 294920 | tf_op jit(solution)/shard_map/ppermute | solution.py:384
  12.5 58.8 %collective-permute-start = (bf16[2,960,128]{2,1,0:T(8,128)(2,1)}, bf16[2,960,128]{2,1,0:T(8,128)(2,1)S(1)}, u32[]{:S(2)}, u32[]{:S(2)}) collective-permute-start(bf16[2,960,128]{2,1,0:T(8,128)(2,1)} %get-tuple-element.38), channel_id=1, source_target_pairs={{0,1},{2,3},{4,5},{6,7},{8,9},{10,11},{12,13},{14,15},{16,17},{18,... | collective-permute-start | bytes 1474568 | tf_op jit(solution)/shard_map/ppermute | solution.py:377
  13.8 12.3 %collective-permute-start.26 = (bf16[6,2,32,128]{3,2,1,0:T(8,128)(2,1)}, bf16[6,2,32,128]{3,2,1,0:T(8,128)(2,1)S(1)}, u32[]{:S(2)}, u32[]{:S(2)}) collective-permute-start(bf16[6,2,32,128]{3,2,1,0:T(8,128)(2,1)} %get-tuple-element.68), channel_id=1, source_target_pairs={{0,10},{2,8},{4,14},{6,12},{8,2},{10,0},{12,6},{14,4},{1,11},{3,9}... | collective-permute-start | bytes 294920 | tf_op jit(solution)/shard_map/ppermute | solution.py:384
  14.8 9.8 %copy-start.7 = (bf16[6,2,32,128]{3,2,1,0:T(8,128)(2,1)S(1)}, bf16[6,2,32,128]{3,2,1,0:T(8,128)(2,1)}, u32[]{:S(2)}) copy-start(bf16[6,2,32,128]{3,2,1,0:T(8,128)(2,1)} %get-tuple-element.70) | copy-start | bytes 294916
  14.8 11.2 %collective-permute-start.27 = (bf16[6,2,32,128]{3,2,1,0:T(8,128)(2,1)}, bf16[6,2,32,128]{3,2,1,0:T(8,128)(2,1)S(1)}, u32[]{:S(2)}, u32[]{:S(2)}) collective-permute-start(bf16[6,2,32,128]{3,2,1,0:T(8,128)(2,1)} %get-tuple-element.69), channel_id=1, source_target_pairs={{0,12},{2,14},{4,8},{6,10},{8,4},{10,6},{12,0},{14,2},{1,13},{3,15... | collective-permute-start | bytes 294920 | tf_op jit(solution)/shard_map/ppermute | solution.py:384
  24.4 7.8 %collective-permute-start.15 = (bf16[8,2,32,128]{3,2,1,0:T(8,128)(2,1)S(1)}, bf16[8,2,32,128]{3,2,1,0:T(8,128)(2,1)S(1)}, u32[]{:S(2)}, u32[]{:S(2)}) collective-permute-start(bf16[8,2,32,128]{3,2,1,0:T(8,128)(2,1)S(1)} %get-tuple-element.56), channel_id=1, source_target_pairs={{0,2},{2,0},{4,6},{6,4},{8,10},{10,8},{12,14},{14,12},{1,3},{3,1},... | collective-permute-start | bytes 393224 | tf_op jit(solution)/shard_map/ppermute | solution.py:384
  24.7 6.3 %collective-permute-start.28 = (bf16[6,2,32,128]{3,2,1,0:T(8,128)(2,1)S(1)}, bf16[6,2,32,128]{3,2,1,0:T(8,128)(2,1)S(1)}, u32[]{:S(2)}, u32[]{:S(2)}) collective-permute-start(bf16[6,2,32,128]{3,2,1,0:T(8,128)(2,1)S(1)} %copy-done.7), channel_id=1, source_target_pairs={{0,14},{2,12},{4,10},{6,8},{8,6},{10,4},{12,2},{14,0},{1,15},{3,13... | collective-permute-start | bytes 294920 | tf_op jit(solution)/shard_map/ppermute | solution.py:384
  26.1 18.8 %collective-permute-start.16 = (bf16[8,2,32,128]{3,2,1,0:T(8,128)(2,1)S(1)}, bf16[8,2,32,128]{3,2,1,0:T(8,128)(2,1)S(1)}, u32[]{:S(2)}, u32[]{:S(2)}) collective-permute-start(bf16[8,2,32,128]{3,2,1,0:T(8,128)(2,1)S(1)} %get-tuple-element.57), channel_id=1, source_target_pairs={{0,4},{2,6},{4,0},{6,2},{8,12},{10,14},{12,8},{14,10},{1,5},{3,7},... | collective-permute-start | bytes 393224 | tf_op jit(solution)/shard_map/ppermute | solution.py:384
  26.1 18.9 %collective-permute-start.17 = (bf16[8,2,32,128]{3,2,1,0:T(8,128)(2,1)S(1)}, bf16[8,2,32,128]{3,2,1,0:T(8,128)(2,1)S(1)}, u32[]{:S(2)}, u32[]{:S(2)}) collective-permute-start(bf16[8,2,32,128]{3,2,1,0:T(8,128)(2,1)S(1)} %get-tuple-element.58), channel_id=1, source_target_pairs={{0,6},{2,4},{4,2},{6,0},{8,14},{10,12},{12,10},{14,8},{1,7},{3,5},... | collective-permute-start | bytes 393224 | tf_op jit(solution)/shard_map/ppermute | solution.py:384
  30.9 14.5 %collective-permute-start.18 = (bf16[8,2,32,128]{3,2,1,0:T(8,128)(2,1)S(1)}, bf16[8,2,32,128]{3,2,1,0:T(8,128)(2,1)S(1)}, u32[]{:S(2)}, u32[]{:S(2)}) collective-permute-start(bf16[8,2,32,128]{3,2,1,0:T(8,128)(2,1)S(1)} %get-tuple-element.59), channel_id=1, source_target_pairs={{0,8},{2,10},{4,12},{6,14},{8,0},{10,2},{12,4},{14,6},{1,9},{3,11}... | collective-permute-start | bytes 393224 | tf_op jit(solution)/shard_map/ppermute | solution.py:384
  32.2 16.2 %collective-permute-start.19 = (bf16[8,2,32,128]{3,2,1,0:T(8,128)(2,1)S(1)}, bf16[8,2,32,128]{3,2,1,0:T(8,128)(2,1)S(1)}, u32[]{:S(2)}, u32[]{:S(2)}) collective-permute-start(bf16[8,2,32,128]{3,2,1,0:T(8,128)(2,1)S(1)} %get-tuple-element.60), channel_id=1, source_target_pairs={{0,10},{2,8},{4,14},{6,12},{8,2},{10,0},{12,6},{14,4},{1,11},{3,9}... | collective-permute-start | bytes 393224 | tf_op jit(solution)/shard_map/ppermute | solution.py:384
  44.9 22.1 %collective-permute-start.10 = (bf16[14,2,32,128]{3,2,1,0:T(8,128)(2,1)S(1)}, bf16[14,2,32,128]{3,2,1,0:T(8,128)(2,1)S(1)}, u32[]{:S(2)}, u32[]{:S(2)}) collective-permute-start(bf16[14,2,32,128]{3,2,1,0:T(8,128)(2,1)S(1)} %get-tuple-element.50), channel_id=1, source_target_pairs={{0,6},{2,4},{4,2},{6,0},{8,14},{10,12},{12,10},{14,8},{1,7},{3,5},... | collective-permute-start | bytes 688136 | tf_op jit(solution)/shard_map/ppermute | solution.py:384
  45.0 26.2 %collective-permute-start.11 = (bf16[14,2,32,128]{3,2,1,0:T(8,128)(2,1)S(1)}, bf16[14,2,32,128]{3,2,1,0:T(8,128)(2,1)S(1)}, u32[]{:S(2)}, u32[]{:S(2)}) collective-permute-start(bf16[14,2,32,128]{3,2,1,0:T(8,128)(2,1)S(1)} %get-tuple-element.51), channel_id=1, source_target_pairs={{0,8},{2,10},{4,12},{6,14},{8,0},{10,2},{12,4},{14,6},{1,9},{3,11}... | collective-permute-start | bytes 688136 | tf_op jit(solution)/shard_map/ppermute | solution.py:384
  45.4 11.2 %collective-permute-start.20 = (bf16[8,2,32,128]{3,2,1,0:T(8,128)(2,1)S(1)}, bf16[8,2,32,128]{3,2,1,0:T(8,128)(2,1)S(1)}, u32[]{:S(2)}, u32[]{:S(2)}) collective-permute-start(bf16[8,2,32,128]{3,2,1,0:T(8,128)(2,1)S(1)} %get-tuple-element.61), channel_id=1, source_target_pairs={{0,12},{2,14},{4,8},{6,10},{8,4},{10,6},{12,0},{14,2},{1,13},{3,15... | collective-permute-start | bytes 393224 | tf_op jit(solution)/shard_map/ppermute | solution.py:384
  48.4 18.1 %collective-permute-start.21 = (bf16[8,2,32,128]{3,2,1,0:T(8,128)(2,1)S(1)}, bf16[8,2,32,128]{3,2,1,0:T(8,128)(2,1)S(1)}, u32[]{:S(2)}, u32[]{:S(2)}) collective-permute-start(bf16[8,2,32,128]{3,2,1,0:T(8,128)(2,1)S(1)} %get-tuple-element.62), channel_id=1, source_target_pairs={{0,14},{2,12},{4,10},{6,8},{8,6},{10,4},{12,2},{14,0},{1,15},{3,13... | collective-permute-start | bytes 393224 | tf_op jit(solution)/shard_map/ppermute | solution.py:384
  56.6 30.8 %collective-permute-start.12 = (bf16[14,2,32,128]{3,2,1,0:T(8,128)(2,1)S(1)}, bf16[14,2,32,128]{3,2,1,0:T(8,128)(2,1)S(1)}, u32[]{:S(2)}, u32[]{:S(2)}) collective-permute-start(bf16[14,2,32,128]{3,2,1,0:T(8,128)(2,1)S(1)} %get-tuple-element.52), channel_id=1, source_target_pairs={{0,10},{2,8},{4,14},{6,12},{8,2},{10,0},{12,6},{14,4},{1,11},{3,9}... | collective-permute-start | bytes 688136 | tf_op jit(solution)/shard_map/ppermute | solution.py:384
  66.5 22.6 %collective-permute-start.13 = (bf16[14,2,32,128]{3,2,1,0:T(8,128)(2,1)S(1)}, bf16[14,2,32,128]{3,2,1,0:T(8,128)(2,1)S(1)}, u32[]{:S(2)}, u32[]{:S(2)}) collective-permute-start(bf16[14,2,32,128]{3,2,1,0:T(8,128)(2,1)S(1)} %get-tuple-element.53), channel_id=1, source_target_pairs={{0,12},{2,14},{4,8},{6,10},{8,4},{10,6},{12,0},{14,2},{1,13},{3,15... | collective-permute-start | bytes 688136 | tf_op jit(solution)/shard_map/ppermute | solution.py:384
  67.0 26.1 %collective-permute-start.14 = (bf16[14,2,32,128]{3,2,1,0:T(8,128)(2,1)S(1)}, bf16[14,2,32,128]{3,2,1,0:T(8,128)(2,1)S(1)}, u32[]{:S(2)}, u32[]{:S(2)}) collective-permute-start(bf16[14,2,32,128]{3,2,1,0:T(8,128)(2,1)S(1)} %get-tuple-element.54), channel_id=1, source_target_pairs={{0,14},{2,12},{4,10},{6,8},{8,6},{10,4},{12,2},{14,0},{1,15},{3,13... | collective-permute-start | bytes 688136 | tf_op jit(solution)/shard_map/ppermute | solution.py:384
  71.2 27.7 %collective-permute-start.8 = (bf16[14,2,32,128]{3,2,1,0:T(8,128)(2,1)S(1)}, bf16[14,2,32,128]{3,2,1,0:T(8,128)(2,1)S(1)}, u32[]{:S(2)}, u32[]{:S(2)}) collective-permute-start(bf16[14,2,32,128]{3,2,1,0:T(8,128)(2,1)S(1)} %get-tuple-element.48), channel_id=1, source_target_pairs={{0,2},{2,0},{4,6},{6,4},{8,10},{10,8},{12,14},{14,12},{1,3},{3,1},... | collective-permute-start | bytes 688136 | tf_op jit(solution)/shard_map/ppermute | solution.py:384
  71.2 34.3 %copy-start.6 = (bf16[6,2,32,128]{3,2,1,0:T(8,128)(2,1)S(1)}, bf16[6,2,32,128]{3,2,1,0:T(8,128)(2,1)}, u32[]{:S(2)}) copy-start(bf16[6,2,32,128]{3,2,1,0:T(8,128)(2,1)} %get-tuple-element.63.refs_0_) | copy-start | bytes 294916
  71.2 27.9 %collective-permute-start.9 = (bf16[14,2,32,128]{3,2,1,0:T(8,128)(2,1)S(1)}, bf16[14,2,32,128]{3,2,1,0:T(8,128)(2,1)S(1)}, u32[]{:S(2)}, u32[]{:S(2)}) collective-permute-start(bf16[14,2,32,128]{3,2,1,0:T(8,128)(2,1)S(1)} %get-tuple-element.49), channel_id=1, source_target_pairs={{0,4},{2,6},{4,0},{6,2},{8,12},{10,14},{12,8},{14,10},{1,5},{3,7},... | collective-permute-start | bytes 688136 | tf_op jit(solution)/shard_map/ppermute | solution.py:384
  87.4 13.4 %collective-permute-start.1 = (bf16[4,2,32,128]{3,2,1,0:T(8,128)(2,1)S(1)}, bf16[4,2,32,128]{3,2,1,0:T(8,128)(2,1)S(1)}, u32[]{:S(2)}, u32[]{:S(2)}) collective-permute-start(bf16[4,2,32,128]{3,2,1,0:T(8,128)(2,1)S(1)} %get-tuple-element.40), channel_id=1, source_target_pairs={{0,2},{2,0},{4,6},{6,4},{8,10},{10,8},{12,14},{14,12},{1,3},{3,1},... | collective-permute-start | bytes 196616 | tf_op jit(solution)/shard_map/ppermute | solution.py:384
  89.1 14.5 %collective-permute-start.2 = (bf16[4,2,32,128]{3,2,1,0:T(8,128)(2,1)S(1)}, bf16[4,2,32,128]{3,2,1,0:T(8,128)(2,1)S(1)}, u32[]{:S(2)}, u32[]{:S(2)}) collective-permute-start(bf16[4,2,32,128]{3,2,1,0:T(8,128)(2,1)S(1)} %get-tuple-element.41), channel_id=1, source_target_pairs={{0,4},{2,6},{4,0},{6,2},{8,12},{10,14},{12,8},{14,10},{1,5},{3,7},... | collective-permute-start | bytes 196616 | tf_op jit(solution)/shard_map/ppermute | solution.py:384
  93.1 23.0 %collective-permute-start.3 = (bf16[4,2,32,128]{3,2,1,0:T(8,128)(2,1)S(1)}, bf16[4,2,32,128]{3,2,1,0:T(8,128)(2,1)S(1)}, u32[]{:S(2)}, u32[]{:S(2)}) collective-permute-start(bf16[4,2,32,128]{3,2,1,0:T(8,128)(2,1)S(1)} %get-tuple-element.42), channel_id=1, source_target_pairs={{0,6},{2,4},{4,2},{6,0},{8,14},{10,12},{12,10},{14,8},{1,7},{3,5},... | collective-permute-start | bytes 196616 | tf_op jit(solution)/shard_map/ppermute | solution.py:384
  99.0 17.2 %collective-permute-start.4 = (bf16[4,2,32,128]{3,2,1,0:T(8,128)(2,1)S(1)}, bf16[4,2,32,128]{3,2,1,0:T(8,128)(2,1)S(1)}, u32[]{:S(2)}, u32[]{:S(2)}) collective-permute-start(bf16[4,2,32,128]{3,2,1,0:T(8,128)(2,1)S(1)} %get-tuple-element.43), channel_id=1, source_target_pairs={{0,8},{2,10},{4,12},{6,14},{8,0},{10,2},{12,4},{14,6},{1,9},{3,11}... | collective-permute-start | bytes 196616 | tf_op jit(solution)/shard_map/ppermute | solution.py:384
  99.2 17.0 %collective-permute-start.5 = (bf16[4,2,32,128]{3,2,1,0:T(8,128)(2,1)S(1)}, bf16[4,2,32,128]{3,2,1,0:T(8,128)(2,1)S(1)}, u32[]{:S(2)}, u32[]{:S(2)}) collective-permute-start(bf16[4,2,32,128]{3,2,1,0:T(8,128)(2,1)S(1)} %get-tuple-element.44), channel_id=1, source_target_pairs={{0,10},{2,8},{4,14},{6,12},{8,2},{10,0},{12,6},{14,4},{1,11},{3,9}... | collective-permute-start | bytes 196616 | tf_op jit(solution)/shard_map/ppermute | solution.py:384
  100.9 15.3 %collective-permute-start.6 = (bf16[4,2,32,128]{3,2,1,0:T(8,128)(2,1)S(1)}, bf16[4,2,32,128]{3,2,1,0:T(8,128)(2,1)S(1)}, u32[]{:S(2)}, u32[]{:S(2)}) collective-permute-start(bf16[4,2,32,128]{3,2,1,0:T(8,128)(2,1)S(1)} %get-tuple-element.45), channel_id=1, source_target_pairs={{0,12},{2,14},{4,8},{6,10},{8,4},{10,6},{12,0},{14,2},{1,13},{3,15... | collective-permute-start | bytes 196616 | tf_op jit(solution)/shard_map/ppermute | solution.py:384
  103.6 12.6 %collective-permute-start.7 = (bf16[4,2,32,128]{3,2,1,0:T(8,128)(2,1)S(1)}, bf16[4,2,32,128]{3,2,1,0:T(8,128)(2,1)S(1)}, u32[]{:S(2)}, u32[]{:S(2)}) collective-permute-start(bf16[4,2,32,128]{3,2,1,0:T(8,128)(2,1)S(1)} %get-tuple-element.46), channel_id=1, source_target_pairs={{0,14},{2,12},{4,10},{6,8},{8,6},{10,4},{12,2},{14,0},{1,15},{3,13... | collective-permute-start | bytes 196616 | tf_op jit(solution)/shard_map/ppermute | solution.py:384
  118.6 5.1 %collective-permute-start.29 = (f32[1088,128]{1,0:T(8,128)S(1)}, f32[1088,128]{1,0:T(8,128)S(1)}, u32[]{:S(2)}, u32[]{:S(2)}) collective-permute-start(f32[1088,128]{1,0:T(8,128)S(1)} %products.7.own), channel_id=1, source_target_pairs={{0,1},{1,0},{2,3},{3,2},{4,5},{5,4},{6,7},{7,6},{8,9},{9,8},{10,11... | collective-permute-start | bytes 1671176 | tf_op jit(solution)/shard_map/ppermute | solution.py:386

commit v3 on v2

--- a/solution.py
+++ b/solution.py
@@ -11,8 +11,9 @@
 
 FA = 64
 LANES = 128
+SUBLANES = 8
 STEP = 8
-SHARES = (3, 4, 7, 2)
+SHARES = (4, 5, 5, 2)
 F32 = jnp.float32
 BF16 = jnp.bfloat16
 ANY = pl.BlockSpec(memory_space=pl.ANY)
@@ -40,10 +41,11 @@
     return table.reshape(4 * FA, 4 * FA).astype(BF16)
 
 
-def second_table(length, stations):
+def second_table(length, stations, cores=None):
     turn = rotation(*small_tables(length)) * (FA * length) ** -0.5
-    turn = turn.reshape(2, 2, length, stations, length // stations)
-    table = np.einsum("dcbnm,st->nsdmctb", turn, np.eye(2))
+    turn = turn.reshape(2, 2, length, stations, cores or 1, -1)
+    order = "nsdqmctb" if cores is None else "nqdsmctb"
+    table = np.einsum("dcbnqm,st->" + order, turn, np.eye(2))
     return table.reshape(4 * length, 4 * length).astype(BF16)
 
 
@@ -56,12 +58,12 @@
     return lax.dot_general(left, right, (((1,), (axis,)), ((), ())), preferred_element_type=F32)
 
 
-def spectra_kernel(first, count, taps, stations, last, *refs):
+def spectra_kernel(first, count, taps, stations, last, split, *refs):
     samples, earlier, passed, prototype, first_hbm, twist_hbm, second_hbm = refs[:7]
     outs = refs[7 : 7 + stations]
     refs = refs[7 + stations :]
     tail = None
-    if last:
+    if last or split:
         tail, refs = refs[0], refs[1:]
     frames, wide, filtered, proto, weights, first_ref, twist_ref, second_in, second, sems = refs
     per = FA
@@ -149,9 +151,14 @@
         copy.wait()
     share = second_in.shape[0] // stations
     me = lax.axis_index("stn")
-    for offset in range(stations):
-        start = pl.multiple_of((me ^ offset) * share, share)
-        second[offset * share : (offset + 1) * share] = second_in[pl.ds(start, share)]
+    parts = 2 if split else 1
+    block = share // parts
+    for part in range(parts):
+        core = (lax.axis_index("chan") ^ part) * block if split else 0
+        for offset in range(stations):
+            start = pl.multiple_of((me ^ offset) * share + core, block)
+            at = (part * stations + offset) * block
+            second[at : at + block] = second_in[pl.ds(start, block)]
     low_half = lax.broadcasted_iota(jnp.int32, (2 * per, LANES), 1) < LANES // 2
 
     def transform(index, carry):
@@ -177,8 +184,11 @@
         for member in range(2):
             lane = member * LANES
             for offset in range(stations):
-                row = offset * share
-                outs[offset][index, member] = spectra[row : row + share, lane : lane + LANES]
+                row = offset * block
+                outs[offset][index, member] = spectra[row : row + block, lane : lane + LANES]
+                if split:
+                    row = (stations + offset) * block
+                    tail[offset, index, member] = spectra[row : row + block, lane : lane + LANES]
         return carry
 
     lax.fori_loop(0, count // 4, transform, 0, unroll=2 if count % 16 else 4)
@@ -186,21 +196,24 @@
         tail_copy.wait()
 
 
-def spectra_of(first, count, samples, earlier, passed, prototype, stations, last):
+def spectra_of(first, count, samples, earlier, passed, prototype, stations, last, cores=None):
     taps, channels = prototype.shape
     length = channels // FA
     share = 4 * length // stations
     held = (taps - 1) * FA
     rows = held + count * FA
-    tables = (first_table(), twist_tables(length), second_table(length, stations))
-    out_shape = [jax.ShapeDtypeStruct((count // 4, 2, share, LANES), BF16)] * stations
+    tables = (first_table(), twist_tables(length), second_table(length, stations, cores))
+    sent = (count // 4, 2, share // (cores or 1), LANES)
+    out_shape = [jax.ShapeDtypeStruct(sent, BF16)] * stations
+    if cores:
+        out_shape.append(jax.ShapeDtypeStruct((stations,) + sent, BF16))
     if last:
         out_shape.append(jax.ShapeDtypeStruct((2, held, LANES), BF16))
     return pl.pallas_call(
-        functools.partial(spectra_kernel, first, count, taps, stations, last),
+        functools.partial(spectra_kernel, first, count, taps, stations, last, bool(cores)),
         out_shape=out_shape,
         in_specs=[ANY] * 7,
-        out_specs=[VMEM] * stations + [ANY] * last,
+        out_specs=[VMEM] * stations + [ANY] * last + [VMEM] * bool(cores),
         scratch_shapes=[
             pltpu.VMEM((2, rows, LANES), BF16),
             pltpu.VMEM((2, rows, LANES), F32),
@@ -220,6 +233,27 @@
     )(samples, earlier, passed, prototype, *tables)
 
 
+def join_kernel(stations, *refs):
+    mine, twin, outs = refs[:stations], refs[stations], refs[stations + 1 :]
+    half = mine[0].shape[0]
+    for offset in range(stations):
+        outs[offset][:half] = mine[offset][...]
+        outs[offset][half:] = twin[offset]
+
+
+def join(mine, twin):
+    shape = (2 * mine[0].shape[0],) + mine[0].shape[1:]
+    return pl.pallas_call(
+        functools.partial(join_kernel, len(mine)),
+        out_shape=[jax.ShapeDtypeStruct(shape, BF16)] * len(mine),
+        in_specs=[VMEM] * (len(mine) + 1),
+        out_specs=[VMEM] * len(mine),
+        compiler_params=pltpu.CompilerParams(vmem_limit_bytes=12 * 2**20),
+        cost_estimate=pl.CostEstimate(flops=10**6, bytes_accessed=10**6, transcendentals=0),
+        name="join",
+    )(*mine, twin)
+
+
 def pair_rows(inputs):
     pairs = [(a, b) for a in range(inputs) for b in range(a, inputs)]
     return {pair: row for row, pair in enumerate(pairs)}
@@ -230,7 +264,7 @@
     before = refs[stations] if carried else None
     out = refs[-1]
     rows = pair_rows(2 * stations)
-    span = blocks[0].shape[2] // 4
+    span = SUBLANES
     group = 4
 
     def load(member, step, low):
@@ -246,7 +280,7 @@
             wanted = [(a, b, comp) for a, b in members for comp in range(2) if a != b or comp == 0]
 
             def body(step, sums):
-                for low in range(2):
+                for low in range(blocks[0].shape[2] // (2 * span)):
                     a_side = {a: load(a, step, low) for a in a_list}
                     b_side = a_side
                     if right != left:
@@ -288,10 +322,10 @@
 def products_of(blocks, before, fold):
     stations = len(blocks)
     count = len(pair_rows(2 * stations)) * (1 if fold else 2)
-    span = blocks[0].shape[2] // 4
+    span = SUBLANES
     carried = before is not None
     arrays = list(blocks) + ([before] if carried else [])
-    steps = 4 * blocks[0].shape[0]
+    steps = blocks[0].shape[0] * blocks[0].shape[2] // 8
     return pl.pallas_call(
         functools.partial(products_kernel, stations, carried, fold),
         out_shape=jax.ShapeDtypeStruct((count * span, LANES), F32),
@@ -305,7 +339,7 @@
     )(*arrays)
 
 
-def visibility_kernel(stations, total, own, other, out):
+def visibility_kernel(stations, total, own, other, late, out):
     inputs = 2 * stations
     rows = pair_rows(inputs)
     count = len(rows)
@@ -328,7 +362,10 @@
     core = lax.axis_index("chan")
     for low in range(mine):
         at = pl.ds(core * mine + low, count, stride=span)
-        lanes = ((own[at] + other[at]) * (1.0 / total)).T
+        both = own[at] + other[at]
+        for half in range(2):
+            both = both + late[pl.ds(half * mine + low, count, stride=span)]
+        lanes = (both * (1.0 / total)).T
         for comp in range(2):
             rest = lanes[comp * FA : (comp + 1) * FA]
             value = None
@@ -360,6 +397,7 @@
     stream = by_tile(voltage)
     earlier = by_tile(earlier_samples)
     whole = sum(SHARES)
+    staged = length // stations == SUBLANES
     first = spectra_here
     chunks = []
     passed = earlier
@@ -369,30 +407,46 @@
         history = earlier if first else passed
         blocks = list(
             spectra_of(
-                first, count, stream, earlier, history, prototype, stations, chunk == 0
+                first,
+                count,
+                stream,
+                earlier,
+                history,
+                prototype,
+                stations,
+                chunk == 0,
+                cores if staged and first == 0 else None,
             )
         )
         if chunk == 0:
             route = [(i, i + 1) for i in range(cores - 1)]
             passed = lax.ppermute(blocks.pop(), "chan", route)
         chunks.append(blocks)
-    if 2 * length // stations == 16:
+    if staged:
+        swap = [(i, i ^ 1) for i in range(cores)]
         sums = None
         for chunk, blocks in enumerate(chunks):
+            late = chunk == len(chunks) - 1
+            if late:
+                twin = lax.ppermute(blocks.pop(), "chan", swap)
+                blocks = list(join(blocks, twin))
             for offset in send_order(stations):
                 route = [(i, i ^ offset) for i in range(stations)]
                 blocks[offset] = lax.ppermute(blocks[offset], "stn", route)
-            sums = products_of(blocks, sums, chunk == len(chunks) - 1)
-        other = lax.ppermute(sums, "chan", [(i, i ^ 1) for i in range(cores)])
+            if late:
+                newest = products_of(blocks, None, True)
+            else:
+                sums = products_of(blocks, sums, chunk == len(chunks) - 2)
+        other = lax.ppermute(sums, "chan", swap)
         owned = channels // (stations * cores)
         return pl.pallas_call(
             functools.partial(visibility_kernel, stations, total),
             out_shape=jax.ShapeDtypeStruct((2, owned, 4 * stations * stations), F32),
-            in_specs=[VMEM, VMEM],
+            in_specs=[VMEM] * 3,
             out_specs=VMEM,
             compiler_params=pltpu.CompilerParams(vmem_limit_bytes=12 * 2**20),
             name="visibility",
-        )(sums, other)
+        )(sums, other, newest)
     joined = [jnp.concatenate([blocks[d] for blocks in chunks]) for d in range(stations)]
     joined = jnp.stack(joined)[jnp.arange(stations) ^ lax.axis_index("stn")]
     span = length // stations // cores

time: 126 us -> 147 us (1.17); the launches traced: 125 us -> 144 us
  waiting for transfers between devices: 24.3 us -> 36.9 us
  starting transfers between devices: 59.4 us -> 65 us
    ppermute x28, waiting for transfers between devices: 22.7 us -> 35.4 us  [shards(): blocks[offset] = lax.ppermute(blocks[offset], 'stn', route)]
    ppermute x28, starting transfers between devices: 54.6 us -> 58.5 us  [shards(): blocks[offset] = lax.ppermute(blocks[offset], 'stn', route)]
    ppermute x1 -> x2, starting transfers between devices: 3.47 us -> 5.03 us  [the longest x1 4.93 us: shards(): other = lax.ppermute(sums, 'chan', swap)]
  transfers between devices with their start and end apart: 30 -> 31, of which waited for: 5 -> 8; matrix products, arithmetic and copies ran while one was open for 0% -> 0% of each run, Pallas kernels for 25% -> 23%
where the time goes in v3:
time: 147 us; the launch traced here: 144 us
  starting transfers between devices  65 us (44%)
  Pallas kernels  42.3 us (29%)
  waiting for transfers between devices  36.9 us (25%)
    ppermute x28, starting transfers between devices, shards(): blocks[offset] = lax.ppermute(blocks[offset], 'stn', route)  58.5 us
    ppermute x28, waiting for transfers between devices, shards(): blocks[offset] = lax.ppermute(blocks[offset], 'stn', route)  35.4 us
    pallas_call x4, Pallas kernels, spectra_of(): pl.pallas_call(functools.partial(spectra_kernel, first, count, taps, stat...  26.6 us
    pallas_call x4, Pallas kernels, products_of(): pl.pallas_call(functools.partial(products_kernel, stations, carried, fold...  14.3 us
    ppermute x1, starting transfers between devices, shards(): other = lax.ppermute(sums, 'chan', swap)  4.93 us
  transfers between devices with their start and end apart: 31, of which 8 were waited for; matrix products, arithmetic and copies ran while one was open for 0% of the time, Pallas kernels for 23%

profile of v3, /device:TPU:1, one launch (start us, length us, event | category | flops | bytes accessed | tf_op | source)
XLA Modules:
  0.0 144.4 jit_solution(16221563782766976888)
XLA Ops:
  0.0 0.0 copy-start.3
  0.0 0.0 copy-start.4
  0.0 7.2 %shard_map.147 = (bf16[8,2,32,128]{3,2,1,0:T(8,128)(2,1)}, bf16[8,2,32,128]{3,2,1,0:T(8,128)(2,1)}, bf16[8,2,32,128]{3,2,1,0:T(8,128)(2,1)}, bf16[8,2,32,128]{3,...) custom-call(bf16[2,8192,128]{2,1,0:T(8,128)(2,1)} %bitcast.10, ...), custom_call_target="tpu_custom_call" | custom-call | flops 256000000 | bytes 2097152 | tf_op jit(solution)/shard_map/pallas_call | solution.py:212
  7.3 2.1 %collective-permute-start.14 = (bf16[8,2,32,128]{3,2,1,0:T(8,128)(2,1)}, bf16[8,2,32,128]{3,2,1,0:T(8,128)(2,1)S(1)}, u32[]{:S(2)}, u32[]{:S(2)}) collective-permute-start(bf16[8,2,32,128]{3,2,1,0:T(8,128)(2,1)} %get-tuple-element.64), channel_id=1, source_target_pairs={{0,2},{2,0},{4,6},{6,4},{8,10},{10,8},{12,14},{14,12},{1,3},{3,1},... | collective-permute-start | bytes 393224 | tf_op jit(solution)/shard_map/ppermute | solution.py:435
  9.4 1.3 collective-permute-start.15
  10.7 0.1 collective-permute-start.16
  10.9 8.0 %shard_map.146 = (bf16[10,2,32,128]{3,2,1,0:T(8,128)(2,1)S(1)}, bf16[10,2,32,128]{3,2,1,0:T(8,128)(2,1)S(1)}, bf16[10,2,32,128]{3,2,1,0:T(8,128)(2,1)S(1)}, bf16...) custom-call(bf16[2,8192,128]{2,1,0:T(8,128)(2,1)S(1)} %bitcast.11, ...), custom_call_target="tpu_custom_call" | custom-call | flops 320000000 | bytes 2621440 | tf_op jit(solution)/shard_map/pallas_call | solution.py:212
  18.8 2.4 %collective-permute-start.10 = (bf16[10,2,32,128]{3,2,1,0:T(8,128)(2,1)S(1)}, bf16[10,2,32,128]{3,2,1,0:T(8,128)(2,1)S(1)}, u32[]{:S(2)}, u32[]{:S(2)}) collective-permute-start(bf16[10,2,32,128]{3,2,1,0:T(8,128)(2,1)S(1)} %get-tuple-element.59), channel_id=1, source_target_pairs={{0,8},{2,10},{4,12},{6,14},{8,0},{10,2},{12,4},{14,6},{1,9},{3,11}... | collective-permute-start | bytes 491528 | tf_op jit(solution)/shard_map/ppermute | solution.py:435
  21.3 0.1 collective-permute-start.17
  21.4 3.2 %collective-permute-start.18 = (bf16[8,2,32,128]{3,2,1,0:T(8,128)(2,1)S(1)}, bf16[8,2,32,128]{3,2,1,0:T(8,128)(2,1)S(1)}, u32[]{:S(2)}, u32[]{:S(2)}) collective-permute-start(bf16[8,2,32,128]{3,2,1,0:T(8,128)(2,1)S(1)} %copy-done.11), channel_id=1, source_target_pairs={{0,10},{2,8},{4,14},{6,12},{8,2},{10,0},{12,6},{14,4},{1,11},{3,9}... | collective-permute-start | bytes 393224 | tf_op jit(solution)/shard_map/ppermute | solution.py:435
  24.6 1.1 collective-permute-start.19
  25.7 2.1 %collective-permute-start.20 = (bf16[8,2,32,128]{3,2,1,0:T(8,128)(2,1)S(1)}, bf16[8,2,32,128]{3,2,1,0:T(8,128)(2,1)S(1)}, u32[]{:S(2)}, u32[]{:S(2)}) collective-permute-start(bf16[8,2,32,128]{3,2,1,0:T(8,128)(2,1)S(1)} %copy-done.9), channel_id=1, source_target_pairs={{0,14},{2,12},{4,10},{6,8},{8,6},{10,4},{12,2},{14,0},{1,15},{3,13... | collective-permute-start | bytes 393224 | tf_op jit(solution)/shard_map/ppermute | solution.py:435
  27.8 14.6 %collective-permute-done.17.refs_4_ = bf16[8,2,32,128]{3,2,1,0:T(8,128)(2,1)S(1)} collective-permute-done((bf16[8,2,32,128]{3,2,1,0:T(8,128)(2,1)S(1)}, bf16[8,2,32,128]{3,2,1,0:T(8,128)(2,1)S(1)}, u32[]{:S(2)}, u32[]{:S(2)}) %collective-permute-start.17) | collective-permute-done | bytes 131104 | tf_op jit(solution)/shard_map/ppermute | solution.py:435
  42.4 0.3 collective-permute-start.11
  42.7 3.5 %collective-permute-done.18.refs_5_ = bf16[8,2,32,128]{3,2,1,0:T(8,128)(2,1)S(1)} collective-permute-done((bf16[8,2,32,128]{3,2,1,0:T(8,128)(2,1)S(1)}, bf16[8,2,32,128]{3,2,1,0:T(8,128)(2,1)S(1)}, u32[]{:S(2)}, u32[]{:S(2)}) %collective-permute-start.18) | collective-permute-done | bytes 131104 | tf_op jit(solution)/shard_map/ppermute | solution.py:435
  46.3 7.7 %collective-permute-start.12 = (bf16[10,2,32,128]{3,2,1,0:T(8,128)(2,1)S(1)}, bf16[10,2,32,128]{3,2,1,0:T(8,128)(2,1)S(1)}, u32[]{:S(2)}, u32[]{:S(2)}) collective-permute-start(bf16[10,2,32,128]{3,2,1,0:T(8,128)(2,1)S(1)} %get-tuple-element.61), channel_id=1, source_target_pairs={{0,12},{2,14},{4,8},{6,10},{8,4},{10,6},{12,0},{14,2},{1,13},{3,15... | collective-permute-start | bytes 491528 | tf_op jit(solution)/shard_map/ppermute | solution.py:435
  54.0 1.2 collective-permute-start.7
  55.2 8.9 %collective-permute-start.8 = (bf16[10,2,32,128]{3,2,1,0:T(8,128)(2,1)S(1)}, bf16[10,2,32,128]{3,2,1,0:T(8,128)(2,1)S(1)}, u32[]{:S(2)}, u32[]{:S(2)}) collective-permute-start(bf16[10,2,32,128]{3,2,1,0:T(8,128)(2,1)S(1)} %get-tuple-element.57), channel_id=1, source_target_pairs={{0,4},{2,6},{4,0},{6,2},{8,12},{10,14},{12,8},{14,10},{1,5},{3,7},... | collective-permute-start | bytes 491528 | tf_op jit(solution)/shard_map/ppermute | solution.py:435
  64.1 1.8 %collective-permute-done.11.refs_5_ = bf16[10,2,32,128]{3,2,1,0:T(8,128)(2,1)S(1)} collective-permute-done((bf16[10,2,32,128]{3,2,1,0:T(8,128)(2,1)S(1)}, bf16[10,2,32,128]{3,2,1,0:T(8,128)(2,1)S(1)}, u32[]{:S(2)}, u32[]{:S(2)}) %collective-permute-start.11) | collective-permute-done | bytes 163872 | tf_op jit(solution)/shard_map/ppermute | solution.py:435
  66.0 1.4 collective-permute-start.22
  67.4 8.0 %shard_map.145 = (bf16[10,2,32,128]{3,2,1,0:T(8,128)(2,1)S(1)}, bf16[10,2,32,128]{3,2,1,0:T(8,128)(2,1)S(1)}, bf16[10,2,32,128]{3,2,1,0:T(8,128)(2,1)S(1)}, bf16...) custom-call(bf16[2,8192,128]{2,1,0:T(8,128)(2,1)S(1)} %bitcast.12, ...), custom_call_target="tpu_custom_call" | custom-call | flops 320000000 | bytes 2621440 | tf_op jit(solution)/shard_map/pallas_call | solution.py:212
  75.4 1.5 %collective-permute-start.9 = (bf16[10,2,32,128]{3,2,1,0:T(8,128)(2,1)S(1)}, bf16[10,2,32,128]{3,2,1,0:T(8,128)(2,1)S(1)}, u32[]{:S(2)}, u32[]{:S(2)}) collective-permute-start(bf16[10,2,32,128]{3,2,1,0:T(8,128)(2,1)S(1)} %get-tuple-element.58), channel_id=1, source_target_pairs={{0,6},{2,4},{4,2},{6,0},{8,14},{10,12},{12,10},{14,8},{1,7},{3,5},... | collective-permute-start | bytes 491528 | tf_op jit(solution)/shard_map/ppermute | solution.py:435
  76.8 0.2 collective-permute-start
  77.1 1.0 collective-permute-start.1
  78.1 1.4 collective-permute-start.2
  79.5 1.1 collective-permute-done.9.refs_3_
  80.6 2.7 %collective-permute-start.3 = (bf16[10,2,32,128]{3,2,1,0:T(8,128)(2,1)S(1)}, bf16[10,2,32,128]{3,2,1,0:T(8,128)(2,1)S(1)}, u32[]{:S(2)}, u32[]{:S(2)}) collective-permute-start(bf16[10,2,32,128]{3,2,1,0:T(8,128)(2,1)S(1)} %get-tuple-element.51), channel_id=1, source_target_pairs={{0,8},{2,10},{4,12},{6,14},{8,0},{10,2},{12,4},{14,6},{1,9},{3,11}... | collective-permute-start | bytes 491528 | tf_op jit(solution)/shard_map/ppermute | solution.py:435
  83.3 3.4 %collective-permute-done.refs_1_ = bf16[10,2,32,128]{3,2,1,0:T(8,128)(2,1)S(1)} collective-permute-done((bf16[10,2,32,128]{3,2,1,0:T(8,128)(2,1)S(1)}, bf16[10,2,32,128]{3,2,1,0:T(8,128)(2,1)S(1)}, u32[]{:S(2)}, u32[]{:S(2)}) %collective-permute-start) | collective-permute-done | bytes 163872 | tf_op jit(solution)/shard_map/ppermute | solution.py:435
  86.7 3.0 %collective-permute-start.4 = (bf16[10,2,32,128]{3,2,1,0:T(8,128)(2,1)S(1)}, bf16[10,2,32,128]{3,2,1,0:T(8,128)(2,1)S(1)}, u32[]{:S(2)}, u32[]{:S(2)}) collective-permute-start(bf16[10,2,32,128]{3,2,1,0:T(8,128)(2,1)S(1)} %get-tuple-element.52), channel_id=1, source_target_pairs={{0,10},{2,8},{4,14},{6,12},{8,2},{10,0},{12,6},{14,4},{1,11},{3,9}... | collective-permute-start | bytes 491528 | tf_op jit(solution)/shard_map/ppermute | solution.py:435
  89.7 5.1 %collective-permute-start.6 = (bf16[10,2,32,128]{3,2,1,0:T(8,128)(2,1)S(1)}, bf16[10,2,32,128]{3,2,1,0:T(8,128)(2,1)S(1)}, u32[]{:S(2)}, u32[]{:S(2)}) collective-permute-start(bf16[10,2,32,128]{3,2,1,0:T(8,128)(2,1)S(1)} %get-tuple-element.54), channel_id=1, source_target_pairs={{0,14},{2,12},{4,10},{6,8},{8,6},{10,4},{12,2},{14,0},{1,15},{3,13... | collective-permute-start | bytes 491528 | tf_op jit(solution)/shard_map/ppermute | solution.py:435
  94.8 3.1 %products.4.refs_8_ = f32[2176,128]{1,0:T(8,128)S(1)} custom-call(bf16[8,2,32,128]{3,2,1,0:T(8,128)(2,1)S(1)} %copy-done.7, bf16[8,2,32,128]{3,2,1,0:T(8,128)(2,1)S(1)} %collective-permute-done.14.refs_1_, bf16[8,2,32,128]{3,2,1,0:T(8,128)(2,1)S(1)} %collective-permute-done.15.refs_2_, bf16[8,2,32,128]{3,2,1,0:T(8,128)(2,1)S(1)} %collective-permute-done.16.refs_3_, ...), custom_call_target="tpu_custom_call" | custom-call | flops 128000000 | bytes 2097152 | tf_op jit(solution)/shard_map/products/pallas_call | solution.py:329
  97.8 3.8 %products.5.refs_8_ = f32[2176,128]{1,0:T(8,128)S(1)} custom-call(bf16[10,2,32,128]{3,2,1,0:T(8,128)(2,1)S(1)} %get-tuple-element.55.refs_0_, bf16[10,2,32,128]{3,2,1,0:T(8,128)(2,1)S(1)} %collective-permute-done.7.refs_1_, bf16[10,2,32,128]{3,2,1,0:T(8,128)(2,1)S(1)} %collective-permute-done.8.refs_2_, ...), custom_call_target="tpu_custom_call" | custom-call | flops 160000000 | bytes 2621440 | tf_op jit(solution)/shard_map/products/pallas_call | solution.py:329
  101.7 5.9 %collective-permute-done.4.refs_5_ = bf16[10,2,32,128]{3,2,1,0:T(8,128)(2,1)S(1)} collective-permute-done((bf16[10,2,32,128]{3,2,1,0:T(8,128)(2,1)S(1)}, bf16[10,2,32,128]{3,2,1,0:T(8,128)(2,1)S(1)}, u32[]{:S(2)}, u32[]{:S(2)}) %collective-permute-start.4) | collective-permute-done | bytes 163872 | tf_op jit(solution)/shard_map/ppermute | solution.py:435
  107.6 4.7 %products.6.own = f32[1088,128]{1,0:T(8,128)S(1)} custom-call(bf16[10,2,32,128]{3,2,1,0:T(8,128)(2,1)S(1)} %get-tuple-element.47.refs_0_, bf16[10,2,32,128]{3,2,1,0:T(8,128)(2,1)S(1)} %collective-permute-done.refs_1_, bf16[10,2,32,128]{3,2,1,0:T(8,128)(2,1)S(1)} %collective-permute-done.1.refs_2_, ...), custom_call_target="tpu_custom_call" | custom-call | flops 160000000 | bytes 2621440 | tf_op jit(solution)/shard_map/products/pallas_call | solution.py:329
  112.3 4.9 %collective-permute-start.21 = (f32[1088,128]{1,0:T(8,128)S(1)}, f32[1088,128]{1,0:T(8,128)S(1)}, u32[]{:S(2)}, u32[]{:S(2)}) collective-permute-start(f32[1088,128]{1,0:T(8,128)S(1)} %products.6.own), channel_id=1, source_target_pairs={{0,1},{1,0},{2,3},{3,2},{4,5},{5,4},{6,7},{7,6},{8,9},{9,8},{10,11... | collective-permute-start | bytes 1671176 | tf_op jit(solution)/shard_map/ppermute | solution.py:440
  117.2 3.4 %shard_map.148 = (bf16[4,2,16,128]{3,2,1,0:T(8,128)(2,1)S(1)}, bf16[4,2,16,128]{3,2,1,0:T(8,128)(2,1)S(1)}, bf16[4,2,16,128]{3,2,1,0:T(8,128)(2,1)S(1)}, bf16[4,...) custom-call(bf16[2,8192,128]{2,1,0:T(8,128)(2,1)S(1)} %bitcast.13, ...), custom_call_target="tpu_custom_call" | custom-call | flops 128000000 | bytes 1048576 | tf_op jit(solution)/shard_map/pallas_call | solution.py:212
  120.6 0.1 collective-permute-start.23
  120.7 1.5 %collective-permute-done.23.refs_8_ = bf16[8,4,2,16,128]{4,3,2,1,0:T(8,128)(2,1)S(1)} collective-permute-done((bf16[8,4,2,16,128]{4,3,2,1,0:T(8,128)(2,1)S(1)}, bf16[8,4,2,16,128]{4,3,2,1,0:T(8,128)(2,1)S(1)}, u32[]{:S(2)}, u32[]{:S(2)}) %collective-permute-start.23) | collective-permute-done | bytes 262176 | tf_op jit(solution)/shard_map/ppermute | solution.py:431
  122.3 1.3 collective-permute-start.24
  123.6 4.6 %collective-permute-start.25 = (bf16[8,2,16,128]{3,2,1,0:T(8,128)(2,1)S(1)}, bf16[8,2,16,128]{3,2,1,0:T(8,128)(2,1)S(1)}, u32[]{:S(2)}, u32[]{:S(2)}) collective-permute-start(bf16[8,2,16,128]{3,2,1,0:T(8,128)(2,1)S(1)} %get-tuple-element.83), channel_id=1, source_target_pairs={{0,4},{2,6},{4,0},{6,2},{8,12},{10,14},{12,8},{14,10},{1,5},{3,7},... | collective-permute-start | bytes 196616 | tf_op jit(solution)/shard_map/ppermute | solution.py:435
  128.2 0.6 collective-permute-start.26
  128.7 1.2 collective-permute-start.27
  129.9 1.5 %collective-permute-start.28 = (bf16[8,2,16,128]{3,2,1,0:T(8,128)(2,1)S(1)}, bf16[8,2,16,128]{3,2,1,0:T(8,128)(2,1)S(1)}, u32[]{:S(2)}, u32[]{:S(2)}) collective-permute-start(bf16[8,2,16,128]{3,2,1,0:T(8,128)(2,1)S(1)} %get-tuple-element.86), channel_id=1, source_target_pairs={{0,10},{2,8},{4,14},{6,12},{8,2},{10,0},{12,6},{14,4},{1,11},{3,9}... | collective-permute-start | bytes 196616 | tf_op jit(solution)/shard_map/ppermute | solution.py:435
  131.4 2.0 %collective-permute-start.29 = (bf16[8,2,16,128]{3,2,1,0:T(8,128)(2,1)S(1)}, bf16[8,2,16,128]{3,2,1,0:T(8,128)(2,1)S(1)}, u32[]{:S(2)}, u32[]{:S(2)}) collective-permute-start(bf16[8,2,16,128]{3,2,1,0:T(8,128)(2,1)S(1)} %get-tuple-element.87), channel_id=1, source_target_pairs={{0,12},{2,14},{4,8},{6,10},{8,4},{10,6},{12,0},{14,2},{1,13},{3,15... | collective-permute-start | bytes 196616 | tf_op jit(solution)/shard_map/ppermute | solution.py:435
  133.5 1.8 %collective-permute-start.30 = (bf16[8,2,16,128]{3,2,1,0:T(8,128)(2,1)S(1)}, bf16[8,2,16,128]{3,2,1,0:T(8,128)(2,1)S(1)}, u32[]{:S(2)}, u32[]{:S(2)}) collective-permute-start(bf16[8,2,16,128]{3,2,1,0:T(8,128)(2,1)S(1)} %get-tuple-element.88), channel_id=1, source_target_pairs={{0,14},{2,12},{4,10},{6,8},{8,6},{10,4},{12,2},{14,0},{1,15},{3,13... | collective-permute-start | bytes 196616 | tf_op jit(solution)/shard_map/ppermute | solution.py:435
  135.2 5.0 %collective-permute-done.28.refs_5_ = bf16[8,2,16,128]{3,2,1,0:T(8,128)(2,1)S(1)} collective-permute-done((bf16[8,2,16,128]{3,2,1,0:T(8,128)(2,1)S(1)}, bf16[8,2,16,128]{3,2,1,0:T(8,128)(2,1)S(1)}, u32[]{:S(2)}, u32[]{:S(2)}) %collective-permute-start.28) | collective-permute-done | bytes 65568 | tf_op jit(solution)/shard_map/ppermute | solution.py:435
  140.3 2.7 %products.7.late = f32[1088,128]{1,0:T(8,128)S(1)} custom-call(bf16[8,2,16,128]{3,2,1,0:T(8,128)(2,1)S(1)} %get-tuple-element.81.refs_0_, bf16[8,2,16,128]{3,2,1,0:T(8,128)(2,1)S(1)} %collective-permute-done.24.refs_1_, bf16[8,2,16,128]{3,2,1,0:T(8,128)(2,1)S(1)} %collective-permute-done.25.refs_2_, ...), custom_call_target="tpu_custom_call" | custom-call | flops 64000000 | bytes 1048576 | tf_op jit(solution)/shard_map/products/pallas_call | solution.py:329
  143.0 1.4 visibility.1
  (50 shorter events, 0.2 us)
Async XLA Ops:
  0.0 10.8 %copy-start = (bf16[2,2,524288]{2,1,0:T(2,128)(2,1)S(1)}, bf16[2,2,524288]{2,1,0:T(2,128)(2,1)}, u32[]{:S(2)}) copy-start(bf16[2,2,524288]{2,1,0:T(2,128)(2,1)} %param.15) | copy-start | bytes 12582916
  0.0 10.8 %copy-start.1 = (bf16[2,2,61440]{2,1,0:T(2,128)(2,1)S(1)}, bf16[2,2,61440]{2,1,0:T(2,128)(2,1)}, u32[]{:S(2)}) copy-start(bf16[2,2,61440]{2,1,0:T(2,128)(2,1)} %param.16) | copy-start | bytes 1474564
  0.0 10.8 %copy-start.2 = (f32[16,4096]{1,0:T(8,128)S(1)}, f32[16,4096]{1,0:T(8,128)}, u32[]{:S(2)}) copy-start(f32[16,4096]{1,0:T(8,128)} %refs_3_.7) | copy-start | bytes 786436
  0.0 10.8 %copy-start.3 = (bf16[256,256]{1,0:T(8,128)(2,1)S(1)}, bf16[256,256]{1,0:T(8,128)(2,1)}, u32[]{:S(2)}) copy-start(bf16[256,256]{1,0:T(8,128)(2,1)} %constant.8.clone.refs_4_) | copy-start | bytes 393220
  0.0 10.8 %copy-start.4 = (bf16[256,256]{1,0:T(8,128)(2,1)S(1)}, bf16[256,256]{1,0:T(8,128)(2,1)}, u32[]{:S(2)}) copy-start(bf16[256,256]{1,0:T(8,128)(2,1)} %constant.10.clone.refs_6_) | copy-start | bytes 393220
  0.0 10.8 %copy-start.5 = (f32[2,64,128]{2,1,0:T(8,128)S(1)}, f32[2,64,128]{2,1,0:T(8,128)}, u32[]{:S(2)}) copy-start(f32[2,64,128]{2,1,0:T(8,128)} %constant.9.clone.refs_5_) | copy-start | bytes 196612
  7.3 14.1 %collective-permute-start.14 = (bf16[8,2,32,128]{3,2,1,0:T(8,128)(2,1)}, bf16[8,2,32,128]{3,2,1,0:T(8,128)(2,1)S(1)}, u32[]{:S(2)}, u32[]{:S(2)}) collective-permute-start(bf16[8,2,32,128]{3,2,1,0:T(8,128)(2,1)} %get-tuple-element.64), channel_id=1, source_target_pairs={{0,2},{2,0},{4,6},{6,4},{8,10},{10,8},{12,14},{14,12},{1,3},{3,1},... | collective-permute-start | bytes 393224 | tf_op jit(solution)/shard_map/ppermute | solution.py:435
  9.4 15.2 %collective-permute-start.15 = (bf16[8,2,32,128]{3,2,1,0:T(8,128)(2,1)}, bf16[8,2,32,128]{3,2,1,0:T(8,128)(2,1)S(1)}, u32[]{:S(2)}, u32[]{:S(2)}) collective-permute-start(bf16[8,2,32,128]{3,2,1,0:T(8,128)(2,1)} %get-tuple-element.65), channel_id=1, source_target_pairs={{0,4},{2,6},{4,0},{6,2},{8,12},{10,14},{12,8},{14,10},{1,5},{3,7},... | collective-permute-start | bytes 393224 | tf_op jit(solution)/shard_map/ppermute | solution.py:435
  10.7 10.6 %copy-start.12 = (bf16[8,2,32,128]{3,2,1,0:T(8,128)(2,1)S(1)}, bf16[8,2,32,128]{3,2,1,0:T(8,128)(2,1)}, u32[]{:S(2)}) copy-start(bf16[8,2,32,128]{3,2,1,0:T(8,128)(2,1)} %get-tuple-element.67) | copy-start | bytes 393220
  10.7 10.7 %copy-start.11 = (bf16[8,2,32,128]{3,2,1,0:T(8,128)(2,1)S(1)}, bf16[8,2,32,128]{3,2,1,0:T(8,128)(2,1)}, u32[]{:S(2)}) copy-start(bf16[8,2,32,128]{3,2,1,0:T(8,128)(2,1)} %get-tuple-element.68) | copy-start | bytes 393220
  10.7 13.9 %copy-start.10 = (bf16[8,2,32,128]{3,2,1,0:T(8,128)(2,1)S(1)}, bf16[8,2,32,128]{3,2,1,0:T(8,128)(2,1)}, u32[]{:S(2)}) copy-start(bf16[8,2,32,128]{3,2,1,0:T(8,128)(2,1)} %get-tuple-element.69) | copy-start | bytes 393220
  10.7 15.0 %copy-start.9 = (bf16[8,2,32,128]{3,2,1,0:T(8,128)(2,1)S(1)}, bf16[8,2,32,128]{3,2,1,0:T(8,128)(2,1)}, u32[]{:S(2)}) copy-start(bf16[8,2,32,128]{3,2,1,0:T(8,128)(2,1)} %get-tuple-element.70) | copy-start | bytes 393220
  10.7 55.2 %copy-start.8 = (bf16[2,960,128]{2,1,0:T(8,128)(2,1)S(1)}, bf16[2,960,128]{2,1,0:T(8,128)(2,1)}, u32[]{:S(2)}) copy-start(bf16[2,960,128]{2,1,0:T(8,128)(2,1)} %get-tuple-element.71) | copy-start | bytes 1474564
  10.7 15.0 %collective-permute-start.16 = (bf16[8,2,32,128]{3,2,1,0:T(8,128)(2,1)}, bf16[8,2,32,128]{3,2,1,0:T(8,128)(2,1)S(1)}, u32[]{:S(2)}, u32[]{:S(2)}) collective-permute-start(bf16[8,2,32,128]{3,2,1,0:T(8,128)(2,1)} %get-tuple-element.66), channel_id=1, source_target_pairs={{0,6},{2,4},{4,2},{6,0},{8,14},{10,12},{12,10},{14,8},{1,7},{3,5},... | collective-permute-start | bytes 393224 | tf_op jit(solution)/shard_map/ppermute | solution.py:435
  18.8 36.4 %collective-permute-start.10 = (bf16[10,2,32,128]{3,2,1,0:T(8,128)(2,1)S(1)}, bf16[10,2,32,128]{3,2,1,0:T(8,128)(2,1)S(1)}, u32[]{:S(2)}, u32[]{:S(2)}) collective-permute-start(bf16[10,2,32,128]{3,2,1,0:T(8,128)(2,1)S(1)} %get-tuple-element.59), channel_id=1, source_target_pairs={{0,8},{2,10},{4,12},{6,14},{8,0},{10,2},{12,4},{14,6},{1,9},{3,11}... | collective-permute-start | bytes 491528 | tf_op jit(solution)/shard_map/ppermute | solution.py:435
  21.3 21.1 %collective-permute-start.17 = (bf16[8,2,32,128]{3,2,1,0:T(8,128)(2,1)S(1)}, bf16[8,2,32,128]{3,2,1,0:T(8,128)(2,1)S(1)}, u32[]{:S(2)}, u32[]{:S(2)}) collective-permute-start(bf16[8,2,32,128]{3,2,1,0:T(8,128)(2,1)S(1)} %copy-done.12), channel_id=1, source_target_pairs={{0,8},{2,10},{4,12},{6,14},{8,0},{10,2},{12,4},{14,6},{1,9},{3,11}... | collective-permute-start | bytes 393224 | tf_op jit(solution)/shard_map/ppermute | solution.py:435
  21.4 24.9 %collective-permute-start.18 = (bf16[8,2,32,128]{3,2,1,0:T(8,128)(2,1)S(1)}, bf16[8,2,32,128]{3,2,1,0:T(8,128)(2,1)S(1)}, u32[]{:S(2)}, u32[]{:S(2)}) collective-permute-start(bf16[8,2,32,128]{3,2,1,0:T(8,128)(2,1)S(1)} %copy-done.11), channel_id=1, source_target_pairs={{0,10},{2,8},{4,14},{6,12},{8,2},{10,0},{12,6},{14,4},{1,11},{3,9}... | collective-permute-start | bytes 393224 | tf_op jit(solution)/shard_map/ppermute | solution.py:435
  24.6 29.4 %collective-permute-start.19 = (bf16[8,2,32,128]{3,2,1,0:T(8,128)(2,1)S(1)}, bf16[8,2,32,128]{3,2,1,0:T(8,128)(2,1)S(1)}, u32[]{:S(2)}, u32[]{:S(2)}) collective-permute-start(bf16[8,2,32,128]{3,2,1,0:T(8,128)(2,1)S(1)} %copy-done.10), channel_id=1, source_target_pairs={{0,12},{2,14},{4,8},{6,10},{8,4},{10,6},{12,0},{14,2},{1,13},{3,15... | collective-permute-start | bytes 393224 | tf_op jit(solution)/shard_map/ppermute | solution.py:435
  25.7 28.3 %collective-permute-start.20 = (bf16[8,2,32,128]{3,2,1,0:T(8,128)(2,1)S(1)}, bf16[8,2,32,128]{3,2,1,0:T(8,128)(2,1)S(1)}, u32[]{:S(2)}, u32[]{:S(2)}) collective-permute-start(bf16[8,2,32,128]{3,2,1,0:T(8,128)(2,1)S(1)} %copy-done.9), channel_id=1, source_target_pairs={{0,14},{2,12},{4,10},{6,8},{8,6},{10,4},{12,2},{14,0},{1,15},{3,13... | collective-permute-start | bytes 393224 | tf_op jit(solution)/shard_map/ppermute | solution.py:435
  42.4 23.5 %collective-permute-start.11 = (bf16[10,2,32,128]{3,2,1,0:T(8,128)(2,1)S(1)}, bf16[10,2,32,128]{3,2,1,0:T(8,128)(2,1)S(1)}, u32[]{:S(2)}, u32[]{:S(2)}) collective-permute-start(bf16[10,2,32,128]{3,2,1,0:T(8,128)(2,1)S(1)} %get-tuple-element.60), channel_id=1, source_target_pairs={{0,10},{2,8},{4,14},{6,12},{8,2},{10,0},{12,6},{14,4},{1,11},{3,9}... | collective-permute-start | bytes 491528 | tf_op jit(solution)/shard_map/ppermute | solution.py:435
  46.3 29.1 %collective-permute-start.12 = (bf16[10,2,32,128]{3,2,1,0:T(8,128)(2,1)S(1)}, bf16[10,2,32,128]{3,2,1,0:T(8,128)(2,1)S(1)}, u32[]{:S(2)}, u32[]{:S(2)}) collective-permute-start(bf16[10,2,32,128]{3,2,1,0:T(8,128)(2,1)S(1)} %get-tuple-element.61), channel_id=1, source_target_pairs={{0,12},{2,14},{4,8},{6,10},{8,4},{10,6},{12,0},{14,2},{1,13},{3,15... | collective-permute-start | bytes 491528 | tf_op jit(solution)/shard_map/ppermute | solution.py:435
  54.0 22.8 %collective-permute-start.13 = (bf16[10,2,32,128]{3,2,1,0:T(8,128)(2,1)S(1)}, bf16[10,2,32,128]{3,2,1,0:T(8,128)(2,1)S(1)}, u32[]{:S(2)}, u32[]{:S(2)}) collective-permute-start(bf16[10,2,32,128]{3,2,1,0:T(8,128)(2,1)S(1)} %get-tuple-element.62), channel_id=1, source_target_pairs={{0,14},{2,12},{4,10},{6,8},{8,6},{10,4},{12,2},{14,0},{1,15},{3,13... | collective-permute-start | bytes 491528 | tf_op jit(solution)/shard_map/ppermute | solution.py:435
  54.0 23.0 %collective-permute-start.7 = (bf16[10,2,32,128]{3,2,1,0:T(8,128)(2,1)S(1)}, bf16[10,2,32,128]{3,2,1,0:T(8,128)(2,1)S(1)}, u32[]{:S(2)}, u32[]{:S(2)}) collective-permute-start(bf16[10,2,32,128]{3,2,1,0:T(8,128)(2,1)S(1)} %get-tuple-element.56), channel_id=1, source_target_pairs={{0,2},{2,0},{4,6},{6,4},{8,10},{10,8},{12,14},{14,12},{1,3},{3,1},... | collective-permute-start | bytes 491528 | tf_op jit(solution)/shard_map/ppermute | solution.py:435
  55.2 22.9 %collective-permute-start.8 = (bf16[10,2,32,128]{3,2,1,0:T(8,128)(2,1)S(1)}, bf16[10,2,32,128]{3,2,1,0:T(8,128)(2,1)S(1)}, u32[]{:S(2)}, u32[]{:S(2)}) collective-permute-start(bf16[10,2,32,128]{3,2,1,0:T(8,128)(2,1)S(1)} %get-tuple-element.57), channel_id=1, source_target_pairs={{0,4},{2,6},{4,0},{6,2},{8,12},{10,14},{12,8},{14,10},{1,5},{3,7},... | collective-permute-start | bytes 491528 | tf_op jit(solution)/shard_map/ppermute | solution.py:435
  66.0 28.8 %copy-start.7 = (bf16[8,2,32,128]{3,2,1,0:T(8,128)(2,1)S(1)}, bf16[8,2,32,128]{3,2,1,0:T(8,128)(2,1)}, u32[]{:S(2)}) copy-start(bf16[8,2,32,128]{3,2,1,0:T(8,128)(2,1)} %get-tuple-element.63.refs_0_) | copy-start | bytes 393220
  66.0 51.2 %collective-permute-start.22 = (bf16[2,960,128]{2,1,0:T(8,128)(2,1)S(1)}, bf16[2,960,128]{2,1,0:T(8,128)(2,1)S(1)}, u32[]{:S(2)}, u32[]{:S(2)}) collective-permute-start(bf16[2,960,128]{2,1,0:T(8,128)(2,1)S(1)} %copy-done.8), channel_id=1, source_target_pairs={{0,1},{2,3},{4,5},{6,7},{8,9},{10,11},{12,13},{14,15},{16,17},{18,... | collective-permute-start | bytes 1474568 | tf_op jit(solution)/shard_map/ppermute | solution.py:423
  75.4 5.2 %collective-permute-start.9 = (bf16[10,2,32,128]{3,2,1,0:T(8,128)(2,1)S(1)}, bf16[10,2,32,128]{3,2,1,0:T(8,128)(2,1)S(1)}, u32[]{:S(2)}, u32[]{:S(2)}) collective-permute-start(bf16[10,2,32,128]{3,2,1,0:T(8,128)(2,1)S(1)} %get-tuple-element.58), channel_id=1, source_target_pairs={{0,6},{2,4},{4,2},{6,0},{8,14},{10,12},{12,10},{14,8},{1,7},{3,5},... | collective-permute-start | bytes 491528 | tf_op jit(solution)/shard_map/ppermute | solution.py:435
  76.8 9.8 %collective-permute-start = (bf16[10,2,32,128]{3,2,1,0:T(8,128)(2,1)S(1)}, bf16[10,2,32,128]{3,2,1,0:T(8,128)(2,1)S(1)}, u32[]{:S(2)}, u32[]{:S(2)}) collective-permute-start(bf16[10,2,32,128]{3,2,1,0:T(8,128)(2,1)S(1)} %get-tuple-element.48), channel_id=1, source_target_pairs={{0,2},{2,0},{4,6},{6,4},{8,10},{10,8},{12,14},{14,12},{1,3},{3,1},... | collective-permute-start | bytes 491528 | tf_op jit(solution)/shard_map/ppermute | solution.py:435
  77.1 12.6 %collective-permute-start.1 = (bf16[10,2,32,128]{3,2,1,0:T(8,128)(2,1)S(1)}, bf16[10,2,32,128]{3,2,1,0:T(8,128)(2,1)S(1)}, u32[]{:S(2)}, u32[]{:S(2)}) collective-permute-start(bf16[10,2,32,128]{3,2,1,0:T(8,128)(2,1)S(1)} %get-tuple-element.49), channel_id=1, source_target_pairs={{0,4},{2,6},{4,0},{6,2},{8,12},{10,14},{12,8},{14,10},{1,5},{3,7},... | collective-permute-start | bytes 491528 | tf_op jit(solution)/shard_map/ppermute | solution.py:435
  78.1 11.6 %collective-permute-start.2 = (bf16[10,2,32,128]{3,2,1,0:T(8,128)(2,1)S(1)}, bf16[10,2,32,128]{3,2,1,0:T(8,128)(2,1)S(1)}, u32[]{:S(2)}, u32[]{:S(2)}) collective-permute-start(bf16[10,2,32,128]{3,2,1,0:T(8,128)(2,1)S(1)} %get-tuple-element.50), channel_id=1, source_target_pairs={{0,6},{2,4},{4,2},{6,0},{8,14},{10,12},{12,10},{14,8},{1,7},{3,5},... | collective-permute-start | bytes 491528 | tf_op jit(solution)/shard_map/ppermute | solution.py:435
  80.6 21.1 %collective-permute-start.3 = (bf16[10,2,32,128]{3,2,1,0:T(8,128)(2,1)S(1)}, bf16[10,2,32,128]{3,2,1,0:T(8,128)(2,1)S(1)}, u32[]{:S(2)}, u32[]{:S(2)}) collective-permute-start(bf16[10,2,32,128]{3,2,1,0:T(8,128)(2,1)S(1)} %get-tuple-element.51), channel_id=1, source_target_pairs={{0,8},{2,10},{4,12},{6,14},{8,0},{10,2},{12,4},{14,6},{1,9},{3,11}... | collective-permute-start | bytes 491528 | tf_op jit(solution)/shard_map/ppermute | solution.py:435
  86.7 20.9 %collective-permute-start.4 = (bf16[10,2,32,128]{3,2,1,0:T(8,128)(2,1)S(1)}, bf16[10,2,32,128]{3,2,1,0:T(8,128)(2,1)S(1)}, u32[]{:S(2)}, u32[]{:S(2)}) collective-permute-start(bf16[10,2,32,128]{3,2,1,0:T(8,128)(2,1)S(1)} %get-tuple-element.52), channel_id=1, source_target_pairs={{0,10},{2,8},{4,14},{6,12},{8,2},{10,0},{12,6},{14,4},{1,11},{3,9}... | collective-permute-start | bytes 491528 | tf_op jit(solution)/shard_map/ppermute | solution.py:435
  89.7 17.8 %collective-permute-start.5 = (bf16[10,2,32,128]{3,2,1,0:T(8,128)(2,1)S(1)}, bf16[10,2,32,128]{3,2,1,0:T(8,128)(2,1)S(1)}, u32[]{:S(2)}, u32[]{:S(2)}) collective-permute-start(bf16[10,2,32,128]{3,2,1,0:T(8,128)(2,1)S(1)} %get-tuple-element.53), channel_id=1, source_target_pairs={{0,12},{2,14},{4,8},{6,10},{8,4},{10,6},{12,0},{14,2},{1,13},{3,15... | collective-permute-start | bytes 491528 | tf_op jit(solution)/shard_map/ppermute | solution.py:435
  89.7 17.8 %collective-permute-start.6 = (bf16[10,2,32,128]{3,2,1,0:T(8,128)(2,1)S(1)}, bf16[10,2,32,128]{3,2,1,0:T(8,128)(2,1)S(1)}, u32[]{:S(2)}, u32[]{:S(2)}) collective-permute-start(bf16[10,2,32,128]{3,2,1,0:T(8,128)(2,1)S(1)} %get-tuple-element.54), channel_id=1, source_target_pairs={{0,14},{2,12},{4,10},{6,8},{8,6},{10,4},{12,2},{14,0},{1,15},{3,13... | collective-permute-start | bytes 491528 | tf_op jit(solution)/shard_map/ppermute | solution.py:435
  107.6 9.6 %copy-start.6 = (bf16[256,256]{1,0:T(8,128)(2,1)S(1)}, bf16[256,256]{1,0:T(8,128)(2,1)}, u32[]{:S(2)}) copy-start(bf16[256,256]{1,0:T(8,128)(2,1)} %constant.11.clone.refs_6_) | copy-start | bytes 393220
  112.3 30.8 %collective-permute-start.21 = (f32[1088,128]{1,0:T(8,128)S(1)}, f32[1088,128]{1,0:T(8,128)S(1)}, u32[]{:S(2)}, u32[]{:S(2)}) collective-permute-start(f32[1088,128]{1,0:T(8,128)S(1)} %products.6.own), channel_id=1, source_target_pairs={{0,1},{1,0},{2,3},{3,2},{4,5},{5,4},{6,7},{7,6},{8,9},{9,8},{10,11... | collective-permute-start | bytes 1671176 | tf_op jit(solution)/shard_map/ppermute | solution.py:440
  120.6 1.6 %collective-permute-start.23 = (bf16[8,4,2,16,128]{4,3,2,1,0:T(8,128)(2,1)S(1)}, bf16[8,4,2,16,128]{4,3,2,1,0:T(8,128)(2,1)S(1)}, u32[]{:S(2)}, u32[]{:S(2)}) collective-permute-start(bf16[8,4,2,16,128]{4,3,2,1,0:T(8,128)(2,1)S(1)} %get-tuple-element.80), channel_id=1, source_target_pairs={{0,1},{1,0},{2,3},{3,2},{4,5},{5,4},{6,7},{7,6},{8,9},{9,8},{10,11... | collective-permute-start | bytes 786440 | tf_op jit(solution)/shard_map/ppermute | solution.py:431
  122.3 7.7 %collective-permute-start.24 = (bf16[8,2,16,128]{3,2,1,0:T(8,128)(2,1)S(1)}, bf16[8,2,16,128]{3,2,1,0:T(8,128)(2,1)S(1)}, u32[]{:S(2)}, u32[]{:S(2)}) collective-permute-start(bf16[8,2,16,128]{3,2,1,0:T(8,128)(2,1)S(1)} %get-tuple-element.82), channel_id=1, source_target_pairs={{0,2},{2,0},{4,6},{6,4},{8,10},{10,8},{12,14},{14,12},{1,3},{3,1},... | collective-permute-start | bytes 196616 | tf_op jit(solution)/shard_map/ppermute | solution.py:435
  123.6 7.9 %collective-permute-start.25 = (bf16[8,2,16,128]{3,2,1,0:T(8,128)(2,1)S(1)}, bf16[8,2,16,128]{3,2,1,0:T(8,128)(2,1)S(1)}, u32[]{:S(2)}, u32[]{:S(2)}) collective-permute-start(bf16[8,2,16,128]{3,2,1,0:T(8,128)(2,1)S(1)} %get-tuple-element.83), channel_id=1, source_target_pairs={{0,4},{2,6},{4,0},{6,2},{8,12},{10,14},{12,8},{14,10},{1,5},{3,7},... | collective-permute-start | bytes 196616 | tf_op jit(solution)/shard_map/ppermute | solution.py:435
  128.2 5.3 %collective-permute-start.26 = (bf16[8,2,16,128]{3,2,1,0:T(8,128)(2,1)S(1)}, bf16[8,2,16,128]{3,2,1,0:T(8,128)(2,1)S(1)}, u32[]{:S(2)}, u32[]{:S(2)}) collective-permute-start(bf16[8,2,16,128]{3,2,1,0:T(8,128)(2,1)S(1)} %get-tuple-element.84), channel_id=1, source_target_pairs={{0,6},{2,4},{4,2},{6,0},{8,14},{10,12},{12,10},{14,8},{1,7},{3,5},... | collective-permute-start | bytes 196616 | tf_op jit(solution)/shard_map/ppermute | solution.py:435
  128.7 6.5 %collective-permute-start.27 = (bf16[8,2,16,128]{3,2,1,0:T(8,128)(2,1)S(1)}, bf16[8,2,16,128]{3,2,1,0:T(8,128)(2,1)S(1)}, u32[]{:S(2)}, u32[]{:S(2)}) collective-permute-start(bf16[8,2,16,128]{3,2,1,0:T(8,128)(2,1)S(1)} %get-tuple-element.85), channel_id=1, source_target_pairs={{0,8},{2,10},{4,12},{6,14},{8,0},{10,2},{12,4},{14,6},{1,9},{3,11}... | collective-permute-start | bytes 196616 | tf_op jit(solution)/shard_map/ppermute | solution.py:435
  129.9 10.4 %collective-permute-start.28 = (bf16[8,2,16,128]{3,2,1,0:T(8,128)(2,1)S(1)}, bf16[8,2,16,128]{3,2,1,0:T(8,128)(2,1)S(1)}, u32[]{:S(2)}, u32[]{:S(2)}) collective-permute-start(bf16[8,2,16,128]{3,2,1,0:T(8,128)(2,1)S(1)} %get-tuple-element.86), channel_id=1, source_target_pairs={{0,10},{2,8},{4,14},{6,12},{8,2},{10,0},{12,6},{14,4},{1,11},{3,9}... | collective-permute-start | bytes 196616 | tf_op jit(solution)/shard_map/ppermute | solution.py:435
  131.4 8.8 %collective-permute-start.29 = (bf16[8,2,16,128]{3,2,1,0:T(8,128)(2,1)S(1)}, bf16[8,2,16,128]{3,2,1,0:T(8,128)(2,1)S(1)}, u32[]{:S(2)}, u32[]{:S(2)}) collective-permute-start(bf16[8,2,16,128]{3,2,1,0:T(8,128)(2,1)S(1)} %get-tuple-element.87), channel_id=1, source_target_pairs={{0,12},{2,14},{4,8},{6,10},{8,4},{10,6},{12,0},{14,2},{1,13},{3,15... | collective-permute-start | bytes 196616 | tf_op jit(solution)/shard_map/ppermute | solution.py:435
  133.5 6.8 %collective-permute-start.30 = (bf16[8,2,16,128]{3,2,1,0:T(8,128)(2,1)S(1)}, bf16[8,2,16,128]{3,2,1,0:T(8,128)(2,1)S(1)}, u32[]{:S(2)}, u32[]{:S(2)}) collective-permute-start(bf16[8,2,16,128]{3,2,1,0:T(8,128)(2,1)S(1)} %get-tuple-element.88), channel_id=1, source_target_pairs={{0,14},{2,12},{4,10},{6,8},{8,6},{10,4},{12,2},{14,0},{1,15},{3,13... | collective-permute-start | bytes 196616 | tf_op jit(solution)/shard_map/ppermute | solution.py:435

commit v4 on v3

--- a/solution.py
+++ b/solution.py
@@ -259,25 +259,30 @@
     return {pair: row for row, pair in enumerate(pairs)}
 
 
-def products_kernel(stations, carried, fold, *refs):
-    blocks = refs[:stations]
-    before = refs[stations] if carried else None
+def products_kernel(inputs, carried, part, *refs):
+    before = refs[-2] if carried else None
+    blocks = refs[: -2 if carried else -1]
     out = refs[-1]
-    rows = pair_rows(2 * stations)
+    rows = pair_rows(inputs)
     span = SUBLANES
     group = 4
+    last = inputs - group
 
     def load(member, step, low):
         tile = blocks[member // 2][step, member % 2, low * 2 * span : (low + 1) * 2 * span]
         both = tile.astype(F32)
         return both[:span], both[span:]
 
-    for left in range(0, 2 * stations, group):
-        for right in range(left, 2 * stations, group):
+    for left in range(0, inputs, group):
+        for right in range(left, inputs, group):
             a_list = range(left, left + group)
             b_list = range(right, right + group)
             members = [(a, b) for a in a_list for b in b_list if a <= b]
             wanted = [(a, b, comp) for a, b in members for comp in range(2) if a != b or comp == 0]
+            active = part == "all" or (part == "early") == (right < last)
+            known = carried and (part != "late" or right < last or carried == 2)
+            if not (active or known):
+                continue
 
             def body(step, sums):
                 for low in range(blocks[0].shape[2] // (2 * span)):
@@ -296,20 +301,18 @@
                     sums = new
                 return sums
 
-            start = []
+            sums = []
             for a, b, comp in wanted:
                 at = (2 * rows[a, b] + comp) * span
-                if carried:
-                    start.append(before[at : at + span])
-                else:
-                    start.append(jnp.zeros((span, LANES), F32))
-            sums = lax.fori_loop(0, blocks[0].shape[0], body, start)
+                sums.append(before[at : at + span] if known else jnp.zeros((span, LANES), F32))
+            if active:
+                sums = lax.fori_loop(0, blocks[0].shape[0], body, sums)
             sums = dict(zip(wanted, sums))
             for a, b in members:
                 re = sums[a, b, 0]
                 im = sums.get((a, b, 1), jnp.zeros_like(re))
                 at = rows[a, b] * span
-                if fold:
+                if part == "late":
                     low_half = lax.broadcasted_iota(jnp.int32, re.shape, 1) < LANES // 2
                     re = re + pltpu.roll(re, LANES // 2, 1)
                     im = im + pltpu.roll(im, LANES // 2, 1)
@@ -319,23 +322,22 @@
                     out[2 * at + span : 2 * at + 2 * span] = im
 
 
-def products_of(blocks, before, fold):
-    stations = len(blocks)
-    count = len(pair_rows(2 * stations)) * (1 if fold else 2)
-    span = SUBLANES
-    carried = before is not None
-    arrays = list(blocks) + ([before] if carried else [])
+def products_of(blocks, before, part="all", whole=True):
+    inputs = 2 * len(blocks)
+    count = len(pair_rows(inputs)) * (1 if part == "late" else 2)
+    carried = 0 if before is None else 1 + whole
+    used = blocks[:-2] if part == "early" else blocks
+    arrays = list(used) + ([before] if carried else [])
     steps = blocks[0].shape[0] * blocks[0].shape[2] // 8
     return pl.pallas_call(
-        functools.partial(products_kernel, stations, carried, fold),
-        out_shape=jax.ShapeDtypeStruct((count * span, LANES), F32),
+        functools.partial(products_kernel, inputs, carried, part),
+        out_shape=jax.ShapeDtypeStruct((count * SUBLANES, LANES), F32),
         in_specs=[VMEM] * len(arrays),
         out_specs=VMEM,
+        compiler_params=pltpu.CompilerParams(vmem_limit_bytes=12 * 2**20),
         cost_estimate=pl.CostEstimate(
             flops=steps * 4 * 10**6, bytes_accessed=steps * 65536, transcendentals=0
         ),
-        compiler_params=pltpu.CompilerParams(vmem_limit_bytes=12 * 2**20),
-        name="products",
     )(*arrays)
 
 
@@ -433,10 +435,14 @@
             for offset in send_order(stations):
                 route = [(i, i ^ offset) for i in range(stations)]
                 blocks[offset] = lax.ppermute(blocks[offset], "stn", route)
-            if late:
-                newest = products_of(blocks, None, True)
-            else:
-                sums = products_of(blocks, sums, chunk == len(chunks) - 2)
+            if chunk < len(chunks) - 2:
+                sums = products_of(blocks, sums)
+                continue
+            start = None if late else sums
+            early = products_of(blocks, start, "early")
+            newest = products_of(blocks, early, "late", not late)
+            if not late:
+                sums = newest
         other = lax.ppermute(sums, "chan", swap)
         owned = channels // (stations * cores)
         return pl.pallas_call(

time: 147 us -> 140 us (0.952)
  waiting for transfers between devices: 36.9 us -> 30.5 us
    ppermute x28, waiting for transfers between devices: 35.4 us -> 29 us  [shards(): blocks[offset] = lax.ppermute(blocks[offset], 'stn', route)]
    pallas_call x4 -> x6, Pallas kernels: 14.3 us -> 13.7 us  [products_of(): pl.pallas_call(functools.partial(products_kernel, inputs, carried, part),...]
  transfers between devices with their start and end apart: 31 -> 31, of which waited for: 8 -> 6; matrix products, arithmetic and copies ran while one was open for 0% -> 0% of each run, Pallas kernels for 23% -> 24%
where the time goes in v4:
time: 140 us; the launch traced here: 138 us
  starting transfers between devices  65.4 us (47%)
  Pallas kernels  41.7 us (30%)
  waiting for transfers between devices  30.5 us (22%)
    ppermute x28, starting transfers between devices, shards(): blocks[offset] = lax.ppermute(blocks[offset], 'stn', route)  59.1 us
    ppermute x28, waiting for transfers between devices, shards(): blocks[offset] = lax.ppermute(blocks[offset], 'stn', route)  29 us
    pallas_call x4, Pallas kernels, spectra_of(): pl.pallas_call(functools.partial(spectra_kernel, first, count, taps, stat...  26.5 us
    pallas_call x6, Pallas kernels, products_of(): pl.pallas_call(functools.partial(products_kernel, inputs, carried, part),...  13.7 us
    ppermute x1, starting transfers between devices, shards(): other = lax.ppermute(sums, 'chan', swap)  4.9 us
  transfers between devices with their start and end apart: 31, of which 6 were waited for; matrix products, arithmetic and copies ran while one was open for 0% of the time, Pallas kernels for 24%

profile of v4, /device:TPU:1, one launch (start us, length us, event | category | flops | bytes accessed | tf_op | source)
XLA Modules:
  0.0 137.9 jit_solution(8792335837493991163)
XLA Ops:
  0.0 0.0 copy-start.3
  0.0 0.0 copy-start.4
  0.0 7.2 %shard_map.147 = (bf16[8,2,32,128]{3,2,1,0:T(8,128)(2,1)}, bf16[8,2,32,128]{3,2,1,0:T(8,128)(2,1)}, bf16[8,2,32,128]{3,2,1,0:T(8,128)(2,1)}, bf16[8,2,32,128]{3,...) custom-call(bf16[2,8192,128]{2,1,0:T(8,128)(2,1)} %bitcast.10, ...), custom_call_target="tpu_custom_call" | custom-call | flops 256000000 | bytes 2097152 | tf_op jit(solution)/shard_map/pallas_call | solution.py:212
  7.3 2.1 %collective-permute-start.14 = (bf16[8,2,32,128]{3,2,1,0:T(8,128)(2,1)}, bf16[8,2,32,128]{3,2,1,0:T(8,128)(2,1)S(1)}, u32[]{:S(2)}, u32[]{:S(2)}) collective-permute-start(bf16[8,2,32,128]{3,2,1,0:T(8,128)(2,1)} %get-tuple-element.64), channel_id=1, source_target_pairs={{0,2},{2,0},{4,6},{6,4},{8,10},{10,8},{12,14},{14,12},{1,3},{3,1},... | collective-permute-start | bytes 393224 | tf_op jit(solution)/shard_map/ppermute | solution.py:437
  9.4 1.3 collective-permute-start.15
  10.7 0.1 collective-permute-start.16
  10.8 8.0 %shard_map.146 = (bf16[10,2,32,128]{3,2,1,0:T(8,128)(2,1)S(1)}, bf16[10,2,32,128]{3,2,1,0:T(8,128)(2,1)S(1)}, bf16[10,2,32,128]{3,2,1,0:T(8,128)(2,1)S(1)}, bf16...) custom-call(bf16[2,8192,128]{2,1,0:T(8,128)(2,1)S(1)} %bitcast.11, ...), custom_call_target="tpu_custom_call" | custom-call | flops 320000000 | bytes 2621440 | tf_op jit(solution)/shard_map/pallas_call | solution.py:212
  18.8 2.5 %collective-permute-start.10 = (bf16[10,2,32,128]{3,2,1,0:T(8,128)(2,1)S(1)}, bf16[10,2,32,128]{3,2,1,0:T(8,128)(2,1)S(1)}, u32[]{:S(2)}, u32[]{:S(2)}) collective-permute-start(bf16[10,2,32,128]{3,2,1,0:T(8,128)(2,1)S(1)} %get-tuple-element.59), channel_id=1, source_target_pairs={{0,8},{2,10},{4,12},{6,14},{8,0},{10,2},{12,4},{14,6},{1,9},{3,11}... | collective-permute-start | bytes 491528 | tf_op jit(solution)/shard_map/ppermute | solution.py:437
  21.3 0.1 collective-permute-start.17
  21.4 3.2 %collective-permute-start.18 = (bf16[8,2,32,128]{3,2,1,0:T(8,128)(2,1)S(1)}, bf16[8,2,32,128]{3,2,1,0:T(8,128)(2,1)S(1)}, u32[]{:S(2)}, u32[]{:S(2)}) collective-permute-start(bf16[8,2,32,128]{3,2,1,0:T(8,128)(2,1)S(1)} %copy-done.11), channel_id=1, source_target_pairs={{0,10},{2,8},{4,14},{6,12},{8,2},{10,0},{12,6},{14,4},{1,11},{3,9}... | collective-permute-start | bytes 393224 | tf_op jit(solution)/shard_map/ppermute | solution.py:437
  24.6 1.1 collective-permute-start.19
  25.7 2.1 %collective-permute-start.20 = (bf16[8,2,32,128]{3,2,1,0:T(8,128)(2,1)S(1)}, bf16[8,2,32,128]{3,2,1,0:T(8,128)(2,1)S(1)}, u32[]{:S(2)}, u32[]{:S(2)}) collective-permute-start(bf16[8,2,32,128]{3,2,1,0:T(8,128)(2,1)S(1)} %copy-done.9), channel_id=1, source_target_pairs={{0,14},{2,12},{4,10},{6,8},{8,6},{10,4},{12,2},{14,0},{1,15},{3,13... | collective-permute-start | bytes 393224 | tf_op jit(solution)/shard_map/ppermute | solution.py:437
  27.8 14.6 %collective-permute-done.17.refs_4_ = bf16[8,2,32,128]{3,2,1,0:T(8,128)(2,1)S(1)} collective-permute-done((bf16[8,2,32,128]{3,2,1,0:T(8,128)(2,1)S(1)}, bf16[8,2,32,128]{3,2,1,0:T(8,128)(2,1)S(1)}, u32[]{:S(2)}, u32[]{:S(2)}) %collective-permute-start.17) | collective-permute-done | bytes 131104 | tf_op jit(solution)/shard_map/ppermute | solution.py:437
  42.4 0.3 collective-permute-start.11
  42.7 3.5 %collective-permute-done.18.refs_5_ = bf16[8,2,32,128]{3,2,1,0:T(8,128)(2,1)S(1)} collective-permute-done((bf16[8,2,32,128]{3,2,1,0:T(8,128)(2,1)S(1)}, bf16[8,2,32,128]{3,2,1,0:T(8,128)(2,1)S(1)}, u32[]{:S(2)}, u32[]{:S(2)}) %collective-permute-start.18) | collective-permute-done | bytes 131104 | tf_op jit(solution)/shard_map/ppermute | solution.py:437
  46.3 7.7 %collective-permute-start.12 = (bf16[10,2,32,128]{3,2,1,0:T(8,128)(2,1)S(1)}, bf16[10,2,32,128]{3,2,1,0:T(8,128)(2,1)S(1)}, u32[]{:S(2)}, u32[]{:S(2)}) collective-permute-start(bf16[10,2,32,128]{3,2,1,0:T(8,128)(2,1)S(1)} %get-tuple-element.61), channel_id=1, source_target_pairs={{0,12},{2,14},{4,8},{6,10},{8,4},{10,6},{12,0},{14,2},{1,13},{3,15... | collective-permute-start | bytes 491528 | tf_op jit(solution)/shard_map/ppermute | solution.py:437
  54.0 1.2 collective-permute-start.7
  55.2 8.9 %collective-permute-start.8 = (bf16[10,2,32,128]{3,2,1,0:T(8,128)(2,1)S(1)}, bf16[10,2,32,128]{3,2,1,0:T(8,128)(2,1)S(1)}, u32[]{:S(2)}, u32[]{:S(2)}) collective-permute-start(bf16[10,2,32,128]{3,2,1,0:T(8,128)(2,1)S(1)} %get-tuple-element.57), channel_id=1, source_target_pairs={{0,4},{2,6},{4,0},{6,2},{8,12},{10,14},{12,8},{14,10},{1,5},{3,7},... | collective-permute-start | bytes 491528 | tf_op jit(solution)/shard_map/ppermute | solution.py:437
  64.1 7.9 %shard_map.145 = (bf16[10,2,32,128]{3,2,1,0:T(8,128)(2,1)S(1)}, bf16[10,2,32,128]{3,2,1,0:T(8,128)(2,1)S(1)}, bf16[10,2,32,128]{3,2,1,0:T(8,128)(2,1)S(1)}, bf16...) custom-call(bf16[2,8192,128]{2,1,0:T(8,128)(2,1)S(1)} %bitcast.12, ...), custom_call_target="tpu_custom_call" | custom-call | flops 320000000 | bytes 2621440 | tf_op jit(solution)/shard_map/pallas_call | solution.py:212
  72.1 0.1 collective-permute-start.9
  72.2 1.2 collective-permute-start
  73.4 1.3 collective-permute-start.22
  74.7 1.5 %collective-permute-start.1 = (bf16[10,2,32,128]{3,2,1,0:T(8,128)(2,1)S(1)}, bf16[10,2,32,128]{3,2,1,0:T(8,128)(2,1)S(1)}, u32[]{:S(2)}, u32[]{:S(2)}) collective-permute-start(bf16[10,2,32,128]{3,2,1,0:T(8,128)(2,1)S(1)} %get-tuple-element.49), channel_id=1, source_target_pairs={{0,4},{2,6},{4,0},{6,2},{8,12},{10,14},{12,8},{14,10},{1,5},{3,7},... | collective-permute-start | bytes 491528 | tf_op jit(solution)/shard_map/ppermute | solution.py:437
  76.2 0.1 collective-permute-start.2
  76.3 1.1 collective-permute-done.9.refs_3_
  77.3 3.1 %collective-permute-start.3 = (bf16[10,2,32,128]{3,2,1,0:T(8,128)(2,1)S(1)}, bf16[10,2,32,128]{3,2,1,0:T(8,128)(2,1)S(1)}, u32[]{:S(2)}, u32[]{:S(2)}) collective-permute-start(bf16[10,2,32,128]{3,2,1,0:T(8,128)(2,1)S(1)} %get-tuple-element.51), channel_id=1, source_target_pairs={{0,8},{2,10},{4,12},{6,14},{8,0},{10,2},{12,4},{14,6},{1,9},{3,11}... | collective-permute-start | bytes 491528 | tf_op jit(solution)/shard_map/ppermute | solution.py:437
  80.5 6.6 %collective-permute-start.4 = (bf16[10,2,32,128]{3,2,1,0:T(8,128)(2,1)S(1)}, bf16[10,2,32,128]{3,2,1,0:T(8,128)(2,1)S(1)}, u32[]{:S(2)}, u32[]{:S(2)}) collective-permute-start(bf16[10,2,32,128]{3,2,1,0:T(8,128)(2,1)S(1)} %get-tuple-element.52), channel_id=1, source_target_pairs={{0,10},{2,8},{4,14},{6,12},{8,2},{10,0},{12,6},{14,4},{1,11},{3,9}... | collective-permute-start | bytes 491528 | tf_op jit(solution)/shard_map/ppermute | solution.py:437
  87.1 5.1 %collective-permute-start.6 = (bf16[10,2,32,128]{3,2,1,0:T(8,128)(2,1)S(1)}, bf16[10,2,32,128]{3,2,1,0:T(8,128)(2,1)S(1)}, u32[]{:S(2)}, u32[]{:S(2)}) collective-permute-start(bf16[10,2,32,128]{3,2,1,0:T(8,128)(2,1)S(1)} %get-tuple-element.54), channel_id=1, source_target_pairs={{0,14},{2,12},{4,10},{6,8},{8,6},{10,4},{12,2},{14,0},{1,15},{3,13... | collective-permute-start | bytes 491528 | tf_op jit(solution)/shard_map/ppermute | solution.py:437
  92.1 3.1 %shard_map.148.refs_8_ = f32[2176,128]{1,0:T(8,128)S(1)} custom-call(bf16[8,2,32,128]{3,2,1,0:T(8,128)(2,1)S(1)} %copy-done.7, bf16[8,2,32,128]{3,2,1,0:T(8,128)(2,1)S(1)} %collective-permute-done.14.refs_1_, bf16[8,2,32,128]{3,2,1,0:T(8,128)(2,1)S(1)} %collective-permute-done.15.refs_2_, bf16[8,2,32,128]{3,2,1,0:T(8,128)(2,1)S(1)} %collective-permute-done.16.refs_3_, ...), custom_call_target="tpu_custom_call" | custom-call | flops 128000000 | bytes 2097152 | tf_op jit(solution)/shard_map/pallas_call | solution.py:332
  95.2 3.8 %shard_map.149.refs_6_ = f32[2176,128]{1,0:T(8,128)S(1)} custom-call(bf16[10,2,32,128]{3,2,1,0:T(8,128)(2,1)S(1)} %get-tuple-element.55.refs_0_, bf16[10,2,32,128]{3,2,1,0:T(8,128)(2,1)S(1)} %collective-permute-done.7.refs_1_, bf16[10,2,32,128]{3,2,1,0:T(8,128)(2,1)S(1)} %collective-permute-done.8.refs_2_, ...), custom_call_target="tpu_custom_call" | custom-call | flops 160000000 | bytes 2621440 | tf_op jit(solution)/shard_map/pallas_call | solution.py:332
  99.0 5.2 %collective-permute-done.4.refs_5_ = bf16[10,2,32,128]{3,2,1,0:T(8,128)(2,1)S(1)} collective-permute-done((bf16[10,2,32,128]{3,2,1,0:T(8,128)(2,1)S(1)}, bf16[10,2,32,128]{3,2,1,0:T(8,128)(2,1)S(1)}, u32[]{:S(2)}, u32[]{:S(2)}) %collective-permute-start.4) | collective-permute-done | bytes 163872 | tf_op jit(solution)/shard_map/ppermute | solution.py:437
  104.2 2.2 %shard_map.150.refs_8_ = f32[2176,128]{1,0:T(8,128)S(1)} custom-call(bf16[10,2,32,128]{3,2,1,0:T(8,128)(2,1)S(1)} %get-tuple-element.47.refs_0_, bf16[10,2,32,128]{3,2,1,0:T(8,128)(2,1)S(1)} %collective-permute-done.refs_1_, bf16[10,2,32,128]{3,2,1,0:T(8,128)(2,1)S(1)} %collective-permute-done.1.refs_2_, ...), custom_call_target="tpu_custom_call" | custom-call | flops 160000000 | bytes 2621440 | tf_op jit(solution)/shard_map/pallas_call | solution.py:332
  106.4 2.2 %shard_map.151.own = f32[1088,128]{1,0:T(8,128)S(1)} custom-call(bf16[10,2,32,128]{3,2,1,0:T(8,128)(2,1)S(1)} %get-tuple-element.47.refs_0_, bf16[10,2,32,128]{3,2,1,0:T(8,128)(2,1)S(1)} %collective-permute-done.refs_1_, bf16[10,2,32,128]{3,2,1,0:T(8,128)(2,1)S(1)} %collective-permute-done.1.refs_2_, ...), custom_call_target="tpu_custom_call" | custom-call | flops 160000000 | bytes 2621440 | tf_op jit(solution)/shard_map/pallas_call | solution.py:332
  108.7 4.9 %collective-permute-start.21 = (f32[1088,128]{1,0:T(8,128)S(1)}, f32[1088,128]{1,0:T(8,128)S(1)}, u32[]{:S(2)}, u32[]{:S(2)}) collective-permute-start(f32[1088,128]{1,0:T(8,128)S(1)} %shard_map.151.own), channel_id=1, source_target_pairs={{0,1},{1,0},{2,3},{3,2},{4,5},{5,4},{6,7},{7,6},{8,9},{9,8},{10,11... | collective-permute-start | bytes 1671176 | tf_op jit(solution)/shard_map/ppermute | solution.py:446
  113.6 3.4 %shard_map.152 = (bf16[4,2,16,128]{3,2,1,0:T(8,128)(2,1)S(1)}, bf16[4,2,16,128]{3,2,1,0:T(8,128)(2,1)S(1)}, bf16[4,2,16,128]{3,2,1,0:T(8,128)(2,1)S(1)}, bf16[4,...) custom-call(bf16[2,8192,128]{2,1,0:T(8,128)(2,1)S(1)} %bitcast.13, ...), custom_call_target="tpu_custom_call" | custom-call | flops 128000000 | bytes 1048576 | tf_op jit(solution)/shard_map/pallas_call | solution.py:212
  117.0 0.1 collective-permute-start.23
  117.1 1.5 %collective-permute-done.23.refs_8_ = bf16[8,4,2,16,128]{4,3,2,1,0:T(8,128)(2,1)S(1)} collective-permute-done((bf16[8,4,2,16,128]{4,3,2,1,0:T(8,128)(2,1)S(1)}, bf16[8,4,2,16,128]{4,3,2,1,0:T(8,128)(2,1)S(1)}, u32[]{:S(2)}, u32[]{:S(2)}) %collective-permute-start.23) | collective-permute-done | bytes 262176 | tf_op jit(solution)/shard_map/ppermute | solution.py:433
  118.6 0.1 collective-permute-start.24
  118.7 3.2 %collective-permute-start.25 = (bf16[8,2,16,128]{3,2,1,0:T(8,128)(2,1)S(1)}, bf16[8,2,16,128]{3,2,1,0:T(8,128)(2,1)S(1)}, u32[]{:S(2)}, u32[]{:S(2)}) collective-permute-start(bf16[8,2,16,128]{3,2,1,0:T(8,128)(2,1)S(1)} %get-tuple-element.83), channel_id=1, source_target_pairs={{0,4},{2,6},{4,0},{6,2},{8,12},{10,14},{12,8},{14,10},{1,5},{3,7},... | collective-permute-start | bytes 196616 | tf_op jit(solution)/shard_map/ppermute | solution.py:437
  121.9 1.0 collective-permute-start.26
  122.9 0.6 collective-permute-start.27
  123.6 1.7 %collective-permute-start.28 = (bf16[8,2,16,128]{3,2,1,0:T(8,128)(2,1)S(1)}, bf16[8,2,16,128]{3,2,1,0:T(8,128)(2,1)S(1)}, u32[]{:S(2)}, u32[]{:S(2)}) collective-permute-start(bf16[8,2,16,128]{3,2,1,0:T(8,128)(2,1)S(1)} %get-tuple-element.86), channel_id=1, source_target_pairs={{0,10},{2,8},{4,14},{6,12},{8,2},{10,0},{12,6},{14,4},{1,11},{3,9}... | collective-permute-start | bytes 196616 | tf_op jit(solution)/shard_map/ppermute | solution.py:437
  125.3 1.9 %collective-permute-start.29 = (bf16[8,2,16,128]{3,2,1,0:T(8,128)(2,1)S(1)}, bf16[8,2,16,128]{3,2,1,0:T(8,128)(2,1)S(1)}, u32[]{:S(2)}, u32[]{:S(2)}) collective-permute-start(bf16[8,2,16,128]{3,2,1,0:T(8,128)(2,1)S(1)} %get-tuple-element.87), channel_id=1, source_target_pairs={{0,12},{2,14},{4,8},{6,10},{8,4},{10,6},{12,0},{14,2},{1,13},{3,15... | collective-permute-start | bytes 196616 | tf_op jit(solution)/shard_map/ppermute | solution.py:437
  127.3 2.2 %collective-permute-start.30 = (bf16[8,2,16,128]{3,2,1,0:T(8,128)(2,1)S(1)}, bf16[8,2,16,128]{3,2,1,0:T(8,128)(2,1)S(1)}, u32[]{:S(2)}, u32[]{:S(2)}) collective-permute-start(bf16[8,2,16,128]{3,2,1,0:T(8,128)(2,1)S(1)} %get-tuple-element.88), channel_id=1, source_target_pairs={{0,14},{2,12},{4,10},{6,8},{8,6},{10,4},{12,2},{14,0},{1,15},{3,13... | collective-permute-start | bytes 196616 | tf_op jit(solution)/shard_map/ppermute | solution.py:437
  129.5 4.5 %collective-permute-done.28.refs_5_ = bf16[8,2,16,128]{3,2,1,0:T(8,128)(2,1)S(1)} collective-permute-done((bf16[8,2,16,128]{3,2,1,0:T(8,128)(2,1)S(1)}, bf16[8,2,16,128]{3,2,1,0:T(8,128)(2,1)S(1)}, u32[]{:S(2)}, u32[]{:S(2)}) %collective-permute-start.28) | collective-permute-done | bytes 65568 | tf_op jit(solution)/shard_map/ppermute | solution.py:437
  134.0 1.1 shard_map.153.refs_8_
  135.1 1.4 %shard_map.154.late = f32[1088,128]{1,0:T(8,128)S(1)} custom-call(bf16[8,2,16,128]{3,2,1,0:T(8,128)(2,1)S(1)} %get-tuple-element.81.refs_0_, bf16[8,2,16,128]{3,2,1,0:T(8,128)(2,1)S(1)} %collective-permute-done.24.refs_1_, bf16[8,2,16,128]{3,2,1,0:T(8,128)(2,1)S(1)} %collective-permute-done.25.refs_2_, ...), custom_call_target="tpu_custom_call" | custom-call | flops 64000000 | bytes 1048576 | tf_op jit(solution)/shard_map/pallas_call | solution.py:332
  136.5 1.4 %visibility.1 = f32[2,256,256]{2,1,0:T(8,128)} custom-call(f32[1088,128]{1,0:T(8,128)S(1)} %shard_map.151.own, f32[1088,128]{1,0:T(8,128)S(1)} %collective-permute-done.21.other, f32[1088,128]{1,0:T(8,128)S(1)} %shard_map.154.late), custom_call_target="tpu_custom_call" | custom-call | tf_op jit(solution)/shard_map/visibility/pallas_call | solution.py:448
  (52 shorter events, 0.2 us)
Async XLA Ops:
  0.0 10.8 %copy-start = (bf16[2,2,524288]{2,1,0:T(2,128)(2,1)S(1)}, bf16[2,2,524288]{2,1,0:T(2,128)(2,1)}, u32[]{:S(2)}) copy-start(bf16[2,2,524288]{2,1,0:T(2,128)(2,1)} %param.15) | copy-start | bytes 12582916
  0.0 10.8 %copy-start.1 = (bf16[2,2,61440]{2,1,0:T(2,128)(2,1)S(1)}, bf16[2,2,61440]{2,1,0:T(2,128)(2,1)}, u32[]{:S(2)}) copy-start(bf16[2,2,61440]{2,1,0:T(2,128)(2,1)} %param.16) | copy-start | bytes 1474564
  0.0 10.8 %copy-start.2 = (f32[16,4096]{1,0:T(8,128)S(1)}, f32[16,4096]{1,0:T(8,128)}, u32[]{:S(2)}) copy-start(f32[16,4096]{1,0:T(8,128)} %refs_3_.7) | copy-start | bytes 786436
  0.0 10.8 %copy-start.3 = (bf16[256,256]{1,0:T(8,128)(2,1)S(1)}, bf16[256,256]{1,0:T(8,128)(2,1)}, u32[]{:S(2)}) copy-start(bf16[256,256]{1,0:T(8,128)(2,1)} %constant.8.clone.refs_4_) | copy-start | bytes 393220
  0.0 10.8 %copy-start.4 = (bf16[256,256]{1,0:T(8,128)(2,1)S(1)}, bf16[256,256]{1,0:T(8,128)(2,1)}, u32[]{:S(2)}) copy-start(bf16[256,256]{1,0:T(8,128)(2,1)} %constant.10.clone.refs_6_) | copy-start | bytes 393220
  0.0 10.8 %copy-start.5 = (f32[2,64,128]{2,1,0:T(8,128)S(1)}, f32[2,64,128]{2,1,0:T(8,128)}, u32[]{:S(2)}) copy-start(f32[2,64,128]{2,1,0:T(8,128)} %constant.9.clone.refs_5_) | copy-start | bytes 196612
  7.3 14.1 %collective-permute-start.14 = (bf16[8,2,32,128]{3,2,1,0:T(8,128)(2,1)}, bf16[8,2,32,128]{3,2,1,0:T(8,128)(2,1)S(1)}, u32[]{:S(2)}, u32[]{:S(2)}) collective-permute-start(bf16[8,2,32,128]{3,2,1,0:T(8,128)(2,1)} %get-tuple-element.64), channel_id=1, source_target_pairs={{0,2},{2,0},{4,6},{6,4},{8,10},{10,8},{12,14},{14,12},{1,3},{3,1},... | collective-permute-start | bytes 393224 | tf_op jit(solution)/shard_map/ppermute | solution.py:437
  9.4 15.2 %collective-permute-start.15 = (bf16[8,2,32,128]{3,2,1,0:T(8,128)(2,1)}, bf16[8,2,32,128]{3,2,1,0:T(8,128)(2,1)S(1)}, u32[]{:S(2)}, u32[]{:S(2)}) collective-permute-start(bf16[8,2,32,128]{3,2,1,0:T(8,128)(2,1)} %get-tuple-element.65), channel_id=1, source_target_pairs={{0,4},{2,6},{4,0},{6,2},{8,12},{10,14},{12,8},{14,10},{1,5},{3,7},... | collective-permute-start | bytes 393224 | tf_op jit(solution)/shard_map/ppermute | solution.py:437
  10.7 10.6 %copy-start.12 = (bf16[8,2,32,128]{3,2,1,0:T(8,128)(2,1)S(1)}, bf16[8,2,32,128]{3,2,1,0:T(8,128)(2,1)}, u32[]{:S(2)}) copy-start(bf16[8,2,32,128]{3,2,1,0:T(8,128)(2,1)} %get-tuple-element.67) | copy-start | bytes 393220
  10.7 10.7 %copy-start.11 = (bf16[8,2,32,128]{3,2,1,0:T(8,128)(2,1)S(1)}, bf16[8,2,32,128]{3,2,1,0:T(8,128)(2,1)}, u32[]{:S(2)}) copy-start(bf16[8,2,32,128]{3,2,1,0:T(8,128)(2,1)} %get-tuple-element.68) | copy-start | bytes 393220
  10.7 13.9 %copy-start.10 = (bf16[8,2,32,128]{3,2,1,0:T(8,128)(2,1)S(1)}, bf16[8,2,32,128]{3,2,1,0:T(8,128)(2,1)}, u32[]{:S(2)}) copy-start(bf16[8,2,32,128]{3,2,1,0:T(8,128)(2,1)} %get-tuple-element.69) | copy-start | bytes 393220
  10.7 15.0 %copy-start.9 = (bf16[8,2,32,128]{3,2,1,0:T(8,128)(2,1)S(1)}, bf16[8,2,32,128]{3,2,1,0:T(8,128)(2,1)}, u32[]{:S(2)}) copy-start(bf16[8,2,32,128]{3,2,1,0:T(8,128)(2,1)} %get-tuple-element.70) | copy-start | bytes 393220
  10.7 15.0 %collective-permute-start.16 = (bf16[8,2,32,128]{3,2,1,0:T(8,128)(2,1)}, bf16[8,2,32,128]{3,2,1,0:T(8,128)(2,1)S(1)}, u32[]{:S(2)}, u32[]{:S(2)}) collective-permute-start(bf16[8,2,32,128]{3,2,1,0:T(8,128)(2,1)} %get-tuple-element.66), channel_id=1, source_target_pairs={{0,6},{2,4},{4,2},{6,0},{8,14},{10,12},{12,10},{14,8},{1,7},{3,5},... | collective-permute-start | bytes 393224 | tf_op jit(solution)/shard_map/ppermute | solution.py:437
  18.8 36.4 %collective-permute-start.10 = (bf16[10,2,32,128]{3,2,1,0:T(8,128)(2,1)S(1)}, bf16[10,2,32,128]{3,2,1,0:T(8,128)(2,1)S(1)}, u32[]{:S(2)}, u32[]{:S(2)}) collective-permute-start(bf16[10,2,32,128]{3,2,1,0:T(8,128)(2,1)S(1)} %get-tuple-element.59), channel_id=1, source_target_pairs={{0,8},{2,10},{4,12},{6,14},{8,0},{10,2},{12,4},{14,6},{1,9},{3,11}... | collective-permute-start | bytes 491528 | tf_op jit(solution)/shard_map/ppermute | solution.py:437
  21.3 21.1 %collective-permute-start.17 = (bf16[8,2,32,128]{3,2,1,0:T(8,128)(2,1)S(1)}, bf16[8,2,32,128]{3,2,1,0:T(8,128)(2,1)S(1)}, u32[]{:S(2)}, u32[]{:S(2)}) collective-permute-start(bf16[8,2,32,128]{3,2,1,0:T(8,128)(2,1)S(1)} %copy-done.12), channel_id=1, source_target_pairs={{0,8},{2,10},{4,12},{6,14},{8,0},{10,2},{12,4},{14,6},{1,9},{3,11}... | collective-permute-start | bytes 393224 | tf_op jit(solution)/shard_map/ppermute | solution.py:437
  21.4 24.9 %collective-permute-start.18 = (bf16[8,2,32,128]{3,2,1,0:T(8,128)(2,1)S(1)}, bf16[8,2,32,128]{3,2,1,0:T(8,128)(2,1)S(1)}, u32[]{:S(2)}, u32[]{:S(2)}) collective-permute-start(bf16[8,2,32,128]{3,2,1,0:T(8,128)(2,1)S(1)} %copy-done.11), channel_id=1, source_target_pairs={{0,10},{2,8},{4,14},{6,12},{8,2},{10,0},{12,6},{14,4},{1,11},{3,9}... | collective-permute-start | bytes 393224 | tf_op jit(solution)/shard_map/ppermute | solution.py:437
  24.6 29.4 %collective-permute-start.19 = (bf16[8,2,32,128]{3,2,1,0:T(8,128)(2,1)S(1)}, bf16[8,2,32,128]{3,2,1,0:T(8,128)(2,1)S(1)}, u32[]{:S(2)}, u32[]{:S(2)}) collective-permute-start(bf16[8,2,32,128]{3,2,1,0:T(8,128)(2,1)S(1)} %copy-done.10), channel_id=1, source_target_pairs={{0,12},{2,14},{4,8},{6,10},{8,4},{10,6},{12,0},{14,2},{1,13},{3,15... | collective-permute-start | bytes 393224 | tf_op jit(solution)/shard_map/ppermute | solution.py:437
  25.7 28.3 %collective-permute-start.20 = (bf16[8,2,32,128]{3,2,1,0:T(8,128)(2,1)S(1)}, bf16[8,2,32,128]{3,2,1,0:T(8,128)(2,1)S(1)}, u32[]{:S(2)}, u32[]{:S(2)}) collective-permute-start(bf16[8,2,32,128]{3,2,1,0:T(8,128)(2,1)S(1)} %copy-done.9), channel_id=1, source_target_pairs={{0,14},{2,12},{4,10},{6,8},{8,6},{10,4},{12,2},{14,0},{1,15},{3,13... | collective-permute-start | bytes 393224 | tf_op jit(solution)/shard_map/ppermute | solution.py:437
  42.4 29.7 %collective-permute-start.11 = (bf16[10,2,32,128]{3,2,1,0:T(8,128)(2,1)S(1)}, bf16[10,2,32,128]{3,2,1,0:T(8,128)(2,1)S(1)}, u32[]{:S(2)}, u32[]{:S(2)}) collective-permute-start(bf16[10,2,32,128]{3,2,1,0:T(8,128)(2,1)S(1)} %get-tuple-element.60), channel_id=1, source_target_pairs={{0,10},{2,8},{4,14},{6,12},{8,2},{10,0},{12,6},{14,4},{1,11},{3,9}... | collective-permute-start | bytes 491528 | tf_op jit(solution)/shard_map/ppermute | solution.py:437
  46.3 25.9 %collective-permute-start.12 = (bf16[10,2,32,128]{3,2,1,0:T(8,128)(2,1)S(1)}, bf16[10,2,32,128]{3,2,1,0:T(8,128)(2,1)S(1)}, u32[]{:S(2)}, u32[]{:S(2)}) collective-permute-start(bf16[10,2,32,128]{3,2,1,0:T(8,128)(2,1)S(1)} %get-tuple-element.61), channel_id=1, source_target_pairs={{0,12},{2,14},{4,8},{6,10},{8,4},{10,6},{12,0},{14,2},{1,13},{3,15... | collective-permute-start | bytes 491528 | tf_op jit(solution)/shard_map/ppermute | solution.py:437
  54.0 19.4 %collective-permute-start.13 = (bf16[10,2,32,128]{3,2,1,0:T(8,128)(2,1)S(1)}, bf16[10,2,32,128]{3,2,1,0:T(8,128)(2,1)S(1)}, u32[]{:S(2)}, u32[]{:S(2)}) collective-permute-start(bf16[10,2,32,128]{3,2,1,0:T(8,128)(2,1)S(1)} %get-tuple-element.62), channel_id=1, source_target_pairs={{0,14},{2,12},{4,10},{6,8},{8,6},{10,4},{12,2},{14,0},{1,15},{3,13... | collective-permute-start | bytes 491528 | tf_op jit(solution)/shard_map/ppermute | solution.py:437
  54.0 20.6 %collective-permute-start.7 = (bf16[10,2,32,128]{3,2,1,0:T(8,128)(2,1)S(1)}, bf16[10,2,32,128]{3,2,1,0:T(8,128)(2,1)S(1)}, u32[]{:S(2)}, u32[]{:S(2)}) collective-permute-start(bf16[10,2,32,128]{3,2,1,0:T(8,128)(2,1)S(1)} %get-tuple-element.56), channel_id=1, source_target_pairs={{0,2},{2,0},{4,6},{6,4},{8,10},{10,8},{12,14},{14,12},{1,3},{3,1},... | collective-permute-start | bytes 491528 | tf_op jit(solution)/shard_map/ppermute | solution.py:437
  55.2 18.2 %copy-start.8 = (bf16[2,960,128]{2,1,0:T(8,128)(2,1)S(1)}, bf16[2,960,128]{2,1,0:T(8,128)(2,1)}, u32[]{:S(2)}) copy-start(bf16[2,960,128]{2,1,0:T(8,128)(2,1)} %get-tuple-element.71) | copy-start | bytes 1474564
  55.2 36.9 %copy-start.7 = (bf16[8,2,32,128]{3,2,1,0:T(8,128)(2,1)S(1)}, bf16[8,2,32,128]{3,2,1,0:T(8,128)(2,1)}, u32[]{:S(2)}) copy-start(bf16[8,2,32,128]{3,2,1,0:T(8,128)(2,1)} %get-tuple-element.63.refs_0_) | copy-start | bytes 393220
  55.2 21.0 %collective-permute-start.8 = (bf16[10,2,32,128]{3,2,1,0:T(8,128)(2,1)S(1)}, bf16[10,2,32,128]{3,2,1,0:T(8,128)(2,1)S(1)}, u32[]{:S(2)}, u32[]{:S(2)}) collective-permute-start(bf16[10,2,32,128]{3,2,1,0:T(8,128)(2,1)S(1)} %get-tuple-element.57), channel_id=1, source_target_pairs={{0,4},{2,6},{4,0},{6,2},{8,12},{10,14},{12,8},{14,10},{1,5},{3,7},... | collective-permute-start | bytes 491528 | tf_op jit(solution)/shard_map/ppermute | solution.py:437
  72.1 5.2 %collective-permute-start.9 = (bf16[10,2,32,128]{3,2,1,0:T(8,128)(2,1)S(1)}, bf16[10,2,32,128]{3,2,1,0:T(8,128)(2,1)S(1)}, u32[]{:S(2)}, u32[]{:S(2)}) collective-permute-start(bf16[10,2,32,128]{3,2,1,0:T(8,128)(2,1)S(1)} %get-tuple-element.58), channel_id=1, source_target_pairs={{0,6},{2,4},{4,2},{6,0},{8,14},{10,12},{12,10},{14,8},{1,7},{3,5},... | collective-permute-start | bytes 491528 | tf_op jit(solution)/shard_map/ppermute | solution.py:437
  72.2 8.3 %collective-permute-start = (bf16[10,2,32,128]{3,2,1,0:T(8,128)(2,1)S(1)}, bf16[10,2,32,128]{3,2,1,0:T(8,128)(2,1)S(1)}, u32[]{:S(2)}, u32[]{:S(2)}) collective-permute-start(bf16[10,2,32,128]{3,2,1,0:T(8,128)(2,1)S(1)} %get-tuple-element.48), channel_id=1, source_target_pairs={{0,2},{2,0},{4,6},{6,4},{8,10},{10,8},{12,14},{14,12},{1,3},{3,1},... | collective-permute-start | bytes 491528 | tf_op jit(solution)/shard_map/ppermute | solution.py:437
  73.4 40.2 %collective-permute-start.22 = (bf16[2,960,128]{2,1,0:T(8,128)(2,1)S(1)}, bf16[2,960,128]{2,1,0:T(8,128)(2,1)S(1)}, u32[]{:S(2)}, u32[]{:S(2)}) collective-permute-start(bf16[2,960,128]{2,1,0:T(8,128)(2,1)S(1)} %copy-done.8), channel_id=1, source_target_pairs={{0,1},{2,3},{4,5},{6,7},{8,9},{10,11},{12,13},{14,15},{16,17},{18,... | collective-permute-start | bytes 1474568 | tf_op jit(solution)/shard_map/ppermute | solution.py:425
  74.7 12.4 %collective-permute-start.1 = (bf16[10,2,32,128]{3,2,1,0:T(8,128)(2,1)S(1)}, bf16[10,2,32,128]{3,2,1,0:T(8,128)(2,1)S(1)}, u32[]{:S(2)}, u32[]{:S(2)}) collective-permute-start(bf16[10,2,32,128]{3,2,1,0:T(8,128)(2,1)S(1)} %get-tuple-element.49), channel_id=1, source_target_pairs={{0,4},{2,6},{4,0},{6,2},{8,12},{10,14},{12,8},{14,10},{1,5},{3,7},... | collective-permute-start | bytes 491528 | tf_op jit(solution)/shard_map/ppermute | solution.py:437
  76.2 10.9 %collective-permute-start.2 = (bf16[10,2,32,128]{3,2,1,0:T(8,128)(2,1)S(1)}, bf16[10,2,32,128]{3,2,1,0:T(8,128)(2,1)S(1)}, u32[]{:S(2)}, u32[]{:S(2)}) collective-permute-start(bf16[10,2,32,128]{3,2,1,0:T(8,128)(2,1)S(1)} %get-tuple-element.50), channel_id=1, source_target_pairs={{0,6},{2,4},{4,2},{6,0},{8,14},{10,12},{12,10},{14,8},{1,7},{3,5},... | collective-permute-start | bytes 491528 | tf_op jit(solution)/shard_map/ppermute | solution.py:437
  77.3 21.7 %collective-permute-start.3 = (bf16[10,2,32,128]{3,2,1,0:T(8,128)(2,1)S(1)}, bf16[10,2,32,128]{3,2,1,0:T(8,128)(2,1)S(1)}, u32[]{:S(2)}, u32[]{:S(2)}) collective-permute-start(bf16[10,2,32,128]{3,2,1,0:T(8,128)(2,1)S(1)} %get-tuple-element.51), channel_id=1, source_target_pairs={{0,8},{2,10},{4,12},{6,14},{8,0},{10,2},{12,4},{14,6},{1,9},{3,11}... | collective-permute-start | bytes 491528 | tf_op jit(solution)/shard_map/ppermute | solution.py:437
  80.5 23.8 %collective-permute-start.4 = (bf16[10,2,32,128]{3,2,1,0:T(8,128)(2,1)S(1)}, bf16[10,2,32,128]{3,2,1,0:T(8,128)(2,1)S(1)}, u32[]{:S(2)}, u32[]{:S(2)}) collective-permute-start(bf16[10,2,32,128]{3,2,1,0:T(8,128)(2,1)S(1)} %get-tuple-element.52), channel_id=1, source_target_pairs={{0,10},{2,8},{4,14},{6,12},{8,2},{10,0},{12,6},{14,4},{1,11},{3,9}... | collective-permute-start | bytes 491528 | tf_op jit(solution)/shard_map/ppermute | solution.py:437
  87.1 19.3 %collective-permute-start.5 = (bf16[10,2,32,128]{3,2,1,0:T(8,128)(2,1)S(1)}, bf16[10,2,32,128]{3,2,1,0:T(8,128)(2,1)S(1)}, u32[]{:S(2)}, u32[]{:S(2)}) collective-permute-start(bf16[10,2,32,128]{3,2,1,0:T(8,128)(2,1)S(1)} %get-tuple-element.53), channel_id=1, source_target_pairs={{0,12},{2,14},{4,8},{6,10},{8,4},{10,6},{12,0},{14,2},{1,13},{3,15... | collective-permute-start | bytes 491528 | tf_op jit(solution)/shard_map/ppermute | solution.py:437
  87.1 19.3 %collective-permute-start.6 = (bf16[10,2,32,128]{3,2,1,0:T(8,128)(2,1)S(1)}, bf16[10,2,32,128]{3,2,1,0:T(8,128)(2,1)S(1)}, u32[]{:S(2)}, u32[]{:S(2)}) collective-permute-start(bf16[10,2,32,128]{3,2,1,0:T(8,128)(2,1)S(1)} %get-tuple-element.54), channel_id=1, source_target_pairs={{0,14},{2,12},{4,10},{6,8},{8,6},{10,4},{12,2},{14,0},{1,15},{3,13... | collective-permute-start | bytes 491528 | tf_op jit(solution)/shard_map/ppermute | solution.py:437
  106.4 7.2 %copy-start.6 = (bf16[256,256]{1,0:T(8,128)(2,1)S(1)}, bf16[256,256]{1,0:T(8,128)(2,1)}, u32[]{:S(2)}) copy-start(bf16[256,256]{1,0:T(8,128)(2,1)} %constant.11.clone.refs_6_) | copy-start | bytes 393220
  108.7 27.8 %collective-permute-start.21 = (f32[1088,128]{1,0:T(8,128)S(1)}, f32[1088,128]{1,0:T(8,128)S(1)}, u32[]{:S(2)}, u32[]{:S(2)}) collective-permute-start(f32[1088,128]{1,0:T(8,128)S(1)} %shard_map.151.own), channel_id=1, source_target_pairs={{0,1},{1,0},{2,3},{3,2},{4,5},{5,4},{6,7},{7,6},{8,9},{9,8},{10,11... | collective-permute-start | bytes 1671176 | tf_op jit(solution)/shard_map/ppermute | solution.py:446
  117.0 1.6 %collective-permute-start.23 = (bf16[8,4,2,16,128]{4,3,2,1,0:T(8,128)(2,1)S(1)}, bf16[8,4,2,16,128]{4,3,2,1,0:T(8,128)(2,1)S(1)}, u32[]{:S(2)}, u32[]{:S(2)}) collective-permute-start(bf16[8,4,2,16,128]{4,3,2,1,0:T(8,128)(2,1)S(1)} %get-tuple-element.80), channel_id=1, source_target_pairs={{0,1},{1,0},{2,3},{3,2},{4,5},{5,4},{6,7},{7,6},{8,9},{9,8},{10,11... | collective-permute-start | bytes 786440 | tf_op jit(solution)/shard_map/ppermute | solution.py:433
  118.6 4.9 %collective-permute-start.24 = (bf16[8,2,16,128]{3,2,1,0:T(8,128)(2,1)S(1)}, bf16[8,2,16,128]{3,2,1,0:T(8,128)(2,1)S(1)}, u32[]{:S(2)}, u32[]{:S(2)}) collective-permute-start(bf16[8,2,16,128]{3,2,1,0:T(8,128)(2,1)S(1)} %get-tuple-element.82), channel_id=1, source_target_pairs={{0,2},{2,0},{4,6},{6,4},{8,10},{10,8},{12,14},{14,12},{1,3},{3,1},... | collective-permute-start | bytes 196616 | tf_op jit(solution)/shard_map/ppermute | solution.py:437
  118.7 6.6 %collective-permute-start.25 = (bf16[8,2,16,128]{3,2,1,0:T(8,128)(2,1)S(1)}, bf16[8,2,16,128]{3,2,1,0:T(8,128)(2,1)S(1)}, u32[]{:S(2)}, u32[]{:S(2)}) collective-permute-start(bf16[8,2,16,128]{3,2,1,0:T(8,128)(2,1)S(1)} %get-tuple-element.83), channel_id=1, source_target_pairs={{0,4},{2,6},{4,0},{6,2},{8,12},{10,14},{12,8},{14,10},{1,5},{3,7},... | collective-permute-start | bytes 196616 | tf_op jit(solution)/shard_map/ppermute | solution.py:437
  121.9 5.3 %collective-permute-start.26 = (bf16[8,2,16,128]{3,2,1,0:T(8,128)(2,1)S(1)}, bf16[8,2,16,128]{3,2,1,0:T(8,128)(2,1)S(1)}, u32[]{:S(2)}, u32[]{:S(2)}) collective-permute-start(bf16[8,2,16,128]{3,2,1,0:T(8,128)(2,1)S(1)} %get-tuple-element.84), channel_id=1, source_target_pairs={{0,6},{2,4},{4,2},{6,0},{8,14},{10,12},{12,10},{14,8},{1,7},{3,5},... | collective-permute-start | bytes 196616 | tf_op jit(solution)/shard_map/ppermute | solution.py:437
  122.9 6.5 %collective-permute-start.27 = (bf16[8,2,16,128]{3,2,1,0:T(8,128)(2,1)S(1)}, bf16[8,2,16,128]{3,2,1,0:T(8,128)(2,1)S(1)}, u32[]{:S(2)}, u32[]{:S(2)}) collective-permute-start(bf16[8,2,16,128]{3,2,1,0:T(8,128)(2,1)S(1)} %get-tuple-element.85), channel_id=1, source_target_pairs={{0,8},{2,10},{4,12},{6,14},{8,0},{10,2},{12,4},{14,6},{1,9},{3,11}... | collective-permute-start | bytes 196616 | tf_op jit(solution)/shard_map/ppermute | solution.py:437
  123.6 10.4 %collective-permute-start.28 = (bf16[8,2,16,128]{3,2,1,0:T(8,128)(2,1)S(1)}, bf16[8,2,16,128]{3,2,1,0:T(8,128)(2,1)S(1)}, u32[]{:S(2)}, u32[]{:S(2)}) collective-permute-start(bf16[8,2,16,128]{3,2,1,0:T(8,128)(2,1)S(1)} %get-tuple-element.86), channel_id=1, source_target_pairs={{0,10},{2,8},{4,14},{6,12},{8,2},{10,0},{12,6},{14,4},{1,11},{3,9}... | collective-permute-start | bytes 196616 | tf_op jit(solution)/shard_map/ppermute | solution.py:437
  125.3 9.7 %collective-permute-start.29 = (bf16[8,2,16,128]{3,2,1,0:T(8,128)(2,1)S(1)}, bf16[8,2,16,128]{3,2,1,0:T(8,128)(2,1)S(1)}, u32[]{:S(2)}, u32[]{:S(2)}) collective-permute-start(bf16[8,2,16,128]{3,2,1,0:T(8,128)(2,1)S(1)} %get-tuple-element.87), channel_id=1, source_target_pairs={{0,12},{2,14},{4,8},{6,10},{8,4},{10,6},{12,0},{14,2},{1,13},{3,15... | collective-permute-start | bytes 196616 | tf_op jit(solution)/shard_map/ppermute | solution.py:437
  127.3 7.8 %collective-permute-start.30 = (bf16[8,2,16,128]{3,2,1,0:T(8,128)(2,1)S(1)}, bf16[8,2,16,128]{3,2,1,0:T(8,128)(2,1)S(1)}, u32[]{:S(2)}, u32[]{:S(2)}) collective-permute-start(bf16[8,2,16,128]{3,2,1,0:T(8,128)(2,1)S(1)} %get-tuple-element.88), channel_id=1, source_target_pairs={{0,14},{2,12},{4,10},{6,8},{8,6},{10,4},{12,2},{14,0},{1,15},{3,13... | collective-permute-start | bytes 196616 | tf_op jit(solution)/shard_map/ppermute | solution.py:437

commit v5 on v4

--- a/solution.py
+++ b/solution.py
@@ -117,13 +117,19 @@
         )
         tail_copy.start()
 
-    def widen(frame, carry):
-        at = pl.multiple_of(frame * per, per)
+    def widen(start, rows):
         for comp in range(2):
-            wide[comp, pl.ds(at, per)] = frames[comp, pl.ds(at, per)].astype(F32)
+            wide[comp, pl.ds(start, rows)] = frames[comp, pl.ds(start, rows)].astype(F32)
+
+    rows = 5 * per
+
+    def widen_rows(index, carry):
+        widen(pl.multiple_of(index * rows, per), rows)
         return carry
 
-    lax.fori_loop(0, total // per, widen, 0)
+    lax.fori_loop(0, total // rows, widen_rows, 0)
+    if total % rows:
+        widen(total - total % rows, total % rows)
 
     def strip(index, carry):
         comp = index // (per // 16)
@@ -191,7 +197,7 @@
                     tail[offset, index, member] = spectra[row : row + block, lane : lane + LANES]
         return carry
 
-    lax.fori_loop(0, count // 4, transform, 0, unroll=2 if count % 16 else 4)
+    lax.fori_loop(0, count // 4, transform, 0, unroll=5 if count % 40 == 0 else 2 if count % 16 else 8 if count % 32 == 0 else 4)
     if last:
         tail_copy.wait()
 
@@ -306,7 +312,7 @@
                 at = (2 * rows[a, b] + comp) * span
                 sums.append(before[at : at + span] if known else jnp.zeros((span, LANES), F32))
             if active:
-                sums = lax.fori_loop(0, blocks[0].shape[0], body, sums)
+                sums = lax.fori_loop(0, blocks[0].shape[0], body, sums, unroll=2)
             sums = dict(zip(wanted, sums))
             for a, b in members:
                 re = sums[a, b, 0]

time: 140 us -> 136 us (0.971)
  Pallas kernels: 41.7 us -> 37.2 us
  starting transfers between devices: 65.4 us -> 67 us
    pallas_call x4, Pallas kernels: 26.5 us -> 23.2 us  [spectra_of(): pl.pallas_call(functools.partial(spectra_kernel, first, count, taps, stat...]
  transfers between devices with their start and end apart: 31 -> 31, of which waited for: 6 -> 7; matrix products, arithmetic and copies ran while one was open for 0% -> 0% of each run, Pallas kernels for 24% -> 22%
where the time goes in v5:
time: 136 us; the launch traced here: 134 us
  starting transfers between devices  67 us (49%)
  Pallas kernels  37.2 us (27%)
  waiting for transfers between devices  29.3 us (22%)
    ppermute x28, starting transfers between devices, shards(): blocks[offset] = lax.ppermute(blocks[offset], 'stn', route)  60.1 us
    ppermute x28, waiting for transfers between devices, shards(): blocks[offset] = lax.ppermute(blocks[offset], 'stn', route)  27.8 us
    pallas_call x4, Pallas kernels, spectra_of(): pl.pallas_call(functools.partial(spectra_kernel, first, count, taps, stat...  23.2 us
    pallas_call x6, Pallas kernels, products_of(): pl.pallas_call(functools.partial(products_kernel, inputs, carried, part),...  12.5 us
    ppermute x1, starting transfers between devices, shards(): other = lax.ppermute(sums, 'chan', swap)  5.49 us
  transfers between devices with their start and end apart: 31, of which 7 were waited for; matrix products, arithmetic and copies ran while one was open for 0% of the time, Pallas kernels for 22%

profile of v5, /device:TPU:1, one launch (start us, length us, event | category | flops | bytes accessed | tf_op | source)
XLA Modules:
  0.0 133.8 jit_solution(334510668398249150)
XLA Ops:
  0.0 6.6 %shard_map.147 = (bf16[8,2,32,128]{3,2,1,0:T(8,128)(2,1)}, bf16[8,2,32,128]{3,2,1,0:T(8,128)(2,1)}, bf16[8,2,32,128]{3,2,1,0:T(8,128)(2,1)}, bf16[8,2,32,128]{3,...) custom-call(bf16[2,8192,128]{2,1,0:T(8,128)(2,1)} %bitcast.10, ...), custom_call_target="tpu_custom_call" | custom-call | flops 256000000 | bytes 2097152 | tf_op jit(solution)/shard_map/pallas_call | solution.py:218
  6.7 2.1 %collective-permute-start.14 = (bf16[8,2,32,128]{3,2,1,0:T(8,128)(2,1)}, bf16[8,2,32,128]{3,2,1,0:T(8,128)(2,1)S(1)}, u32[]{:S(2)}, u32[]{:S(2)}) collective-permute-start(bf16[8,2,32,128]{3,2,1,0:T(8,128)(2,1)} %get-tuple-element.64), channel_id=1, source_target_pairs={{0,2},{2,0},{4,6},{6,4},{8,10},{10,8},{12,14},{14,12},{1,3},{3,1},... | collective-permute-start | bytes 393224 | tf_op jit(solution)/shard_map/ppermute | solution.py:443
  8.8 1.3 collective-permute-start.15
  10.1 0.1 collective-permute-start.16
  10.2 6.6 %shard_map.146 = (bf16[10,2,32,128]{3,2,1,0:T(8,128)(2,1)S(1)}, bf16[10,2,32,128]{3,2,1,0:T(8,128)(2,1)S(1)}, bf16[10,2,32,128]{3,2,1,0:T(8,128)(2,1)S(1)}, bf16...) custom-call(bf16[2,8192,128]{2,1,0:T(8,128)(2,1)S(1)} %bitcast.11, ...), custom_call_target="tpu_custom_call" | custom-call | flops 320000000 | bytes 2621440 | tf_op jit(solution)/shard_map/pallas_call | solution.py:218
  16.8 2.4 %collective-permute-start.10 = (bf16[10,2,32,128]{3,2,1,0:T(8,128)(2,1)S(1)}, bf16[10,2,32,128]{3,2,1,0:T(8,128)(2,1)S(1)}, u32[]{:S(2)}, u32[]{:S(2)}) collective-permute-start(bf16[10,2,32,128]{3,2,1,0:T(8,128)(2,1)S(1)} %get-tuple-element.59), channel_id=1, source_target_pairs={{0,8},{2,10},{4,12},{6,14},{8,0},{10,2},{12,4},{14,6},{1,9},{3,11}... | collective-permute-start | bytes 491528 | tf_op jit(solution)/shard_map/ppermute | solution.py:443
  19.3 0.1 collective-permute-start.17
  19.4 3.2 %collective-permute-start.18 = (bf16[8,2,32,128]{3,2,1,0:T(8,128)(2,1)S(1)}, bf16[8,2,32,128]{3,2,1,0:T(8,128)(2,1)S(1)}, u32[]{:S(2)}, u32[]{:S(2)}) collective-permute-start(bf16[8,2,32,128]{3,2,1,0:T(8,128)(2,1)S(1)} %copy-done.11), channel_id=1, source_target_pairs={{0,10},{2,8},{4,14},{6,12},{8,2},{10,0},{12,6},{14,4},{1,11},{3,9}... | collective-permute-start | bytes 393224 | tf_op jit(solution)/shard_map/ppermute | solution.py:443
  22.6 1.1 collective-permute-start.19
  23.7 2.1 %collective-permute-start.20 = (bf16[8,2,32,128]{3,2,1,0:T(8,128)(2,1)S(1)}, bf16[8,2,32,128]{3,2,1,0:T(8,128)(2,1)S(1)}, u32[]{:S(2)}, u32[]{:S(2)}) collective-permute-start(bf16[8,2,32,128]{3,2,1,0:T(8,128)(2,1)S(1)} %copy-done.9), channel_id=1, source_target_pairs={{0,14},{2,12},{4,10},{6,8},{8,6},{10,4},{12,2},{14,0},{1,15},{3,13... | collective-permute-start | bytes 393224 | tf_op jit(solution)/shard_map/ppermute | solution.py:443
  25.8 14.6 %collective-permute-done.17.refs_4_ = bf16[8,2,32,128]{3,2,1,0:T(8,128)(2,1)S(1)} collective-permute-done((bf16[8,2,32,128]{3,2,1,0:T(8,128)(2,1)S(1)}, bf16[8,2,32,128]{3,2,1,0:T(8,128)(2,1)S(1)}, u32[]{:S(2)}, u32[]{:S(2)}) %collective-permute-start.17) | collective-permute-done | bytes 131104 | tf_op jit(solution)/shard_map/ppermute | solution.py:443
  40.4 0.3 collective-permute-start.11
  40.7 3.5 %collective-permute-done.18.refs_5_ = bf16[8,2,32,128]{3,2,1,0:T(8,128)(2,1)S(1)} collective-permute-done((bf16[8,2,32,128]{3,2,1,0:T(8,128)(2,1)S(1)}, bf16[8,2,32,128]{3,2,1,0:T(8,128)(2,1)S(1)}, u32[]{:S(2)}, u32[]{:S(2)}) %collective-permute-start.18) | collective-permute-done | bytes 131104 | tf_op jit(solution)/shard_map/ppermute | solution.py:443
  44.3 7.7 %collective-permute-start.12 = (bf16[10,2,32,128]{3,2,1,0:T(8,128)(2,1)S(1)}, bf16[10,2,32,128]{3,2,1,0:T(8,128)(2,1)S(1)}, u32[]{:S(2)}, u32[]{:S(2)}) collective-permute-start(bf16[10,2,32,128]{3,2,1,0:T(8,128)(2,1)S(1)} %get-tuple-element.61), channel_id=1, source_target_pairs={{0,12},{2,14},{4,8},{6,10},{8,4},{10,6},{12,0},{14,2},{1,13},{3,15... | collective-permute-start | bytes 491528 | tf_op jit(solution)/shard_map/ppermute | solution.py:443
  52.0 1.2 collective-permute-start.7
  53.2 8.9 %collective-permute-start.8 = (bf16[10,2,32,128]{3,2,1,0:T(8,128)(2,1)S(1)}, bf16[10,2,32,128]{3,2,1,0:T(8,128)(2,1)S(1)}, u32[]{:S(2)}, u32[]{:S(2)}) collective-permute-start(bf16[10,2,32,128]{3,2,1,0:T(8,128)(2,1)S(1)} %get-tuple-element.57), channel_id=1, source_target_pairs={{0,4},{2,6},{4,0},{6,2},{8,12},{10,14},{12,8},{14,10},{1,5},{3,7},... | collective-permute-start | bytes 491528 | tf_op jit(solution)/shard_map/ppermute | solution.py:443
  62.1 6.5 %shard_map.145 = (bf16[10,2,32,128]{3,2,1,0:T(8,128)(2,1)S(1)}, bf16[10,2,32,128]{3,2,1,0:T(8,128)(2,1)S(1)}, bf16[10,2,32,128]{3,2,1,0:T(8,128)(2,1)S(1)}, bf16...) custom-call(bf16[2,8192,128]{2,1,0:T(8,128)(2,1)S(1)} %bitcast.12, ...), custom_call_target="tpu_custom_call" | custom-call | flops 320000000 | bytes 2621440 | tf_op jit(solution)/shard_map/pallas_call | solution.py:218
  68.7 0.1 collective-permute-start.9
  68.8 1.2 collective-permute-start
  70.0 1.3 collective-permute-start.22
  71.3 1.5 %collective-permute-start.1 = (bf16[10,2,32,128]{3,2,1,0:T(8,128)(2,1)S(1)}, bf16[10,2,32,128]{3,2,1,0:T(8,128)(2,1)S(1)}, u32[]{:S(2)}, u32[]{:S(2)}) collective-permute-start(bf16[10,2,32,128]{3,2,1,0:T(8,128)(2,1)S(1)} %get-tuple-element.49), channel_id=1, source_target_pairs={{0,4},{2,6},{4,0},{6,2},{8,12},{10,14},{12,8},{14,10},{1,5},{3,7},... | collective-permute-start | bytes 491528 | tf_op jit(solution)/shard_map/ppermute | solution.py:443
  72.8 1.0 collective-permute-start.2
  73.8 0.1 collective-permute-done.9.refs_3_
  73.9 3.1 %collective-permute-start.3 = (bf16[10,2,32,128]{3,2,1,0:T(8,128)(2,1)S(1)}, bf16[10,2,32,128]{3,2,1,0:T(8,128)(2,1)S(1)}, u32[]{:S(2)}, u32[]{:S(2)}) collective-permute-start(bf16[10,2,32,128]{3,2,1,0:T(8,128)(2,1)S(1)} %get-tuple-element.51), channel_id=1, source_target_pairs={{0,8},{2,10},{4,12},{6,14},{8,0},{10,2},{12,4},{14,6},{1,9},{3,11}... | collective-permute-start | bytes 491528 | tf_op jit(solution)/shard_map/ppermute | solution.py:443
  77.1 6.0 %collective-permute-start.4 = (bf16[10,2,32,128]{3,2,1,0:T(8,128)(2,1)S(1)}, bf16[10,2,32,128]{3,2,1,0:T(8,128)(2,1)S(1)}, u32[]{:S(2)}, u32[]{:S(2)}) collective-permute-start(bf16[10,2,32,128]{3,2,1,0:T(8,128)(2,1)S(1)} %get-tuple-element.52), channel_id=1, source_target_pairs={{0,10},{2,8},{4,14},{6,12},{8,2},{10,0},{12,6},{14,4},{1,11},{3,9}... | collective-permute-start | bytes 491528 | tf_op jit(solution)/shard_map/ppermute | solution.py:443
  83.1 0.3 collective-permute-start.5
  83.3 0.4 collective-permute-done.2.refs_3_
  83.8 5.6 %collective-permute-start.6 = (bf16[10,2,32,128]{3,2,1,0:T(8,128)(2,1)S(1)}, bf16[10,2,32,128]{3,2,1,0:T(8,128)(2,1)S(1)}, u32[]{:S(2)}, u32[]{:S(2)}) collective-permute-start(bf16[10,2,32,128]{3,2,1,0:T(8,128)(2,1)S(1)} %get-tuple-element.54), channel_id=1, source_target_pairs={{0,14},{2,12},{4,10},{6,8},{8,6},{10,4},{12,2},{14,0},{1,15},{3,13... | collective-permute-start | bytes 491528 | tf_op jit(solution)/shard_map/ppermute | solution.py:443
  89.4 2.8 %shard_map.148.refs_8_ = f32[2176,128]{1,0:T(8,128)S(1)} custom-call(bf16[8,2,32,128]{3,2,1,0:T(8,128)(2,1)S(1)} %copy-done.7, bf16[8,2,32,128]{3,2,1,0:T(8,128)(2,1)S(1)} %collective-permute-done.14.refs_1_, bf16[8,2,32,128]{3,2,1,0:T(8,128)(2,1)S(1)} %collective-permute-done.15.refs_2_, bf16[8,2,32,128]{3,2,1,0:T(8,128)(2,1)S(1)} %collective-permute-done.16.refs_3_, ...), custom_call_target="tpu_custom_call" | custom-call | flops 128000000 | bytes 2097152 | tf_op jit(solution)/shard_map/pallas_call | solution.py:338
  92.2 3.5 %shard_map.149.refs_6_ = f32[2176,128]{1,0:T(8,128)S(1)} custom-call(bf16[10,2,32,128]{3,2,1,0:T(8,128)(2,1)S(1)} %get-tuple-element.55.refs_0_, bf16[10,2,32,128]{3,2,1,0:T(8,128)(2,1)S(1)} %collective-permute-done.7.refs_1_, bf16[10,2,32,128]{3,2,1,0:T(8,128)(2,1)S(1)} %collective-permute-done.8.refs_2_, ...), custom_call_target="tpu_custom_call" | custom-call | flops 160000000 | bytes 2621440 | tf_op jit(solution)/shard_map/pallas_call | solution.py:338
  95.7 4.5 %collective-permute-done.4.refs_5_ = bf16[10,2,32,128]{3,2,1,0:T(8,128)(2,1)S(1)} collective-permute-done((bf16[10,2,32,128]{3,2,1,0:T(8,128)(2,1)S(1)}, bf16[10,2,32,128]{3,2,1,0:T(8,128)(2,1)S(1)}, u32[]{:S(2)}, u32[]{:S(2)}) %collective-permute-start.4) | collective-permute-done | bytes 163872 | tf_op jit(solution)/shard_map/ppermute | solution.py:443
  100.2 2.0 %shard_map.150.refs_8_ = f32[2176,128]{1,0:T(8,128)S(1)} custom-call(bf16[10,2,32,128]{3,2,1,0:T(8,128)(2,1)S(1)} %get-tuple-element.47.refs_0_, bf16[10,2,32,128]{3,2,1,0:T(8,128)(2,1)S(1)} %collective-permute-done.refs_1_, bf16[10,2,32,128]{3,2,1,0:T(8,128)(2,1)S(1)} %collective-permute-done.1.refs_2_, ...), custom_call_target="tpu_custom_call" | custom-call | flops 160000000 | bytes 2621440 | tf_op jit(solution)/shard_map/pallas_call | solution.py:338
  102.3 2.1 %shard_map.151.own = f32[1088,128]{1,0:T(8,128)S(1)} custom-call(bf16[10,2,32,128]{3,2,1,0:T(8,128)(2,1)S(1)} %get-tuple-element.47.refs_0_, bf16[10,2,32,128]{3,2,1,0:T(8,128)(2,1)S(1)} %collective-permute-done.refs_1_, bf16[10,2,32,128]{3,2,1,0:T(8,128)(2,1)S(1)} %collective-permute-done.1.refs_2_, ...), custom_call_target="tpu_custom_call" | custom-call | flops 160000000 | bytes 2621440 | tf_op jit(solution)/shard_map/pallas_call | solution.py:338
  104.4 5.5 %collective-permute-start.21 = (f32[1088,128]{1,0:T(8,128)S(1)}, f32[1088,128]{1,0:T(8,128)S(1)}, u32[]{:S(2)}, u32[]{:S(2)}) collective-permute-start(f32[1088,128]{1,0:T(8,128)S(1)} %shard_map.151.own), channel_id=1, source_target_pairs={{0,1},{1,0},{2,3},{3,2},{4,5},{5,4},{6,7},{7,6},{8,9},{9,8},{10,11... | collective-permute-start | bytes 1671176 | tf_op jit(solution)/shard_map/ppermute | solution.py:452
  109.9 3.5 %shard_map.152 = (bf16[4,2,16,128]{3,2,1,0:T(8,128)(2,1)S(1)}, bf16[4,2,16,128]{3,2,1,0:T(8,128)(2,1)S(1)}, bf16[4,2,16,128]{3,2,1,0:T(8,128)(2,1)S(1)}, bf16[4,...) custom-call(bf16[2,8192,128]{2,1,0:T(8,128)(2,1)S(1)} %bitcast.13, ...), custom_call_target="tpu_custom_call" | custom-call | flops 128000000 | bytes 1048576 | tf_op jit(solution)/shard_map/pallas_call | solution.py:218
  113.4 0.1 collective-permute-start.23
  113.5 1.5 %collective-permute-done.23.refs_8_ = bf16[8,4,2,16,128]{4,3,2,1,0:T(8,128)(2,1)S(1)} collective-permute-done((bf16[8,4,2,16,128]{4,3,2,1,0:T(8,128)(2,1)S(1)}, bf16[8,4,2,16,128]{4,3,2,1,0:T(8,128)(2,1)S(1)}, u32[]{:S(2)}, u32[]{:S(2)}) %collective-permute-start.23) | collective-permute-done | bytes 262176 | tf_op jit(solution)/shard_map/ppermute | solution.py:439
  115.0 0.1 collective-permute-start.24
  115.1 3.1 %collective-permute-start.25 = (bf16[8,2,16,128]{3,2,1,0:T(8,128)(2,1)S(1)}, bf16[8,2,16,128]{3,2,1,0:T(8,128)(2,1)S(1)}, u32[]{:S(2)}, u32[]{:S(2)}) collective-permute-start(bf16[8,2,16,128]{3,2,1,0:T(8,128)(2,1)S(1)} %get-tuple-element.83), channel_id=1, source_target_pairs={{0,4},{2,6},{4,0},{6,2},{8,12},{10,14},{12,8},{14,10},{1,5},{3,7},... | collective-permute-start | bytes 196616 | tf_op jit(solution)/shard_map/ppermute | solution.py:443
  118.2 1.0 collective-permute-start.26
  119.2 0.6 collective-permute-start.27
  119.8 1.7 %collective-permute-start.28 = (bf16[8,2,16,128]{3,2,1,0:T(8,128)(2,1)S(1)}, bf16[8,2,16,128]{3,2,1,0:T(8,128)(2,1)S(1)}, u32[]{:S(2)}, u32[]{:S(2)}) collective-permute-start(bf16[8,2,16,128]{3,2,1,0:T(8,128)(2,1)S(1)} %get-tuple-element.86), channel_id=1, source_target_pairs={{0,10},{2,8},{4,14},{6,12},{8,2},{10,0},{12,6},{14,4},{1,11},{3,9}... | collective-permute-start | bytes 196616 | tf_op jit(solution)/shard_map/ppermute | solution.py:443
  121.6 2.0 %collective-permute-start.29 = (bf16[8,2,16,128]{3,2,1,0:T(8,128)(2,1)S(1)}, bf16[8,2,16,128]{3,2,1,0:T(8,128)(2,1)S(1)}, u32[]{:S(2)}, u32[]{:S(2)}) collective-permute-start(bf16[8,2,16,128]{3,2,1,0:T(8,128)(2,1)S(1)} %get-tuple-element.87), channel_id=1, source_target_pairs={{0,12},{2,14},{4,8},{6,10},{8,4},{10,6},{12,0},{14,2},{1,13},{3,15... | collective-permute-start | bytes 196616 | tf_op jit(solution)/shard_map/ppermute | solution.py:443
  123.5 2.2 %collective-permute-start.30 = (bf16[8,2,16,128]{3,2,1,0:T(8,128)(2,1)S(1)}, bf16[8,2,16,128]{3,2,1,0:T(8,128)(2,1)S(1)}, u32[]{:S(2)}, u32[]{:S(2)}) collective-permute-start(bf16[8,2,16,128]{3,2,1,0:T(8,128)(2,1)S(1)} %get-tuple-element.88), channel_id=1, source_target_pairs={{0,14},{2,12},{4,10},{6,8},{8,6},{10,4},{12,2},{14,0},{1,15},{3,13... | collective-permute-start | bytes 196616 | tf_op jit(solution)/shard_map/ppermute | solution.py:443
  125.7 4.5 %collective-permute-done.28.refs_5_ = bf16[8,2,16,128]{3,2,1,0:T(8,128)(2,1)S(1)} collective-permute-done((bf16[8,2,16,128]{3,2,1,0:T(8,128)(2,1)S(1)}, bf16[8,2,16,128]{3,2,1,0:T(8,128)(2,1)S(1)}, u32[]{:S(2)}, u32[]{:S(2)}) %collective-permute-start.28) | collective-permute-done | bytes 65568 | tf_op jit(solution)/shard_map/ppermute | solution.py:443
  130.3 0.9 shard_map.153.refs_8_
  131.2 1.2 shard_map.154.late
  132.4 1.4 %visibility.1 = f32[2,256,256]{2,1,0:T(8,128)} custom-call(f32[1088,128]{1,0:T(8,128)S(1)} %shard_map.151.own, f32[1088,128]{1,0:T(8,128)S(1)} %collective-permute-done.21.other, f32[1088,128]{1,0:T(8,128)S(1)} %shard_map.154.late), custom_call_target="tpu_custom_call" | custom-call | tf_op jit(solution)/shard_map/visibility/pallas_call | solution.py:454
  (52 shorter events, 0.2 us)
Async XLA Ops:
  0.0 10.2 %copy-start = (bf16[2,2,524288]{2,1,0:T(2,128)(2,1)S(1)}, bf16[2,2,524288]{2,1,0:T(2,128)(2,1)}, u32[]{:S(2)}) copy-start(bf16[2,2,524288]{2,1,0:T(2,128)(2,1)} %param.15) | copy-start | bytes 12582916
  0.0 10.2 %copy-start.1 = (bf16[2,2,61440]{2,1,0:T(2,128)(2,1)S(1)}, bf16[2,2,61440]{2,1,0:T(2,128)(2,1)}, u32[]{:S(2)}) copy-start(bf16[2,2,61440]{2,1,0:T(2,128)(2,1)} %param.16) | copy-start | bytes 1474564
  0.0 10.2 %copy-start.2 = (f32[16,4096]{1,0:T(8,128)S(1)}, f32[16,4096]{1,0:T(8,128)}, u32[]{:S(2)}) copy-start(f32[16,4096]{1,0:T(8,128)} %refs_3_.7) | copy-start | bytes 786436
  0.0 10.2 %copy-start.3 = (bf16[256,256]{1,0:T(8,128)(2,1)S(1)}, bf16[256,256]{1,0:T(8,128)(2,1)}, u32[]{:S(2)}) copy-start(bf16[256,256]{1,0:T(8,128)(2,1)} %constant.8.clone.refs_4_) | copy-start | bytes 393220
  0.0 10.2 %copy-start.4 = (bf16[256,256]{1,0:T(8,128)(2,1)S(1)}, bf16[256,256]{1,0:T(8,128)(2,1)}, u32[]{:S(2)}) copy-start(bf16[256,256]{1,0:T(8,128)(2,1)} %constant.10.clone.refs_6_) | copy-start | bytes 393220
  0.0 10.2 %copy-start.5 = (f32[2,64,128]{2,1,0:T(8,128)S(1)}, f32[2,64,128]{2,1,0:T(8,128)}, u32[]{:S(2)}) copy-start(f32[2,64,128]{2,1,0:T(8,128)} %constant.9.clone.refs_5_) | copy-start | bytes 196612
  6.7 12.7 %collective-permute-start.14 = (bf16[8,2,32,128]{3,2,1,0:T(8,128)(2,1)}, bf16[8,2,32,128]{3,2,1,0:T(8,128)(2,1)S(1)}, u32[]{:S(2)}, u32[]{:S(2)}) collective-permute-start(bf16[8,2,32,128]{3,2,1,0:T(8,128)(2,1)} %get-tuple-element.64), channel_id=1, source_target_pairs={{0,2},{2,0},{4,6},{6,4},{8,10},{10,8},{12,14},{14,12},{1,3},{3,1},... | collective-permute-start | bytes 393224 | tf_op jit(solution)/shard_map/ppermute | solution.py:443
  8.8 13.8 %collective-permute-start.15 = (bf16[8,2,32,128]{3,2,1,0:T(8,128)(2,1)}, bf16[8,2,32,128]{3,2,1,0:T(8,128)(2,1)S(1)}, u32[]{:S(2)}, u32[]{:S(2)}) collective-permute-start(bf16[8,2,32,128]{3,2,1,0:T(8,128)(2,1)} %get-tuple-element.65), channel_id=1, source_target_pairs={{0,4},{2,6},{4,0},{6,2},{8,12},{10,14},{12,8},{14,10},{1,5},{3,7},... | collective-permute-start | bytes 393224 | tf_op jit(solution)/shard_map/ppermute | solution.py:443
  10.1 9.2 %copy-start.12 = (bf16[8,2,32,128]{3,2,1,0:T(8,128)(2,1)S(1)}, bf16[8,2,32,128]{3,2,1,0:T(8,128)(2,1)}, u32[]{:S(2)}) copy-start(bf16[8,2,32,128]{3,2,1,0:T(8,128)(2,1)} %get-tuple-element.67) | copy-start | bytes 393220
  10.1 9.2 %copy-start.11 = (bf16[8,2,32,128]{3,2,1,0:T(8,128)(2,1)S(1)}, bf16[8,2,32,128]{3,2,1,0:T(8,128)(2,1)}, u32[]{:S(2)}) copy-start(bf16[8,2,32,128]{3,2,1,0:T(8,128)(2,1)} %get-tuple-element.68) | copy-start | bytes 393220
  10.1 12.5 %copy-start.10 = (bf16[8,2,32,128]{3,2,1,0:T(8,128)(2,1)S(1)}, bf16[8,2,32,128]{3,2,1,0:T(8,128)(2,1)}, u32[]{:S(2)}) copy-start(bf16[8,2,32,128]{3,2,1,0:T(8,128)(2,1)} %get-tuple-element.69) | copy-start | bytes 393220
  10.1 13.6 %copy-start.9 = (bf16[8,2,32,128]{3,2,1,0:T(8,128)(2,1)S(1)}, bf16[8,2,32,128]{3,2,1,0:T(8,128)(2,1)}, u32[]{:S(2)}) copy-start(bf16[8,2,32,128]{3,2,1,0:T(8,128)(2,1)} %get-tuple-element.70) | copy-start | bytes 393220
  10.1 13.6 %collective-permute-start.16 = (bf16[8,2,32,128]{3,2,1,0:T(8,128)(2,1)}, bf16[8,2,32,128]{3,2,1,0:T(8,128)(2,1)S(1)}, u32[]{:S(2)}, u32[]{:S(2)}) collective-permute-start(bf16[8,2,32,128]{3,2,1,0:T(8,128)(2,1)} %get-tuple-element.66), channel_id=1, source_target_pairs={{0,6},{2,4},{4,2},{6,0},{8,14},{10,12},{12,10},{14,8},{1,7},{3,5},... | collective-permute-start | bytes 393224 | tf_op jit(solution)/shard_map/ppermute | solution.py:443
  16.8 36.4 %collective-permute-start.10 = (bf16[10,2,32,128]{3,2,1,0:T(8,128)(2,1)S(1)}, bf16[10,2,32,128]{3,2,1,0:T(8,128)(2,1)S(1)}, u32[]{:S(2)}, u32[]{:S(2)}) collective-permute-start(bf16[10,2,32,128]{3,2,1,0:T(8,128)(2,1)S(1)} %get-tuple-element.59), channel_id=1, source_target_pairs={{0,8},{2,10},{4,12},{6,14},{8,0},{10,2},{12,4},{14,6},{1,9},{3,11}... | collective-permute-start | bytes 491528 | tf_op jit(solution)/shard_map/ppermute | solution.py:443
  19.3 21.1 %collective-permute-start.17 = (bf16[8,2,32,128]{3,2,1,0:T(8,128)(2,1)S(1)}, bf16[8,2,32,128]{3,2,1,0:T(8,128)(2,1)S(1)}, u32[]{:S(2)}, u32[]{:S(2)}) collective-permute-start(bf16[8,2,32,128]{3,2,1,0:T(8,128)(2,1)S(1)} %copy-done.12), channel_id=1, source_target_pairs={{0,8},{2,10},{4,12},{6,14},{8,0},{10,2},{12,4},{14,6},{1,9},{3,11}... | collective-permute-start | bytes 393224 | tf_op jit(solution)/shard_map/ppermute | solution.py:443
  19.4 24.9 %collective-permute-start.18 = (bf16[8,2,32,128]{3,2,1,0:T(8,128)(2,1)S(1)}, bf16[8,2,32,128]{3,2,1,0:T(8,128)(2,1)S(1)}, u32[]{:S(2)}, u32[]{:S(2)}) collective-permute-start(bf16[8,2,32,128]{3,2,1,0:T(8,128)(2,1)S(1)} %copy-done.11), channel_id=1, source_target_pairs={{0,10},{2,8},{4,14},{6,12},{8,2},{10,0},{12,6},{14,4},{1,11},{3,9}... | collective-permute-start | bytes 393224 | tf_op jit(solution)/shard_map/ppermute | solution.py:443
  22.6 29.4 %collective-permute-start.19 = (bf16[8,2,32,128]{3,2,1,0:T(8,128)(2,1)S(1)}, bf16[8,2,32,128]{3,2,1,0:T(8,128)(2,1)S(1)}, u32[]{:S(2)}, u32[]{:S(2)}) collective-permute-start(bf16[8,2,32,128]{3,2,1,0:T(8,128)(2,1)S(1)} %copy-done.10), channel_id=1, source_target_pairs={{0,12},{2,14},{4,8},{6,10},{8,4},{10,6},{12,0},{14,2},{1,13},{3,15... | collective-permute-start | bytes 393224 | tf_op jit(solution)/shard_map/ppermute | solution.py:443
  23.7 28.3 %collective-permute-start.20 = (bf16[8,2,32,128]{3,2,1,0:T(8,128)(2,1)S(1)}, bf16[8,2,32,128]{3,2,1,0:T(8,128)(2,1)S(1)}, u32[]{:S(2)}, u32[]{:S(2)}) collective-permute-start(bf16[8,2,32,128]{3,2,1,0:T(8,128)(2,1)S(1)} %copy-done.9), channel_id=1, source_target_pairs={{0,14},{2,12},{4,10},{6,8},{8,6},{10,4},{12,2},{14,0},{1,15},{3,13... | collective-permute-start | bytes 393224 | tf_op jit(solution)/shard_map/ppermute | solution.py:443
  40.4 28.3 %collective-permute-start.11 = (bf16[10,2,32,128]{3,2,1,0:T(8,128)(2,1)S(1)}, bf16[10,2,32,128]{3,2,1,0:T(8,128)(2,1)S(1)}, u32[]{:S(2)}, u32[]{:S(2)}) collective-permute-start(bf16[10,2,32,128]{3,2,1,0:T(8,128)(2,1)S(1)} %get-tuple-element.60), channel_id=1, source_target_pairs={{0,10},{2,8},{4,14},{6,12},{8,2},{10,0},{12,6},{14,4},{1,11},{3,9}... | collective-permute-start | bytes 491528 | tf_op jit(solution)/shard_map/ppermute | solution.py:443
  44.3 24.5 %collective-permute-start.12 = (bf16[10,2,32,128]{3,2,1,0:T(8,128)(2,1)S(1)}, bf16[10,2,32,128]{3,2,1,0:T(8,128)(2,1)S(1)}, u32[]{:S(2)}, u32[]{:S(2)}) collective-permute-start(bf16[10,2,32,128]{3,2,1,0:T(8,128)(2,1)S(1)} %get-tuple-element.61), channel_id=1, source_target_pairs={{0,12},{2,14},{4,8},{6,10},{8,4},{10,6},{12,0},{14,2},{1,13},{3,15... | collective-permute-start | bytes 491528 | tf_op jit(solution)/shard_map/ppermute | solution.py:443
  52.0 17.9 %collective-permute-start.13 = (bf16[10,2,32,128]{3,2,1,0:T(8,128)(2,1)S(1)}, bf16[10,2,32,128]{3,2,1,0:T(8,128)(2,1)S(1)}, u32[]{:S(2)}, u32[]{:S(2)}) collective-permute-start(bf16[10,2,32,128]{3,2,1,0:T(8,128)(2,1)S(1)} %get-tuple-element.62), channel_id=1, source_target_pairs={{0,14},{2,12},{4,10},{6,8},{8,6},{10,4},{12,2},{14,0},{1,15},{3,13... | collective-permute-start | bytes 491528 | tf_op jit(solution)/shard_map/ppermute | solution.py:443
  52.0 19.2 %collective-permute-start.7 = (bf16[10,2,32,128]{3,2,1,0:T(8,128)(2,1)S(1)}, bf16[10,2,32,128]{3,2,1,0:T(8,128)(2,1)S(1)}, u32[]{:S(2)}, u32[]{:S(2)}) collective-permute-start(bf16[10,2,32,128]{3,2,1,0:T(8,128)(2,1)S(1)} %get-tuple-element.56), channel_id=1, source_target_pairs={{0,2},{2,0},{4,6},{6,4},{8,10},{10,8},{12,14},{14,12},{1,3},{3,1},... | collective-permute-start | bytes 491528 | tf_op jit(solution)/shard_map/ppermute | solution.py:443
  53.2 16.8 %copy-start.8 = (bf16[2,960,128]{2,1,0:T(8,128)(2,1)S(1)}, bf16[2,960,128]{2,1,0:T(8,128)(2,1)}, u32[]{:S(2)}) copy-start(bf16[2,960,128]{2,1,0:T(8,128)(2,1)} %get-tuple-element.71) | copy-start | bytes 1474564
  53.2 36.1 %copy-start.7 = (bf16[8,2,32,128]{3,2,1,0:T(8,128)(2,1)S(1)}, bf16[8,2,32,128]{3,2,1,0:T(8,128)(2,1)}, u32[]{:S(2)}) copy-start(bf16[8,2,32,128]{3,2,1,0:T(8,128)(2,1)} %get-tuple-element.63.refs_0_) | copy-start | bytes 393220
  53.2 19.6 %collective-permute-start.8 = (bf16[10,2,32,128]{3,2,1,0:T(8,128)(2,1)S(1)}, bf16[10,2,32,128]{3,2,1,0:T(8,128)(2,1)S(1)}, u32[]{:S(2)}, u32[]{:S(2)}) collective-permute-start(bf16[10,2,32,128]{3,2,1,0:T(8,128)(2,1)S(1)} %get-tuple-element.57), channel_id=1, source_target_pairs={{0,4},{2,6},{4,0},{6,2},{8,12},{10,14},{12,8},{14,10},{1,5},{3,7},... | collective-permute-start | bytes 491528 | tf_op jit(solution)/shard_map/ppermute | solution.py:443
  68.7 5.2 %collective-permute-start.9 = (bf16[10,2,32,128]{3,2,1,0:T(8,128)(2,1)S(1)}, bf16[10,2,32,128]{3,2,1,0:T(8,128)(2,1)S(1)}, u32[]{:S(2)}, u32[]{:S(2)}) collective-permute-start(bf16[10,2,32,128]{3,2,1,0:T(8,128)(2,1)S(1)} %get-tuple-element.58), channel_id=1, source_target_pairs={{0,6},{2,4},{4,2},{6,0},{8,14},{10,12},{12,10},{14,8},{1,7},{3,5},... | collective-permute-start | bytes 491528 | tf_op jit(solution)/shard_map/ppermute | solution.py:443
  68.8 8.3 %collective-permute-start = (bf16[10,2,32,128]{3,2,1,0:T(8,128)(2,1)S(1)}, bf16[10,2,32,128]{3,2,1,0:T(8,128)(2,1)S(1)}, u32[]{:S(2)}, u32[]{:S(2)}) collective-permute-start(bf16[10,2,32,128]{3,2,1,0:T(8,128)(2,1)S(1)} %get-tuple-element.48), channel_id=1, source_target_pairs={{0,2},{2,0},{4,6},{6,4},{8,10},{10,8},{12,14},{14,12},{1,3},{3,1},... | collective-permute-start | bytes 491528 | tf_op jit(solution)/shard_map/ppermute | solution.py:443
  70.0 39.9 %collective-permute-start.22 = (bf16[2,960,128]{2,1,0:T(8,128)(2,1)S(1)}, bf16[2,960,128]{2,1,0:T(8,128)(2,1)S(1)}, u32[]{:S(2)}, u32[]{:S(2)}) collective-permute-start(bf16[2,960,128]{2,1,0:T(8,128)(2,1)S(1)} %copy-done.8), channel_id=1, source_target_pairs={{0,1},{2,3},{4,5},{6,7},{8,9},{10,11},{12,13},{14,15},{16,17},{18,... | collective-permute-start | bytes 1474568 | tf_op jit(solution)/shard_map/ppermute | solution.py:431
  71.3 11.8 %collective-permute-start.1 = (bf16[10,2,32,128]{3,2,1,0:T(8,128)(2,1)S(1)}, bf16[10,2,32,128]{3,2,1,0:T(8,128)(2,1)S(1)}, u32[]{:S(2)}, u32[]{:S(2)}) collective-permute-start(bf16[10,2,32,128]{3,2,1,0:T(8,128)(2,1)S(1)} %get-tuple-element.49), channel_id=1, source_target_pairs={{0,4},{2,6},{4,0},{6,2},{8,12},{10,14},{12,8},{14,10},{1,5},{3,7},... | collective-permute-start | bytes 491528 | tf_op jit(solution)/shard_map/ppermute | solution.py:443
  72.8 11.0 %collective-permute-start.2 = (bf16[10,2,32,128]{3,2,1,0:T(8,128)(2,1)S(1)}, bf16[10,2,32,128]{3,2,1,0:T(8,128)(2,1)S(1)}, u32[]{:S(2)}, u32[]{:S(2)}) collective-permute-start(bf16[10,2,32,128]{3,2,1,0:T(8,128)(2,1)S(1)} %get-tuple-element.50), channel_id=1, source_target_pairs={{0,6},{2,4},{4,2},{6,0},{8,14},{10,12},{12,10},{14,8},{1,7},{3,5},... | collective-permute-start | bytes 491528 | tf_op jit(solution)/shard_map/ppermute | solution.py:443
  73.9 21.8 %collective-permute-start.3 = (bf16[10,2,32,128]{3,2,1,0:T(8,128)(2,1)S(1)}, bf16[10,2,32,128]{3,2,1,0:T(8,128)(2,1)S(1)}, u32[]{:S(2)}, u32[]{:S(2)}) collective-permute-start(bf16[10,2,32,128]{3,2,1,0:T(8,128)(2,1)S(1)} %get-tuple-element.51), channel_id=1, source_target_pairs={{0,8},{2,10},{4,12},{6,14},{8,0},{10,2},{12,4},{14,6},{1,9},{3,11}... | collective-permute-start | bytes 491528 | tf_op jit(solution)/shard_map/ppermute | solution.py:443
  77.1 23.2 %collective-permute-start.4 = (bf16[10,2,32,128]{3,2,1,0:T(8,128)(2,1)S(1)}, bf16[10,2,32,128]{3,2,1,0:T(8,128)(2,1)S(1)}, u32[]{:S(2)}, u32[]{:S(2)}) collective-permute-start(bf16[10,2,32,128]{3,2,1,0:T(8,128)(2,1)S(1)} %get-tuple-element.52), channel_id=1, source_target_pairs={{0,10},{2,8},{4,14},{6,12},{8,2},{10,0},{12,6},{14,4},{1,11},{3,9}... | collective-permute-start | bytes 491528 | tf_op jit(solution)/shard_map/ppermute | solution.py:443
  83.1 19.2 %collective-permute-start.5 = (bf16[10,2,32,128]{3,2,1,0:T(8,128)(2,1)S(1)}, bf16[10,2,32,128]{3,2,1,0:T(8,128)(2,1)S(1)}, u32[]{:S(2)}, u32[]{:S(2)}) collective-permute-start(bf16[10,2,32,128]{3,2,1,0:T(8,128)(2,1)S(1)} %get-tuple-element.53), channel_id=1, source_target_pairs={{0,12},{2,14},{4,8},{6,10},{8,4},{10,6},{12,0},{14,2},{1,13},{3,15... | collective-permute-start | bytes 491528 | tf_op jit(solution)/shard_map/ppermute | solution.py:443
  83.8 18.5 %collective-permute-start.6 = (bf16[10,2,32,128]{3,2,1,0:T(8,128)(2,1)S(1)}, bf16[10,2,32,128]{3,2,1,0:T(8,128)(2,1)S(1)}, u32[]{:S(2)}, u32[]{:S(2)}) collective-permute-start(bf16[10,2,32,128]{3,2,1,0:T(8,128)(2,1)S(1)} %get-tuple-element.54), channel_id=1, source_target_pairs={{0,14},{2,12},{4,10},{6,8},{8,6},{10,4},{12,2},{14,0},{1,15},{3,13... | collective-permute-start | bytes 491528 | tf_op jit(solution)/shard_map/ppermute | solution.py:443
  102.2 7.7 %copy-start.6 = (bf16[256,256]{1,0:T(8,128)(2,1)S(1)}, bf16[256,256]{1,0:T(8,128)(2,1)}, u32[]{:S(2)}) copy-start(bf16[256,256]{1,0:T(8,128)(2,1)} %constant.11.clone.refs_6_) | copy-start | bytes 393220
  104.4 28.0 %collective-permute-start.21 = (f32[1088,128]{1,0:T(8,128)S(1)}, f32[1088,128]{1,0:T(8,128)S(1)}, u32[]{:S(2)}, u32[]{:S(2)}) collective-permute-start(f32[1088,128]{1,0:T(8,128)S(1)} %shard_map.151.own), channel_id=1, source_target_pairs={{0,1},{1,0},{2,3},{3,2},{4,5},{5,4},{6,7},{7,6},{8,9},{9,8},{10,11... | collective-permute-start | bytes 1671176 | tf_op jit(solution)/shard_map/ppermute | solution.py:452
  113.4 1.6 %collective-permute-start.23 = (bf16[8,4,2,16,128]{4,3,2,1,0:T(8,128)(2,1)S(1)}, bf16[8,4,2,16,128]{4,3,2,1,0:T(8,128)(2,1)S(1)}, u32[]{:S(2)}, u32[]{:S(2)}) collective-permute-start(bf16[8,4,2,16,128]{4,3,2,1,0:T(8,128)(2,1)S(1)} %get-tuple-element.80), channel_id=1, source_target_pairs={{0,1},{1,0},{2,3},{3,2},{4,5},{5,4},{6,7},{7,6},{8,9},{9,8},{10,11... | collective-permute-start | bytes 786440 | tf_op jit(solution)/shard_map/ppermute | solution.py:439
  115.0 4.8 %collective-permute-start.24 = (bf16[8,2,16,128]{3,2,1,0:T(8,128)(2,1)S(1)}, bf16[8,2,16,128]{3,2,1,0:T(8,128)(2,1)S(1)}, u32[]{:S(2)}, u32[]{:S(2)}) collective-permute-start(bf16[8,2,16,128]{3,2,1,0:T(8,128)(2,1)S(1)} %get-tuple-element.82), channel_id=1, source_target_pairs={{0,2},{2,0},{4,6},{6,4},{8,10},{10,8},{12,14},{14,12},{1,3},{3,1},... | collective-permute-start | bytes 196616 | tf_op jit(solution)/shard_map/ppermute | solution.py:443
  115.1 6.5 %collective-permute-start.25 = (bf16[8,2,16,128]{3,2,1,0:T(8,128)(2,1)S(1)}, bf16[8,2,16,128]{3,2,1,0:T(8,128)(2,1)S(1)}, u32[]{:S(2)}, u32[]{:S(2)}) collective-permute-start(bf16[8,2,16,128]{3,2,1,0:T(8,128)(2,1)S(1)} %get-tuple-element.83), channel_id=1, source_target_pairs={{0,4},{2,6},{4,0},{6,2},{8,12},{10,14},{12,8},{14,10},{1,5},{3,7},... | collective-permute-start | bytes 196616 | tf_op jit(solution)/shard_map/ppermute | solution.py:443
  118.2 5.3 %collective-permute-start.26 = (bf16[8,2,16,128]{3,2,1,0:T(8,128)(2,1)S(1)}, bf16[8,2,16,128]{3,2,1,0:T(8,128)(2,1)S(1)}, u32[]{:S(2)}, u32[]{:S(2)}) collective-permute-start(bf16[8,2,16,128]{3,2,1,0:T(8,128)(2,1)S(1)} %get-tuple-element.84), channel_id=1, source_target_pairs={{0,6},{2,4},{4,2},{6,0},{8,14},{10,12},{12,10},{14,8},{1,7},{3,5},... | collective-permute-start | bytes 196616 | tf_op jit(solution)/shard_map/ppermute | solution.py:443
  119.2 6.5 %collective-permute-start.27 = (bf16[8,2,16,128]{3,2,1,0:T(8,128)(2,1)S(1)}, bf16[8,2,16,128]{3,2,1,0:T(8,128)(2,1)S(1)}, u32[]{:S(2)}, u32[]{:S(2)}) collective-permute-start(bf16[8,2,16,128]{3,2,1,0:T(8,128)(2,1)S(1)} %get-tuple-element.85), channel_id=1, source_target_pairs={{0,8},{2,10},{4,12},{6,14},{8,0},{10,2},{12,4},{14,6},{1,9},{3,11}... | collective-permute-start | bytes 196616 | tf_op jit(solution)/shard_map/ppermute | solution.py:443
  119.8 10.5 %collective-permute-start.28 = (bf16[8,2,16,128]{3,2,1,0:T(8,128)(2,1)S(1)}, bf16[8,2,16,128]{3,2,1,0:T(8,128)(2,1)S(1)}, u32[]{:S(2)}, u32[]{:S(2)}) collective-permute-start(bf16[8,2,16,128]{3,2,1,0:T(8,128)(2,1)S(1)} %get-tuple-element.86), channel_id=1, source_target_pairs={{0,10},{2,8},{4,14},{6,12},{8,2},{10,0},{12,6},{14,4},{1,11},{3,9}... | collective-permute-start | bytes 196616 | tf_op jit(solution)/shard_map/ppermute | solution.py:443
  121.6 9.6 %collective-permute-start.29 = (bf16[8,2,16,128]{3,2,1,0:T(8,128)(2,1)S(1)}, bf16[8,2,16,128]{3,2,1,0:T(8,128)(2,1)S(1)}, u32[]{:S(2)}, u32[]{:S(2)}) collective-permute-start(bf16[8,2,16,128]{3,2,1,0:T(8,128)(2,1)S(1)} %get-tuple-element.87), channel_id=1, source_target_pairs={{0,12},{2,14},{4,8},{6,10},{8,4},{10,6},{12,0},{14,2},{1,13},{3,15... | collective-permute-start | bytes 196616 | tf_op jit(solution)/shard_map/ppermute | solution.py:443
  123.5 7.6 %collective-permute-start.30 = (bf16[8,2,16,128]{3,2,1,0:T(8,128)(2,1)S(1)}, bf16[8,2,16,128]{3,2,1,0:T(8,128)(2,1)S(1)}, u32[]{:S(2)}, u32[]{:S(2)}) collective-permute-start(bf16[8,2,16,128]{3,2,1,0:T(8,128)(2,1)S(1)} %get-tuple-element.88), channel_id=1, source_target_pairs={{0,14},{2,12},{4,10},{6,8},{8,6},{10,4},{12,2},{14,0},{1,15},{3,13... | collective-permute-start | bytes 196616 | tf_op jit(solution)/shard_map/ppermute | solution.py:443
